TPU v7x, 32 devices: a whole 2x2x4 slice. The times are simulated.
32 devices in a mesh: gx: 8 (over z, core), gy: 4 (over y, x).
Axes of the slice: x: 2, y: 2, z: 4, core: 2. Of those that a mesh axis runs over, the one named last changes fastest.
Arguments:
- e_init: float32 [3, 64, 32, 512], P(None, 'gx', None, 'gy'), may hold values from -13.5 to 13.5
- h_init: float32 [3, 64, 32, 512], P(None, 'gx', None, 'gy'), may hold values from -13.5 to 13.5
- material: int32 [64, 32, 512], P('gx', None, 'gy'), may hold values from 0 to 7
- eps_table: float32 [8], replicated, may hold values from 1 to 12
- target: float32 [8, 64, 64], replicated, may hold values from 0 to 2
Outputs:
- sensitivity: float32 [64, 32, 512], P('gx', None, 'gy')
All inputs are finite; a program needn't handle non-finite values.
Results may differ from a plain program's by a relative error of at most 0.0001.
Values sent between devices are 32-bit elements; how exact they have to be, the bound alone decides.
No kernel may reach another device: no remote copies, remote signals or barrier semaphores. Data moves between devices by JAX's collectives and lax.ppermute only.
A program may use at most 128 MiB of HBM per device.

v0:
```python
import functools
import math

import jax
import jax.numpy as jnp
import ml_dtypes
import numpy as np
from jax import lax
from jax.experimental import pallas as pl
from jax.experimental.pallas import tpu as pltpu
from jax.sharding import PartitionSpec as P

ITERS = 6
NF = 8
FAR = 64
NMAT = 8
GHOST = ITERS
BACK = ITERS - 1
TWO_PI = 2.0 * math.pi
F32 = jnp.float32
BF16 = jnp.bfloat16
VMEM_BYTES = 56 * 1024 * 1024


def split_table(table):
    high = table.astype(np.float32).astype(ml_dtypes.bfloat16)
    low = (table - high.astype(np.float64)).astype(np.float32).astype(ml_dtypes.bfloat16)
    return high, low


def time_table(depth):
    freq = np.arange(NF)[None, :, None]
    moment = np.arange(1, ITERS + 1)[:, None, None]
    turns = ((2 * freq + 1) * (7 * moment + np.arange(depth)[None, None, :])) % 64
    angle = turns * (TWO_PI / 64)
    return np.concatenate([np.cos(angle), -np.sin(angle)], axis=1)


def lens_table(depth):
    weights = time_table(depth)
    wide = np.stack([weights, weights], axis=2)
    wide = wide.transpose(1, 0, 2, 3).reshape(2 * NF, -1)
    return np.concatenate(split_table(wide), axis=0)


def source_table(depth):
    flat = time_table(depth).transpose(0, 2, 1).reshape(ITERS * depth, 2 * NF)
    high, low = split_table(flat)
    return np.concatenate([high, high, low], axis=1)


def phase(cells, length):
    freq = np.arange(NF)[:, None, None]
    order = np.arange(FAR)[None, :, None] - FAR // 2
    period = 4 * length * NF
    turns = (order * (2 * cells[None, None, :] + 1) * (NF + freq)) % period
    angle = turns * (TWO_PI / period)
    return np.cos(angle), np.sin(angle)


def column_table(tile_cols, width):
    lanes = np.arange(width)
    cells = np.where(lanes >= width - GHOST, lanes - width, lanes)
    used = (lanes < tile_cols + GHOST) | (lanes >= width - GHOST)
    cos, sin = (t * used[None, None, :] for t in phase(cells, tile_cols))
    table = np.concatenate(
        [np.concatenate([cos, sin], axis=2), np.concatenate([-sin, cos], axis=2)], axis=1
    )
    return np.concatenate(split_table(table), axis=1)


def column_twist(count_cols):
    freq = np.arange(NF)[None, :, None]
    order = np.arange(FAR)[None, None, :] - FAR // 2
    place = np.arange(count_cols)[:, None, None]
    angle = ((order * (NF + freq) * place) % 16) * (TWO_PI / 16)
    cos, sin = np.cos(angle), np.sin(angle)
    return np.stack(
        [np.concatenate([cos, cos], axis=2), np.concatenate([sin, -sin], axis=2)]
    ).astype(np.float32)


def row_table(rows):
    table = np.concatenate(phase(np.arange(rows), rows), axis=1)
    high, low = split_table(table)
    return np.concatenate([high, high, low], axis=2)


def row_back_table(rows):
    cells = np.arange(rows + 16) - BACK
    cos, sin = phase(cells, rows)
    return np.stack([cos, sin], axis=1).transpose(0, 1, 3, 2).astype(np.float32)


def split(value):
    high = value.astype(BF16)
    return high, (value - high.astype(F32)).astype(BF16)


def dot(left, right):
    return jnp.dot(left, right, preferred_element_type=F32)


def half_turn(value):
    return pltpu.roll(value, FAR, 1)


def z_index(shape):
    return lax.broadcasted_iota(jnp.int32, shape, 0)


def curl_ahead(x, y, z, y_next, z_next):
    depth, width = x.shape
    last = z_index(x.shape) == depth - 1

    def by_y(v):
        return pltpu.roll(v, width - 1, 1) - v

    def by_z(v):
        return jnp.where(last, 0.0, pltpu.roll(v, depth - 1, 0)) - v

    return (by_y(z) - by_z(y), by_z(x) - (z_next - z), (y_next - y) - by_y(x))


def curl_behind(x, y, z, y_prev, z_prev):
    first = z_index(x.shape) == 0

    def by_y(v):
        return v - pltpu.roll(v, 1, 1)

    def by_z(v):
        return v - jnp.where(first, 0.0, pltpu.roll(v, 1, 0))

    return (by_y(z) - by_z(y), by_z(x) - (z - z_prev), (y - y_prev) - by_y(x))


def lane_mask(width, tile_cols, column, count_cols):
    lane = lax.broadcasted_iota(jnp.int32, (1, width), 1)
    upper = tile_cols + jnp.where(column < count_cols - 1, GHOST, 0)
    lower = width - jnp.where(column > 0, GHOST, 0)
    return jnp.where((lane < upper) | (lane >= lower), 1.0, 0.0)


def row_mask(row, ghost, tile_rows, place, count_rows):
    low = jnp.where(place > 0, 1.0, 0.0)
    high = jnp.where(place < count_rows - 1, 1.0, 0.0)
    return jnp.where(row < ghost, low, jnp.where(row >= ghost + tile_rows, high, 1.0))


def pack_kernel(place, e, h, material, row_a, row_b, col_a, col_b):
    tile_rows, depth, tile_cols = material.shape
    even_x = place[0] % 2 == 0
    even_y = place[1] % 2 == 0
    start_a = jnp.where(even_x, tile_rows - GHOST, 0)
    start_b = jnp.where(even_x, 0, tile_rows - GHOST)
    lane = lax.broadcasted_iota(jnp.int32, (depth, tile_cols), 1)
    for part in range(7):

        def planes(index):
            if part < 3:
                return e[part, index]
            if part < 6:
                return h[part - 3, index]
            return material[index].astype(F32)

        row_a[part] = planes(pl.ds(start_a, GHOST))
        row_b[part] = planes(pl.ds(start_b, GHOST))
        first = jnp.zeros((depth, tile_cols), F32)
        last = first
        for x in range(tile_rows):
            plane = planes(x)
            spot = (lane >= GHOST * x) & (lane < GHOST * (x + 1))
            shift = GHOST * x
            first = jnp.where(spot, pltpu.roll(plane, shift, 1) if shift else plane, first)
            shift = (GHOST * (x + 1)) % tile_cols
            last = jnp.where(spot, pltpu.roll(plane, shift, 1) if shift else plane, last)
        col_a[part] = jnp.where(even_y, last, first)
        col_b[part] = jnp.where(even_y, first, last)


def forward_kernel(
    counts, place, eps, e, h, material, row_a, row_b, col_a, col_b, cor_a, cor_b, weights, table, twist,
    kept, inverse, mid, field, stash, lens,
):
    tile_rows, depth, tile_cols = material.shape
    width = field.shape[3]
    count_rows, count_cols = counts
    i, j = place[0], place[1]
    even_x = i % 2 == 0
    even_y = j % 2 == 0
    far_edge = GHOST + tile_rows
    off_a = jnp.where(even_x, far_edge, 0)
    off_b = jnp.where(even_x, 0, far_edge)
    lane = lax.broadcasted_iota(jnp.int32, (depth, tile_cols), 1)

    def turn(value, shift):
        shift = shift % tile_cols
        return pltpu.roll(value, shift, 1) if shift else value

    def ghosts(right, left, x):
        left = jnp.where(lane >= tile_cols - GHOST, turn(left, -GHOST - GHOST * x), 0.0)
        return jnp.where(lane < GHOST, turn(right, -GHOST * x), left)

    for part in range(7):
        target = field.at[part] if part < 6 else inverse
        if part < 3:
            target[GHOST:far_edge, :, :tile_cols] = e[part]
        elif part < 6:
            target[GHOST:far_edge, :, :tile_cols] = h[part - 3]
        else:
            target[GHOST:far_edge, :, :tile_cols] = material[...].astype(F32)
        target[pl.ds(off_a, GHOST), :, :tile_cols] = row_a[part]
        target[pl.ds(off_b, GHOST), :, :tile_cols] = row_b[part]
        a, b = col_a[part], col_b[part]
        right, left = jnp.where(even_y, a, b), jnp.where(even_y, b, a)
        for x in range(tile_rows):
            target[GHOST + x, :, tile_cols:] = ghosts(right, left, x)
        a, b = cor_a[part], cor_b[part]
        for corner, base, skip in (
            (jnp.where(even_x, b, a), 0, tile_rows - GHOST),
            (jnp.where(even_x, a, b), far_edge, 0),
        ):
            turned = turn(corner, -GHOST * tile_rows)
            right, left = jnp.where(even_y, corner, turned), jnp.where(even_y, turned, corner)
            for x in range(GHOST):
                target[base + x, :, tile_cols:] = ghosts(right, left, skip + x)

    mask = lane_mask(width, tile_cols, j, count_cols)

    def masked(row):
        return (0.5 * row_mask(row, GHOST, tile_rows, i, count_rows)) * mask

    def invert(row, carry):
        index = inverse[row]
        permittivity = jnp.full(index.shape, eps[0], F32)
        for m in range(1, NMAT):
            permittivity = jnp.where(index == float(m), eps[m], permittivity)
        inverse[row] = masked(row) / permittivity
        return carry

    lax.fori_loop(0, tile_rows + 2 * GHOST, invert, 0)

    for n in range(ITERS):

        def magnetic_row(r, carry):
            curl = curl_ahead(field[0, r], field[1, r], field[2, r], field[1, r + 1], field[2, r + 1])
            scale = masked(r)
            for part in range(3):
                field[3 + part, r] = field[3 + part, r] - scale * curl[part]
            return carry

        def electric_row(r, carry):
            curl = curl_behind(field[3, r], field[4, r], field[5, r], field[4, r - 1], field[5, r - 1])
            scale = inverse[r]
            new = []
            for part in range(3):
                value = field[part, r] + scale * curl[part]
                field[part, r] = value
                new.append(value)
            return (curl, new) if carry is None else carry

        def own_rows(q, carry):
            for s in range(2):
                x = 2 * q + s
                curl, new = electric_row(GHOST + x, None)
                for part in range(3):
                    kept[n, part, x] = curl[part][:, :tile_cols]
                for part in range(2):
                    high, low = split(new[part][:, :tile_cols])
                    spot = slice(s * tile_cols, (s + 1) * tile_cols)
                    stash[part, q, 2 * n * depth : (2 * n + 1) * depth, spot] = high
                    stash[part, q, (2 * n + 1) * depth : (2 * n + 2) * depth, spot] = low
            return carry

        last = tile_rows + 2 * GHOST - 1 - n
        lax.fori_loop(n, last, magnetic_row, 0)
        if n + 1 < GHOST:
            lax.fori_loop(n + 1, GHOST, electric_row, 0)
        lax.fori_loop(0, tile_rows // 2, own_rows, 0)
        if last > far_edge:
            lax.fori_loop(far_edge, last, electric_row, 0)

    waves = 2 * NF
    for p in range(2):
        for q in range(tile_rows // 2):
            both = dot(weights[...], stash[p, q])
            both = both[:waves] + both[waves:]
            for s in range(2):
                base = (p * tile_rows + 2 * q + s) * waves
                lens[base : base + waves, :] = both[:, s * tile_cols : (s + 1) * tile_cols]
    planes = 2 * tile_rows
    for f in range(NF):
        real = lens[pl.ds(f, planes, stride=waves), :]
        imag = lens[pl.ds(NF + f, planes, stride=waves), :]
        high, low = split(jnp.concatenate([real, imag], axis=1))
        phases = jnp.concatenate([table[f, :, :tile_cols], table[f, :, width : width + tile_cols]], axis=1)
        both = lax.dot_general(
            jnp.concatenate([high, low], axis=0), phases, (((1,), (1,)), ((), ())), preferred_element_type=F32
        )
        both = both[:planes] + both[planes:]
        both = both[:, : 2 * FAR] + both[:, 2 * FAR :]
        mid[f] = both * twist[0, j, f : f + 1, :] + half_turn(both) * twist[1, j, f : f + 1, :]


def backward_kernel(
    counts, place, own, sibling, target, kept, inverse, rows_far, rows_back, table, twist, weights,
    gradient, squares, mid, far, intensity, back, source, electric, magnetic, scaled, accum,
):
    tile_rows, depth, tile_cols = gradient.shape
    width = inverse.shape[2]
    count_rows, count_cols = counts
    i, j = place[0], place[1]
    samples = NF * FAR * FAR
    wide = 2 * FAR
    for k in range(count_rows // 2):
        near = i ^ (2 * k)
        for block, index in ((own, near), (sibling, near ^ 1)):
            spot = pl.ds(pl.multiple_of(index * tile_rows, 8), tile_rows)
            for p in range(2):
                for f in range(NF):
                    mid[f, spot, p * wide : (p + 1) * wide] = block[k, f, p * tile_rows : (p + 1) * tile_rows, :]

    sign = jnp.where(lax.broadcasted_iota(jnp.int32, (1, wide), 1) < FAR, 1.0, -1.0)
    total = jnp.zeros((FAR, wide), F32)
    for f in range(NF):
        high, low = split(mid[f])
        both = dot(rows_far[f], jnp.concatenate([high, low, high], axis=0))
        level = jnp.zeros((FAR, wide), F32)
        for p in range(2):
            cos = both[:FAR, p * wide : (p + 1) * wide]
            sin = both[FAR:, p * wide : (p + 1) * wide]
            value = cos + sign * half_turn(sin)
            far[f, :, p * wide : (p + 1) * wide] = value
            level = level + value * value
        level = level + half_turn(level)
        intensity[f] = level
        total = total + level
    power = jnp.sum(total, keepdims=True) / (2.0 * samples)
    total = jnp.zeros((FAR, wide), F32)
    for f in range(NF):
        level = intensity[f]
        total = total + (level / power - target[f]) * level
    spread = jnp.sum(total, keepdims=True) / (2.0 * samples * power)

    mask = lane_mask(width, tile_cols, j, count_cols)
    span = rows_back.shape[2] - count_rows * tile_rows + tile_rows
    row = lax.broadcasted_iota(jnp.int32, (2 * span, 1), 0)
    row = jnp.where(row >= span, row - span, row)
    lowest = jnp.where(i > 0, 0, BACK)
    highest = jnp.where(i < count_rows - 1, span, BACK + tile_rows)
    inside = jnp.where((row >= lowest) & (row < highest), 1.0, 0.0)
    waves = 2 * NF
    for f in range(NF):
        slope = 2.0 / power * (intensity[f] / power - target[f] - spread)
        slope = 2.0 * slope
        high, low = split(far[f] * jnp.concatenate([slope, slope], axis=1))
        start = pl.multiple_of(i * tile_rows, 8)
        phases = jnp.concatenate(
            [rows_back[f, 0, pl.ds(start, span), :], rows_back[f, 1, pl.ds(start, span), :]], axis=0
        )
        phase_high, phase_low = split(phases)
        both = dot(phase_high, high) + dot(phase_high, low) + dot(phase_low, high)
        turned = []
        for p in range(2):
            cos = both[:span, p * wide : (p + 1) * wide]
            sin = both[span:, p * wide : (p + 1) * wide]
            value = cos - sign * half_turn(sin)
            turned.append(value * twist[0, j, f : f + 1, :] - half_turn(value) * twist[1, j, f : f + 1, :])
        high, low = split(jnp.concatenate(turned, axis=0))
        left = jnp.concatenate(
            [jnp.concatenate([high, high], axis=1), jnp.concatenate([low, low], axis=1)], axis=0
        )
        both = dot(left, table[f])
        both = (both[: 2 * span] + both[2 * span :]) * inside
        for part in range(2):
            value = both[:, part * width : (part + 1) * width] * mask
            for p in range(2):
                for s in range(width // 128):
                    back[2 * p + s, pl.ds(part * NF + f, span, stride=waves), :] = value[
                        p * span : (p + 1) * span, s * 128 : (s + 1) * 128
                    ]

    ext = tile_rows + 2 * BACK

    def source_row(r, carry):
        spot = pl.ds(pl.multiple_of(r * waves, 8), waves)
        for p in range(2):
            high, low = split(jnp.concatenate([back[2 * p, spot, :], back[2 * p + 1, spot, :]], axis=1))
            both = dot(weights[...], jnp.concatenate([high, low, high], axis=0))
            for n in range(ITERS):
                source[n, p, r] = both[n * depth : (n + 1) * depth]
        return carry

    lax.fori_loop(0, ext, source_row, 0)

    def masked(r):
        return (0.5 * row_mask(r, BACK, tile_rows, i, count_rows)) * mask

    for n in reversed(range(ITERS)):
        first = n == ITERS - 1

        def add_source(r):
            new = []
            for part in range(3):
                if part == 2:
                    value = jnp.zeros((depth, width), F32) if first else electric[2, r]
                elif first:
                    value = source[n, part, r]
                else:
                    value = electric[part, r] + source[n, part, r]
                if n > 0:
                    electric[part, r] = value
                    scaled[part, r] = inverse[r + GHOST - BACK] * value
                new.append(value)
            return new

        def ghost_row(r, carry):
            add_source(r)
            return carry

        def own_row(x, carry):
            new = add_source(BACK + x)
            value = new[0][:, :tile_cols] * kept[n, 0, x]
            for part in range(1, 3):
                value = value + new[part][:, :tile_cols] * kept[n, part, x]
            accum[x] = value if first else accum[x] + value
            return carry

        def magnetic_row(r, carry):
            curl = curl_ahead(scaled[0, r], scaled[1, r], scaled[2, r], scaled[1, r + 1], scaled[2, r + 1])
            scale = masked(r)
            for part in range(3):
                value = scale * curl[part]
                magnetic[part, r] = value if first else magnetic[part, r] + value
            return carry

        def electric_row(r, carry):
            curl = curl_behind(
                magnetic[0, r], magnetic[1, r], magnetic[2, r], magnetic[1, r - 1], magnetic[2, r - 1]
            )
            for part in range(3):
                electric[part, r] = electric[part, r] - curl[part]
            return carry

        low, high = BACK - n, BACK + tile_rows + n
        if n > 0:
            lax.fori_loop(low, BACK, ghost_row, 0)
        lax.fori_loop(0, tile_rows, own_row, 0)
        if n > 0:
            lax.fori_loop(BACK + tile_rows, high, ghost_row, 0)
            lax.fori_loop(low, high - 1, magnetic_row, 0)
            lax.fori_loop(low + 1, high - 1, electric_row, 0)

    total = jnp.zeros((depth, tile_cols), F32)
    for x in range(tile_rows):
        value = inverse[GHOST + x, :, :tile_cols]
        value = -2.0 * (value * value) * accum[x]
        gradient[x] = value
        total = total + value * value
    squares[...] = jnp.broadcast_to(jnp.sum(total, keepdims=True), squares.shape)


def scale_kernel(cells, squares, gradient, result):
    copies = 8 * squares.shape[1]
    total = jnp.sum(squares[...], keepdims=True) / copies
    scale = 1.0 / jnp.sqrt(total / cells + 1e-06)
    for x in range(gradient.shape[0]):
        result[x] = gradient[x] * scale


SMEM = pl.BlockSpec(memory_space=pltpu.SMEM)
VMEM = pl.BlockSpec(memory_space=pltpu.VMEM)


def call(kernel, name, specs, outs, scratch=()):
    return pl.pallas_call(
        kernel,
        name=name,
        in_specs=specs,
        out_specs=jax.tree.map(lambda _: VMEM, outs),
        out_shape=outs,
        scratch_shapes=scratch,
        compiler_params=pltpu.CompilerParams(vmem_limit_bytes=VMEM_BYTES),
    )


def array(*shape):
    return jax.ShapeDtypeStruct(shape, F32)


def even_pairs(count):
    return [(k, k ^ 1) for k in range(count)]


def odd_pairs(count):
    return [(k, k + 1 if k % 2 else k - 1) for k in range(1, count - 1)]


def body(count_rows, count_cols, e_init, h_init, material, eps_table, target):
    tile_rows, depth, tile_cols = material.shape
    width = 2 * tile_cols
    counts = (count_rows, count_cols)
    place = jnp.stack([lax.axis_index("gx"), lax.axis_index("gy")]).astype(jnp.int32)

    edge = array(7, GHOST, depth, tile_cols)
    side = array(7, depth, tile_cols)
    row_a, row_b, col_a, col_b = call(
        pack_kernel, "pack", [SMEM, VMEM, VMEM, VMEM], (edge, edge, side, side)
    )(place, e_init, h_init, material)
    col_a = lax.ppermute(col_a, "gy", even_pairs(count_cols))
    col_b = lax.ppermute(col_b, "gy", odd_pairs(count_cols))
    row_b = lax.ppermute(row_b, "gx", odd_pairs(count_rows))
    row_a = lax.ppermute(row_a, "gx", even_pairs(count_rows))
    used = GHOST * tile_rows
    corner = jnp.concatenate(
        [col_a[..., :used], col_b[..., :used], jnp.zeros(side.shape[:2] + (tile_cols - 2 * used,), F32)], axis=2
    )
    cor_b = lax.ppermute(corner, "gx", odd_pairs(count_rows))
    cor_a = lax.ppermute(corner, "gx", even_pairs(count_rows))

    table = jnp.asarray(column_table(tile_cols, width))
    twist = jnp.asarray(column_twist(count_cols))
    ext = tile_rows + 2 * GHOST
    waves = 2 * NF
    kept, inverse, mid = call(
        functools.partial(forward_kernel, counts),
        "forward",
        [SMEM, SMEM] + [VMEM] * 12,
        (
            array(ITERS, 3, tile_rows, depth, tile_cols),
            array(ext, depth, width),
            array(NF, 2 * tile_rows, 2 * FAR),
        ),
        [
            pltpu.VMEM((6, ext, depth, width), F32),
            pltpu.VMEM((2, tile_rows // 2, 2 * ITERS * depth, 2 * tile_cols), BF16),
            pltpu.VMEM((2 * tile_rows * waves, tile_cols), F32),
        ],
    )(
        place, eps_table, e_init, h_init, material, row_a, row_b, col_a, col_b, cor_a, cor_b,
        jnp.asarray(lens_table(depth)), table, twist,
    )

    whole = mid
    for k in range(1, count_cols):
        whole = whole + lax.ppermute(mid, "gy", [(n, n ^ k) for n in range(count_cols)])
    own = jnp.stack(
        [whole]
        + [lax.ppermute(whole, "gx", [(n, n ^ k) for n in range(count_rows)]) for k in range(2, count_rows, 2)]
    )
    sibling = lax.ppermute(own, "gx", even_pairs(count_rows))

    rows = count_rows * tile_rows
    ext = tile_rows + 2 * BACK
    span = tile_rows + 16
    devices = count_rows * count_cols
    grid = pltpu.VMEM((3, ext, depth, width), F32)
    gradient, squares = call(
        functools.partial(backward_kernel, counts),
        "backward",
        [SMEM] + [VMEM] * 10,
        (array(tile_rows, depth, tile_cols), array(8 * devices, 128)),
        [
            pltpu.VMEM((NF, rows, 4 * FAR), F32),
            pltpu.VMEM((NF, FAR, 4 * FAR), F32),
            pltpu.VMEM((NF, FAR, 2 * FAR), F32),
            pltpu.VMEM((2 * width // 128, span * waves, 128), F32),
            pltpu.VMEM((ITERS, 2, ext, depth, width), F32),
            grid,
            grid,
            grid,
            pltpu.VMEM((tile_rows, depth, tile_cols), F32),
        ],
    )(
        place, own, sibling, jnp.concatenate([target, target], axis=2), kept, inverse,
        jnp.asarray(row_table(rows)), jnp.asarray(row_back_table(rows)), table, twist,
        jnp.asarray(source_table(depth)),
    )
    squares = lax.all_to_all(squares, ("gx", "gy"), 0, 0, tiled=True)
    cells = rows * depth * tile_cols * count_cols
    return call(
        functools.partial(scale_kernel, cells), "scale", [VMEM, VMEM], array(tile_rows, depth, tile_cols)
    )(squares, gradient)


def solution(mesh):
    in_specs = (P(None, "gx", None, "gy"), P(None, "gx", None, "gy"), P("gx", None, "gy"), P(), P())
    out_specs = P("gx", None, "gy")
    part = functools.partial(body, mesh.shape["gx"], mesh.shape["gy"])
    return jax.shard_map(part, mesh=mesh, in_specs=in_specs, out_specs=out_specs, check_vma=False)
```

profile of v0, /device:TPU:0, one launch (start us, length us, event | category | flops | bytes accessed | tf_op | source)
XLA Modules:
  0.0 102.7 jit_solution(17995798796719998034)
XLA Ops:
  0.0 0.6 pad_add_fusion.place
  0.6 2.8 %pack.1 = (f32[7,6,32,128]{3,2,1,0:T(8,128)}, f32[7,6,32,128]{3,2,1,0:T(8,128)}, f32[7,32,128]{2,1,0:T(8,128)}, f32[7,32,128]{2,1,0:T(8,128)}) custom-call(s32[2]{0:T(128)} %pad_add_fusion.place, f32[3,8,32,128]{3,2,1,0:T(8,128)} %e.3, f32[3,8,32,128]{3,2,1,0:T(8,128)} %h.3, s32[8,32,128]{2,1,0:T(8,128)} %material.3), custom_call_target="tpu_custom_call" | custom-call | tf_op jit(solution)/shard_map/pack/pallas_call | solution.py:507
  3.4 0.5 collective-permute-start
  3.9 0.7 collective-permute-start.1
  4.6 0.7 collective-permute-start.3
  5.3 5.3 %collective-permute-start.2 = (f32[7,32,128]{2,1,0:T(8,128)}, f32[7,32,128]{2,1,0:T(8,128)S(1)}, u32[]{:S(2)}, u32[]{:S(2)}) collective-permute-start(f32[7,32,128]{2,1,0:T(8,128)} %get-tuple-element.16), channel_id=1, source_target_pairs={{0,1},{1,0},{2,3},{3,2},{4,5},{5,4},{6,7},{7,6},{8,9},{9,8},{10,11... | collective-permute-start | bytes 344072 | tf_op jit(solution)/shard_map/ppermute | solution.py:510
  10.5 0.1 pad.8.clone
  10.6 0.0 collective-permute-done.3.col_b
  10.6 0.0 copy-start.3
  10.6 4.5 %collective-permute-done.2.col_a = f32[7,32,128]{2,1,0:T(8,128)S(1)} collective-permute-done((f32[7,32,128]{2,1,0:T(8,128)}, f32[7,32,128]{2,1,0:T(8,128)S(1)}, u32[]{:S(2)}, u32[]{:S(2)}) %collective-permute-start.2) | collective-permute-done | bytes 114720 | tf_op jit(solution)/shard_map/ppermute | solution.py:510
  15.1 0.0 copy-start.4
  15.1 0.1 maximum_maximum_fusion
  15.2 0.0 copy-start.6
  15.2 1.9 %collective-permute-start.4 = (f32[7,32,128]{2,1,0:T(8,128)S(1)}, f32[7,32,128]{2,1,0:T(8,128)S(1)}, u32[]{:S(2)}, u32[]{:S(2)}) collective-permute-start(f32[7,32,128]{2,1,0:T(8,128)S(1)} %maximum_maximum_fusion), channel_id=1, source_target_pairs={{0,4},{4,0},{8,12},{12,8},{16,20},{20,16},{24,28},{28,24},{1,5},{5... | collective-permute-start | bytes 344072 | tf_op jit(solution)/shard_map/ppermute | solution.py:519
  17.1 0.7 collective-permute-start.5
  17.8 0.3 collective-permute-done.4.cor_a
  18.1 0.0 copy-start.7
  18.1 0.0 collective-permute-done.5.cor_b
  18.1 0.0 copy-start.8
  18.1 0.0 collective-permute-done.row_a
  18.1 0.0 copy-start.1
  18.1 0.0 collective-permute-done.1.row_b
  18.1 0.0 copy-done.3
  18.1 0.0 copy-done.4
  18.1 0.6 copy-done.7
  18.7 0.1 copy-done.8
  18.8 0.3 copy-done.1
  19.0 0.0 copy-start.2
  19.0 0.9 copy-done.2
  19.9 19.6 %forward.1 = (f32[6,3,8,32,128]{4,3,2,1,0:T(8,128)}, f32[20,32,256]{2,1,0:T(8,128)}, f32[8,16,128]{2,1,0:T(8,128)}) custom-call(s32[2]{0:T(128)} %pad_add_fusion.place, f32[8]{0:T(128)} %eps.1, f32[3,8,32,128]{3,2,1,0:T(8,128)} %e.3, f32[3,8,32,128]{3,2,1,0:T(8,128)} %h.3, s32[8,32,128]{2,1,0:T(8,128)} %material.3, f32[7,6,32,128]{3,2,1,0:T(8,128)} %copy-done.1, ...), custom_call_target="tpu_custom_call" | custom-call | tf_op jit(solution)/shard_map/forward/pallas_call | solution.py:525
  39.5 0.2 collective-permute-start.6
  39.8 1.8 %collective-permute-start.7 = (f32[8,16,128]{2,1,0:T(8,128)}, f32[8,16,128]{2,1,0:T(8,128)S(1)}, u32[]{:S(2)}, u32[]{:S(2)}) collective-permute-start(f32[8,16,128]{2,1,0:T(8,128)} %get-tuple-element.18), channel_id=1, source_target_pairs={{0,2},{1,3},{2,0},{3,1},{4,6},{5,7},{6,4},{7,5},{8,10},{9,11},{10,... | collective-permute-start | bytes 196616 | tf_op jit(solution)/shard_map/ppermute | solution.py:546
  41.5 1.5 %collective-permute-start.8 = (f32[8,16,128]{2,1,0:T(8,128)}, f32[8,16,128]{2,1,0:T(8,128)S(1)}, u32[]{:S(2)}, u32[]{:S(2)}) collective-permute-start(f32[8,16,128]{2,1,0:T(8,128)} %get-tuple-element.18), channel_id=1, source_target_pairs={{0,3},{1,2},{2,1},{3,0},{4,7},{5,6},{6,5},{7,4},{8,11},{9,10},{10,... | collective-permute-start | bytes 196616 | tf_op jit(solution)/shard_map/ppermute | solution.py:546
  43.0 1.0 collective-permute-done.6
  44.0 0.2 collective-permute-done.7
  44.2 2.7 %collective-permute-done.8 = f32[8,16,128]{2,1,0:T(8,128)S(1)} collective-permute-done((f32[8,16,128]{2,1,0:T(8,128)}, f32[8,16,128]{2,1,0:T(8,128)S(1)}, u32[]{:S(2)}, u32[]{:S(2)}) %collective-permute-start.8) | collective-permute-done | bytes 65568 | tf_op jit(solution)/shard_map/ppermute | solution.py:546
  46.9 0.9 add_add_fusion
  47.8 8.6 %collective-permute-start.9 = (f32[8,16,128]{2,1,0:T(8,128)S(1)}, f32[8,16,128]{2,1,0:T(8,128)S(1)}, u32[]{:S(2)}, u32[]{:S(2)}) collective-permute-start(f32[8,16,128]{2,1,0:T(8,128)S(1)} %add_add_fusion), channel_id=1, source_target_pairs={{0,8},{4,12},{8,0},{12,4},{16,24},{20,28},{24,16},{28,20},{1,9},{5... | collective-permute-start | bytes 196616 | tf_op jit(solution)/shard_map/ppermute | solution.py:549
  56.4 1.3 %collective-permute-start.10 = (f32[8,16,128]{2,1,0:T(8,128)S(1)}, f32[8,16,128]{2,1,0:T(8,128)S(1)}, u32[]{:S(2)}, u32[]{:S(2)}) collective-permute-start(f32[8,16,128]{2,1,0:T(8,128)S(1)} %add_add_fusion), channel_id=1, source_target_pairs={{0,16},{4,20},{8,24},{12,28},{16,0},{20,4},{24,8},{28,12},{1,17},{... | collective-permute-start | bytes 196616 | tf_op jit(solution)/shard_map/ppermute | solution.py:549
  57.7 1.2 %collective-permute-start.11 = (f32[8,16,128]{2,1,0:T(8,128)S(1)}, f32[8,16,128]{2,1,0:T(8,128)S(1)}, u32[]{:S(2)}, u32[]{:S(2)}) collective-permute-start(f32[8,16,128]{2,1,0:T(8,128)S(1)} %add_add_fusion), channel_id=1, source_target_pairs={{0,24},{4,28},{8,16},{12,20},{16,8},{20,12},{24,0},{28,4},{1,25},{... | collective-permute-start | bytes 196616 | tf_op jit(solution)/shard_map/ppermute | solution.py:549
  58.9 0.4 collective-permute-done.9
  59.3 3.3 %collective-permute-done.10 = f32[8,16,128]{2,1,0:T(8,128)S(1)} collective-permute-done((f32[8,16,128]{2,1,0:T(8,128)S(1)}, f32[8,16,128]{2,1,0:T(8,128)S(1)}, u32[]{:S(2)}, u32[]{:S(2)}) %collective-permute-start.10) | collective-permute-done | bytes 65568 | tf_op jit(solution)/shard_map/ppermute | solution.py:549
  62.6 1.3 %collective-permute-done.11 = f32[8,16,128]{2,1,0:T(8,128)S(1)} collective-permute-done((f32[8,16,128]{2,1,0:T(8,128)S(1)}, f32[8,16,128]{2,1,0:T(8,128)S(1)}, u32[]{:S(2)}, u32[]{:S(2)}) %collective-permute-start.11) | collective-permute-done | bytes 65568 | tf_op jit(solution)/shard_map/ppermute | solution.py:549
  63.9 0.0 copy-start
  63.9 0.1 collective-permute-start.12
  64.0 0.0 copy-done.6
  64.0 0.8 pad_maximum_fusion.1.target
  64.8 0.7 collective-permute-done.12.sibling
  65.5 0.0 copy-start.5
  65.5 0.0 copy-done
  65.5 0.7 copy-done.5
  66.2 23.1 %backward.1 = (f32[8,32,128]{2,1,0:T(8,128)}, f32[256,128]{1,0:T(8,128)}) custom-call(s32[2]{0:T(128)} %pad_add_fusion.place, f32[4,8,16,128]{3,2,1,0:T(8,128)} %copy-done, f32[4,8,16,128]{3,2,1,0:T(8,128)} %copy-done.5, f32[8,64,128]{2,1,0:T(8,128)} %pad_maximum_fusion.1.target, f32[6,3,8,32,128]{4,3,2,1,0:T(8,128)} %get-tuple-element.19.kept, ...), custom_call_target="tpu_custom_call" | custom-call | tf_op jit(solution)/shard_map/backward/pallas_call | solution.py:558
  89.3 11.7 %all_to_all.11 = f32[32,8,128]{2,1,0:T(8,128)} all-to-all(f32[32,8,128]{2,1,0:T(8,128)} %bitcast.14), channel_id=1, replica_groups=mesh['gx'=8,'gy'=4] {'gx','gy'}, dimensions={0} | all-to-all | bytes 262144 | tf_op jit(solution)/shard_map/all_to_all | solution.py:579
  100.9 1.8 %scale.1 = f32[8,32,128]{2,1,0:T(8,128)} custom-call(f32[256,128]{1,0:T(8,128)} %bitcast.10, f32[8,32,128]{2,1,0:T(8,128)} %get-tuple-element.22.gradient), custom_call_target="tpu_custom_call" | custom-call | tf_op jit(solution)/shard_map/scale/pallas_call | solution.py:581
  (2 shorter events, 0.0 us)
Async XLA Ops:
  3.4 14.7 %collective-permute-start = (f32[7,6,32,128]{3,2,1,0:T(8,128)}, f32[7,6,32,128]{3,2,1,0:T(8,128)S(1)}, u32[]{:S(2)}, u32[]{:S(2)}) collective-permute-start(f32[7,6,32,128]{3,2,1,0:T(8,128)} %get-tuple-element.14), channel_id=1, source_target_pairs={{0,4},{4,0},{8,12},{12,8},{16,20},{20,16},{24,28},{28,24},{1,5},{5... | collective-permute-start | bytes 2064392 | tf_op jit(solution)/shard_map/ppermute | solution.py:513
  3.9 14.2 %collective-permute-start.1 = (f32[7,6,32,128]{3,2,1,0:T(8,128)}, f32[7,6,32,128]{3,2,1,0:T(8,128)S(1)}, u32[]{:S(2)}, u32[]{:S(2)}) collective-permute-start(f32[7,6,32,128]{3,2,1,0:T(8,128)} %get-tuple-element.15), channel_id=1, source_target_pairs={{4,8},{8,4},{12,16},{16,12},{20,24},{24,20},{5,9},{9,5},{13,17},{1... | collective-permute-start | bytes 2064392 | tf_op jit(solution)/shard_map/ppermute | solution.py:512
  4.6 6.0 %collective-permute-start.3 = (f32[7,32,128]{2,1,0:T(8,128)}, f32[7,32,128]{2,1,0:T(8,128)S(1)}, u32[]{:S(2)}, u32[]{:S(2)}) collective-permute-start(f32[7,32,128]{2,1,0:T(8,128)} %get-tuple-element.17), channel_id=1, source_target_pairs={{1,2},{2,1},{5,6},{6,5},{9,10},{10,9},{13,14},{14,13},{17,18},{18,... | collective-permute-start | bytes 344072 | tf_op jit(solution)/shard_map/ppermute | solution.py:511
  5.3 9.9 %collective-permute-start.2 = (f32[7,32,128]{2,1,0:T(8,128)}, f32[7,32,128]{2,1,0:T(8,128)S(1)}, u32[]{:S(2)}, u32[]{:S(2)}) collective-permute-start(f32[7,32,128]{2,1,0:T(8,128)} %get-tuple-element.16), channel_id=1, source_target_pairs={{0,1},{1,0},{2,3},{3,2},{4,5},{5,4},{6,7},{7,6},{8,9},{9,8},{10,11... | collective-permute-start | bytes 344072 | tf_op jit(solution)/shard_map/ppermute | solution.py:510
  10.6 7.5 %copy-start.3 = (f32[7,32,128]{2,1,0:T(8,128)}, f32[7,32,128]{2,1,0:T(8,128)S(1)}, u32[]{:S(2)}) copy-start(f32[7,32,128]{2,1,0:T(8,128)S(1)} %collective-permute-done.3.col_b) | copy-start | bytes 344068
  15.1 3.0 %copy-start.4 = (f32[7,32,128]{2,1,0:T(8,128)}, f32[7,32,128]{2,1,0:T(8,128)S(1)}, u32[]{:S(2)}) copy-start(f32[7,32,128]{2,1,0:T(8,128)S(1)} %collective-permute-done.2.col_a) | copy-start | bytes 344068
  15.2 48.8 %copy-start.6 = (f32[8,64,64]{2,1,0:T(8,128)S(1)}, f32[8,64,64]{2,1,0:T(8,128)}, u32[]{:S(2)}) copy-start(f32[8,64,64]{2,1,0:T(8,128)} %param.15) | copy-start | bytes 393220
  15.2 2.8 %collective-permute-start.4 = (f32[7,32,128]{2,1,0:T(8,128)S(1)}, f32[7,32,128]{2,1,0:T(8,128)S(1)}, u32[]{:S(2)}, u32[]{:S(2)}) collective-permute-start(f32[7,32,128]{2,1,0:T(8,128)S(1)} %maximum_maximum_fusion), channel_id=1, source_target_pairs={{0,4},{4,0},{8,12},{12,8},{16,20},{20,16},{24,28},{28,24},{1,5},{5... | collective-permute-start | bytes 344072 | tf_op jit(solution)/shard_map/ppermute | solution.py:519
  17.1 1.0 collective-permute-start.5
  18.1 0.6 copy-start.7
  18.1 0.7 copy-start.8
  18.1 0.9 copy-start.1
  19.0 0.9 copy-start.2
  39.5 4.5 %collective-permute-start.6 = (f32[8,16,128]{2,1,0:T(8,128)}, f32[8,16,128]{2,1,0:T(8,128)S(1)}, u32[]{:S(2)}, u32[]{:S(2)}) collective-permute-start(f32[8,16,128]{2,1,0:T(8,128)} %get-tuple-element.18), channel_id=1, source_target_pairs={{0,1},{1,0},{2,3},{3,2},{4,5},{5,4},{6,7},{7,6},{8,9},{9,8},{10,11... | collective-permute-start | bytes 196616 | tf_op jit(solution)/shard_map/ppermute | solution.py:546
  39.8 4.5 %collective-permute-start.7 = (f32[8,16,128]{2,1,0:T(8,128)}, f32[8,16,128]{2,1,0:T(8,128)S(1)}, u32[]{:S(2)}, u32[]{:S(2)}) collective-permute-start(f32[8,16,128]{2,1,0:T(8,128)} %get-tuple-element.18), channel_id=1, source_target_pairs={{0,2},{1,3},{2,0},{3,1},{4,6},{5,7},{6,4},{7,5},{8,10},{9,11},{10,... | collective-permute-start | bytes 196616 | tf_op jit(solution)/shard_map/ppermute | solution.py:546
  41.5 5.4 %collective-permute-start.8 = (f32[8,16,128]{2,1,0:T(8,128)}, f32[8,16,128]{2,1,0:T(8,128)S(1)}, u32[]{:S(2)}, u32[]{:S(2)}) collective-permute-start(f32[8,16,128]{2,1,0:T(8,128)} %get-tuple-element.18), channel_id=1, source_target_pairs={{0,3},{1,2},{2,1},{3,0},{4,7},{5,6},{6,5},{7,4},{8,11},{9,10},{10,... | collective-permute-start | bytes 196616 | tf_op jit(solution)/shard_map/ppermute | solution.py:546
  47.8 11.5 %collective-permute-start.9 = (f32[8,16,128]{2,1,0:T(8,128)S(1)}, f32[8,16,128]{2,1,0:T(8,128)S(1)}, u32[]{:S(2)}, u32[]{:S(2)}) collective-permute-start(f32[8,16,128]{2,1,0:T(8,128)S(1)} %add_add_fusion), channel_id=1, source_target_pairs={{0,8},{4,12},{8,0},{12,4},{16,24},{20,28},{24,16},{28,20},{1,9},{5... | collective-permute-start | bytes 196616 | tf_op jit(solution)/shard_map/ppermute | solution.py:549
  56.4 6.2 %collective-permute-start.10 = (f32[8,16,128]{2,1,0:T(8,128)S(1)}, f32[8,16,128]{2,1,0:T(8,128)S(1)}, u32[]{:S(2)}, u32[]{:S(2)}) collective-permute-start(f32[8,16,128]{2,1,0:T(8,128)S(1)} %add_add_fusion), channel_id=1, source_target_pairs={{0,16},{4,20},{8,24},{12,28},{16,0},{20,4},{24,8},{28,12},{1,17},{... | collective-permute-start | bytes 196616 | tf_op jit(solution)/shard_map/ppermute | solution.py:549
  57.7 6.2 %collective-permute-start.11 = (f32[8,16,128]{2,1,0:T(8,128)S(1)}, f32[8,16,128]{2,1,0:T(8,128)S(1)}, u32[]{:S(2)}, u32[]{:S(2)}) collective-permute-start(f32[8,16,128]{2,1,0:T(8,128)S(1)} %add_add_fusion), channel_id=1, source_target_pairs={{0,24},{4,28},{8,16},{12,20},{16,8},{20,12},{24,0},{28,4},{1,25},{... | collective-permute-start | bytes 196616 | tf_op jit(solution)/shard_map/ppermute | solution.py:549
  63.9 1.6 %copy-start = (f32[4,8,16,128]{3,2,1,0:T(8,128)}, f32[4,8,16,128]{3,2,1,0:T(8,128)S(1)}, u32[]{:S(2)}) copy-start(f32[4,8,16,128]{3,2,1,0:T(8,128)S(1)} %pad_maximum_fusion.own) | copy-start | bytes 786436
  63.9 1.6 %collective-permute-start.12 = (f32[4,8,16,128]{3,2,1,0:T(8,128)S(1)}, f32[4,8,16,128]{3,2,1,0:T(8,128)S(1)}, u32[]{:S(2)}, u32[]{:S(2)}) collective-permute-start(f32[4,8,16,128]{3,2,1,0:T(8,128)S(1)} %pad_maximum_fusion.own), channel_id=1, source_target_pairs={{0,4},{4,0},{8,12},{12,8},{16,20},{20,16},{24,28},{28,24},{1,5},{5... | collective-permute-start | bytes 786440 | tf_op jit(solution)/shard_map/ppermute | solution.py:551
  65.5 0.7 copy-start.5
where the time goes:
time: 103 us
  Pallas kernels  47.3 us (46%)
  starting transfers between devices  24.3 us (24%)
  waiting for transfers between devices  14.3 us (14%)
  blocking collectives  11.7 us (11%)
  local copies, waits for them, and re-layouts  2.56 us (2%)
  other arithmetic  2.45 us (2%)
    pallas_call x1, Pallas kernels, body(): call(functools.partial(backward_kernel, counts), 'backward', [SMEM] + [VM...  23.1 us
    pallas_call x1, Pallas kernels, body(): call(functools.partial(forward_kernel, counts), 'forward', [SMEM, SMEM] +...  19.6 us
    all_to_all x1, blocking collectives, body(): squares = lax.all_to_all(squares, ('gx', 'gy'), 0, 0, tiled=True)  11.7 us
    ppermute x3, starting transfers between devices, body(): lax.ppermute(whole, 'gx', [(n, n ^ k) for n in range(count_rows)])  11.1 us
    ppermute x1, starting transfers between devices, body(): col_a = lax.ppermute(col_a, 'gy', even_pairs(count_cols))  5.29 us
    ppermute x3, waiting for transfers between devices, body(): lax.ppermute(whole, 'gx', [(n, n ^ k) for n in range(count_rows)])  4.96 us
    ppermute x1, waiting for transfers between devices, body(): col_a = lax.ppermute(col_a, 'gy', even_pairs(count_cols))  4.5 us
    ppermute x3, waiting for transfers between devices, body(): lax.ppermute(mid, 'gy', [(n, n ^ k) for n in range(count_cols)])  3.88 us
  transfers between devices with their start and end apart: 13, of which 9 were waited for; matrix products, arithmetic and copies ran while one was open for 1% of the time, Pallas kernels for 0%

commit v1 on v0

v1 whole, which is shorter than its diff:
```python
import functools
import math

import jax
import jax.numpy as jnp
import ml_dtypes
import numpy as np
from jax import lax
from jax.experimental import pallas as pl
from jax.experimental.pallas import tpu as pltpu
from jax.sharding import PartitionSpec as P

ITERS = 6
NF = 8
FAR = 64
NMAT = 8
GHOST = ITERS
BACK = ITERS - 1
TWO_PI = 2.0 * math.pi
F32 = jnp.float32
BF16 = jnp.bfloat16
PAD = 8
VMEM_BYTES = 64 * 1024 * 1024 - 65536
OWN_GROUP = 8
GROUP = 8


def split_table(table):
    high = table.astype(np.float32).astype(ml_dtypes.bfloat16)
    low = (table - high.astype(np.float64)).astype(np.float32).astype(ml_dtypes.bfloat16)
    return high, low


def time_table(depth):
    freq = np.arange(NF)[None, :, None]
    moment = np.arange(1, ITERS + 1)[:, None, None]
    turns = ((2 * freq + 1) * (7 * moment + np.arange(depth)[None, None, :])) % 64
    angle = turns * (TWO_PI / 64)
    return np.concatenate([np.cos(angle), -np.sin(angle)], axis=1)


def lens_table(depth):
    weights = time_table(depth)
    wide = np.stack([weights, weights], axis=2)
    wide = wide.transpose(1, 0, 2, 3).reshape(2 * NF, -1)
    return np.concatenate(split_table(wide), axis=0)


def source_table(depth):
    flat = time_table(depth).transpose(0, 2, 1).reshape(ITERS * depth, 2 * NF)
    high, low = split_table(flat)
    return np.concatenate([high, high, low], axis=1)


def phase(cells, length):
    freq = np.arange(NF)[:, None, None]
    order = np.arange(FAR)[None, :, None] - FAR // 2
    period = 4 * length * NF
    turns = (order * (2 * cells[None, None, :] + 1) * (NF + freq)) % period
    angle = turns * (TWO_PI / period)
    return np.cos(angle), np.sin(angle)


def column_table(tile_cols, width):
    lanes = np.arange(width)
    cells = np.where(lanes >= width - GHOST, lanes - width, lanes)
    used = (lanes < tile_cols + GHOST) | (lanes >= width - GHOST)
    cos, sin = (t * used[None, None, :] for t in phase(cells, tile_cols))
    return np.stack([np.concatenate(split_table(t), axis=1) for t in (cos, sin, -sin)])


def column_blocks(table, target, lanes):
    pairs = []
    for half in range(2):
        for row, col, block in ((0, 0, 0), (0, 1, 1), (1, 0, 2), (1, 1, 0)):
            start = (2 * half + row) * FAR
            pairs.append(
                (
                    table.at[block, :, half * FAR : (half + 1) * FAR, 0:lanes],
                    target.at[:, start : start + FAR, col * lanes : (col + 1) * lanes],
                )
            )
    return pairs


def column_twist(count_cols):
    freq = np.arange(NF)[None, :, None]
    order = np.arange(FAR)[None, None, :] - FAR // 2
    place = np.arange(count_cols)[:, None, None]
    angle = ((order * (NF + freq) * place) % 16) * (TWO_PI / 16)
    cos, sin = np.cos(angle), np.sin(angle)
    return np.stack(
        [np.concatenate([cos, cos], axis=2), np.concatenate([sin, -sin], axis=2)]
    ).astype(np.float32)


def row_table(rows):
    table = np.concatenate(phase(np.arange(rows), rows), axis=1)
    high, low = split_table(table)
    return np.concatenate([high, high, low], axis=2)


def row_back_table(rows):
    cells = np.arange(rows + 16) - BACK
    cos, sin = phase(cells, rows)
    return np.stack([cos, sin], axis=1).transpose(0, 1, 3, 2).astype(np.float32)


def split(value):
    high = value.astype(BF16)
    return high, (value - high.astype(F32)).astype(BF16)


def dot(left, right):
    return jnp.dot(left, right, preferred_element_type=F32)


def half_turn(value):
    return pltpu.roll(value, FAR, 1)


def ahead_y(own, ghost):
    last = lax.broadcasted_iota(jnp.int32, own.shape, 1) == own.shape[1] - 1
    a, b = (pltpu.roll(v, v.shape[1] - 1, 1) for v in (own, ghost))
    return (jnp.where(last, b, a) - own, jnp.where(last, a, b) - ghost)


def behind_y(own, ghost):
    first = lax.broadcasted_iota(jnp.int32, own.shape, 1) == 0
    a, b = (pltpu.roll(v, 1, 1) for v in (own, ghost))
    return (own - jnp.where(first, b, a), ghost - jnp.where(first, a, b))


def depths(ref, shift=0):
    return slice(PAD + shift, ref.shape[3] - PAD + shift)


def curl_ahead(ref, r):
    def row(part, step=0, shift=0):
        return [ref[part, r + step, s, depths(ref, shift), :] for s in range(2)]

    x, y, z = row(0), row(1), row(2)
    y_next, z_next = row(1, 1), row(2, 1)
    x_deep, y_deep = row(0, 0, 1), row(1, 0, 1)
    zy, xy = ahead_y(*z), ahead_y(*x)
    return (
        [zy[s] - (y_deep[s] - y[s]) for s in range(2)],
        [(x_deep[s] - x[s]) - (z_next[s] - z[s]) for s in range(2)],
        [(y_next[s] - y[s]) - xy[s] for s in range(2)],
    )


def curl_behind(ref, r):
    def row(part, step=0, shift=0):
        return [ref[part, r + step, s, depths(ref, shift), :] for s in range(2)]

    x, y, z = row(0), row(1), row(2)
    y_prev, z_prev = row(1, -1), row(2, -1)
    x_deep, y_deep = row(0, 0, -1), row(1, 0, -1)
    zy, xy = behind_y(*z), behind_y(*x)
    return (
        [zy[s] - (y[s] - y_deep[s]) for s in range(2)],
        [(x[s] - x_deep[s]) - (z[s] - z_prev[s]) for s in range(2)],
        [(y[s] - y_prev[s]) - xy[s] for s in range(2)],
    )


def clear_pads(ref):
    for part in range(ref.shape[0]):
        for start in (0, ref.shape[3] - PAD):
            shape = ref.shape[1:3] + (PAD,) + ref.shape[4:]
            ref[part, :, :, start : start + PAD, :] = jnp.zeros(shape, F32)


def sweep(low, high, *steps):
    def group(start, rows):
        stores = []
        for k in range(rows):
            for step in steps:
                stores += step(start + k)
        for ref, index, value in stores:
            ref[index] = value

    whole = (high - low) // GROUP
    if whole:

        def body(k, carry):
            group(low + GROUP * k, GROUP)
            return carry

        lax.fori_loop(0, whole, body, 0)
    if (high - low) % GROUP:
        group(low + GROUP * whole, (high - low) % GROUP)


def copies(pairs, semaphores):
    started = []
    for k, (source, target) in enumerate(pairs):
        started.append(pltpu.make_async_copy(source, target, semaphores.at[k]))
        started[-1].start()
    return started


def ghost_mask(tile_cols, column, count_cols):
    lane = lax.broadcasted_iota(jnp.int32, (1, tile_cols), 1)
    upper = jnp.where(column < count_cols - 1, GHOST, 0)
    lower = tile_cols - jnp.where(column > 0, GHOST, 0)
    return jnp.where((lane < upper) | (lane >= lower), 1.0, 0.0)


def row_mask(row, ghost, tile_rows, place, count_rows):
    low = jnp.where(place > 0, 1.0, 0.0)
    high = jnp.where(place < count_rows - 1, 1.0, 0.0)
    return jnp.where(row < ghost, low, jnp.where(row >= ghost + tile_rows, high, 1.0))


def pack_rows_kernel(e, h, material, rows_a, rows_b, fields, cells, edges, semaphores):
    tile_rows = material.shape[0]
    even = lax.axis_index("gx") % 2 == 0
    last = tile_rows - GHOST
    starts = (jnp.where(even, last, 0), jnp.where(even, 0, last))
    loads = copies([(e, fields.at[0:3]), (h, fields.at[3:6]), (material, cells)], semaphores)
    for load in loads:
        load.wait()
    pairs = [(fields.at[:, pl.ds(starts[1], GHOST)], rows_b.at[0:6])]
    pairs.append((fields.at[:, pl.ds(starts[0], GHOST)], rows_a.at[0:6]))
    sends = copies(pairs, semaphores)
    for k, out in enumerate((rows_a, rows_b)):
        edges[k] = cells[pl.ds(starts[k], GHOST)].astype(F32)
    sends += copies([(edges.at[0], rows_a.at[6]), (edges.at[1], rows_b.at[6])], semaphores.at[2:4])
    for send in sends:
        send.wait()


def pack_columns_kernel(e, h, material, cols_a, cols_b):
    tile_rows, depth, tile_cols = material.shape
    even = lax.axis_index("gy") % 2 == 0
    lane = lax.broadcasted_iota(jnp.int32, (depth, tile_cols), 1)
    used = GHOST * tile_rows
    for pair in range(4):
        first = last = jnp.zeros((depth, tile_cols), F32)
        for part in range(2 * pair, min(2 * pair + 2, 7)):
            for x in range(tile_rows):
                if part < 3:
                    plane = e[part, x]
                elif part < 6:
                    plane = h[part - 3, x]
                else:
                    plane = material[x].astype(F32)
                shift = used * (part % 2) + GHOST * x
                spot = (lane >= shift) & (lane < shift + GHOST)
                first = jnp.where(spot, pltpu.roll(plane, shift, 1) if shift else plane, first)
                shift = (shift + GHOST) % tile_cols
                last = jnp.where(spot, pltpu.roll(plane, shift, 1) if shift else plane, last)
        cols_a[pair] = jnp.where(even, last, first)
        cols_b[pair] = jnp.where(even, first, last)


def forward_kernel(
    counts, eps, weights, twist, e, h, material, row_a, row_b, own_a, own_b, corner_a, corner_b, table,
    kept_out, inverse_out, mid, electric, magnetic, inverse, kept, index, cols, phases, stash, lens, semaphores,
):
    tile_rows, depth, tile_cols = material.shape
    count_rows, count_cols = counts
    i, j = lax.axis_index("gx"), lax.axis_index("gy")
    even_x = i % 2 == 0
    even_y = j % 2 == 0
    far_edge = GHOST + tile_rows
    ext = tile_rows + 2 * GHOST
    spots = [
        pl.ds(jnp.where(even_x, far_edge, 0), GHOST),
        pl.ds(jnp.where(even_x, 0, far_edge), GHOST),
    ]
    own = pl.ds(GHOST, tile_rows)
    inner = pl.ds(PAD, depth)
    pairs = [(material, index)]
    pairs += [(own_a, cols.at[0, 0]), (own_b, cols.at[0, 1]), (corner_a, cols.at[1]), (corner_b, cols.at[2])]
    for part, spot in ((row_a, spots[0]), (row_b, spots[1])):
        pairs.append((part.at[6], inverse.at[spot, 0]))
        pairs.append((part.at[0:3], electric.at[:, spot, 0, inner, :]))
        pairs.append((part.at[3:6], magnetic.at[:, spot, 0, inner, :]))
    pairs.append((e, electric.at[:, own, 0, inner, :]))
    pairs.append((h, magnetic.at[:, own, 0, inner, :]))
    early = len(pairs)
    pairs += column_blocks(table, phases, tile_cols)
    started = copies(pairs, semaphores)
    clear_pads(electric)
    clear_pads(magnetic)
    for copy in started[:early]:
        copy.wait()

    lane = lax.broadcasted_iota(jnp.int32, (depth, tile_cols), 1)
    right_at = jnp.where(even_y, 0, 1)
    left_at = jnp.where(even_y, 1, 0)
    used = GHOST * tile_rows

    def turn(value, shift):
        shift = shift % tile_cols
        return pltpu.roll(value, shift, 1) if shift else value

    inverse[GHOST:far_edge, 0] = index[...].astype(F32)
    for part in range(7):
        for base, block, skip, rows in (
            (GHOST, 0, 0, tile_rows),
            (0, jnp.where(even_x, 2, 1), tile_rows - GHOST, GHOST),
            (far_edge, jnp.where(even_x, 1, 2), 0, GHOST),
        ):
            right = cols[block, right_at, part // 2]
            left = cols[block, left_at, part // 2]
            for x in range(rows):
                shift = used * (part % 2) + GHOST * (skip + x)
                value = jnp.where(lane >= tile_cols - GHOST, turn(left, -GHOST - shift), 0.0)
                value = jnp.where(lane < GHOST, turn(right, -shift), value)
                if part < 6:
                    (electric, magnetic)[part // 3][part % 3, base + x, 1, inner, :] = value
                else:
                    inverse[base + x, 1] = value

    mask = ghost_mask(tile_cols, j, count_cols)

    def masked(row):
        scale = 0.5 * row_mask(row, GHOST, tile_rows, i, count_rows)
        return (scale, scale * mask)

    def invert(row, carry):
        scale = masked(row)
        for s in range(2):
            value = inverse[row, s]
            permittivity = jnp.full(value.shape, eps[0], F32)
            for m in range(1, NMAT):
                permittivity = jnp.where(value == float(m), eps[m], permittivity)
            inverse[row, s] = scale[s] / permittivity
        return carry

    lax.fori_loop(0, ext, invert, 0)
    sends = copies([(inverse, inverse_out)], semaphores)

    for n in range(ITERS):

        def magnetic_row(r):
            curl = curl_ahead(electric, r)
            scale = masked(r)
            stores = []
            for part in range(3):
                for s in range(2):
                    spot = (part, r, s, inner)
                    stores.append((magnetic, spot, magnetic[spot] - scale[s] * curl[part][s]))
            return stores

        def electric_row(r, x=None, q=None, side=0):
            curl = curl_behind(magnetic, r)
            stores = []
            for part in range(3):
                for s in range(2):
                    spot = (part, r, s, inner)
                    value = electric[spot] + inverse[r, s] * curl[part][s]
                    stores.append((electric, spot, value))
                    if s == 0 and x is not None:
                        stores.append((kept, (n, part, x), curl[part][0]))
                        if part < 2:
                            lanes = slice(side * tile_cols, (side + 1) * tile_cols)
                            for k, half in enumerate(split(value)):
                                start = (2 * n + k) * depth
                                stores.append((stash, (part, q, slice(start, start + depth), lanes), half))
            return stores

        def own_rows(k, carry):
            stores = []
            for step in range(OWN_GROUP):
                q, side = OWN_GROUP // 2 * k + step // 2, step % 2
                x = 2 * q + side
                stores += electric_row(GHOST + x, x, q, side)
            for ref, index, value in stores:
                ref[index] = value
            return carry

        sweep(n, ext - 1 - n, magnetic_row)
        sweep(n + 1, GHOST, electric_row)
        lax.fori_loop(0, tile_rows // OWN_GROUP, own_rows, 0)
        sweep(far_edge, ext - 1 - n, electric_row)
        sends += copies([(kept.at[n], kept_out.at[n])], semaphores.at[n + 1 : n + 2])

    waves = 2 * NF
    for p in range(2):
        for q in range(tile_rows // 2):
            value = dot(weights[...], stash[p, q])
            value = value[:waves] + value[waves:]
            for s in range(2):
                base = (p * tile_rows + 2 * q + s) * waves
                lens[base : base + waves, :] = value[:, s * tile_cols : (s + 1) * tile_cols]
    for copy in started[early:]:
        copy.wait()
    planes = 2 * tile_rows
    for f in range(NF):
        real = lens[pl.ds(f, planes, stride=waves), :]
        imag = lens[pl.ds(NF + f, planes, stride=waves), :]
        high, low = split(jnp.concatenate([real, imag], axis=1))
        value = lax.dot_general(
            jnp.concatenate([high, low], axis=0), phases[f], (((1,), (1,)), ((), ())), preferred_element_type=F32
        )
        value = value[:planes] + value[planes:]
        value = value[:, : 2 * FAR] + value[:, 2 * FAR :]
        mid[f] = value * twist[0, j, f : f + 1, :] + half_turn(value) * twist[1, j, f : f + 1, :]
    for copy in sends:
        copy.wait()


def backward_kernel(
    counts, own, sibling, target, twist, weights, kept_in, inverse_in, rows_far, rows_back_in, table_in,
    gradient, squares, mid, far, intensity, back, source, electric, magnetic, scaled, accum,
    kept, inverse, rows_back, table, semaphores,
):
    tile_rows, depth, tile_cols = gradient.shape
    width = 2 * tile_cols
    count_rows, count_cols = counts
    i, j = lax.axis_index("gx"), lax.axis_index("gy")
    samples = NF * FAR * FAR
    wide = 2 * FAR
    pairs = []
    for k in range(count_rows // 2):
        near = i ^ (2 * k)
        for block, index in ((own, near), (sibling, near ^ 1)):
            spot = pl.ds(pl.multiple_of(index * tile_rows, 8), tile_rows)
            for p in range(2):
                pairs.append(
                    (block.at[k, :, p * tile_rows : (p + 1) * tile_rows], mid.at[:, spot, p * wide : (p + 1) * wide])
                )
    first = len(pairs)
    pairs += [(rows_back_in, rows_back)] + column_blocks(table_in, table, width)
    second = len(pairs)
    pairs += [(inverse_in, inverse), (kept_in, kept)]
    started = copies(pairs, semaphores)
    clear_pads(scaled)
    clear_pads(magnetic)
    for copy in started[:first]:
        copy.wait()
    sign = jnp.where(lax.broadcasted_iota(jnp.int32, (1, wide), 1) < FAR, 1.0, -1.0)
    total = jnp.zeros((FAR, wide), F32)
    for f in range(NF):
        high, low = split(mid[f])
        both = dot(rows_far[f], jnp.concatenate([high, low, high], axis=0))
        level = jnp.zeros((FAR, wide), F32)
        for p in range(2):
            cos = both[:FAR, p * wide : (p + 1) * wide]
            sin = both[FAR:, p * wide : (p + 1) * wide]
            value = cos + sign * half_turn(sin)
            far[f, :, p * wide : (p + 1) * wide] = value
            level = level + value * value
        level = level + half_turn(level)
        intensity[f] = level
        total = total + level
    def wanted(f):
        return jnp.concatenate([target[f], target[f]], axis=1)

    power = jnp.sum(total, keepdims=True) / (2.0 * samples)
    total = jnp.zeros((FAR, wide), F32)
    for f in range(NF):
        level = intensity[f]
        total = total + (level / power - wanted(f)) * level
    spread = jnp.sum(total, keepdims=True) / (2.0 * samples * power)

    for copy in started[first:second]:
        copy.wait()
    mask = ghost_mask(tile_cols, j, count_cols)
    span = rows_back.shape[2] - count_rows * tile_rows + tile_rows
    row = lax.broadcasted_iota(jnp.int32, (2 * span, 1), 0)
    row = jnp.where(row >= span, row - span, row)
    lowest = jnp.where(i > 0, 0, BACK)
    highest = jnp.where(i < count_rows - 1, span, BACK + tile_rows)
    inside = jnp.where((row >= lowest) & (row < highest), 1.0, 0.0)
    waves = 2 * NF
    for f in range(NF):
        slope = 2.0 / power * (intensity[f] / power - wanted(f) - spread)
        slope = 2.0 * slope
        high, low = split(far[f] * jnp.concatenate([slope, slope], axis=1))
        start = pl.multiple_of(i * tile_rows, 8)
        phases = jnp.concatenate(
            [rows_back[f, 0, pl.ds(start, span), :], rows_back[f, 1, pl.ds(start, span), :]], axis=0
        )
        phase_high, phase_low = split(phases)
        both = dot(phase_high, high) + dot(phase_high, low) + dot(phase_low, high)
        turned = []
        for p in range(2):
            cos = both[:span, p * wide : (p + 1) * wide]
            sin = both[span:, p * wide : (p + 1) * wide]
            value = cos - sign * half_turn(sin)
            turned.append(value * twist[0, j, f : f + 1, :] - half_turn(value) * twist[1, j, f : f + 1, :])
        high, low = split(jnp.concatenate(turned, axis=0))
        left = jnp.concatenate(
            [jnp.concatenate([high, high], axis=1), jnp.concatenate([low, low], axis=1)], axis=0
        )
        both = dot(left, table[f])
        both = (both[: 2 * span] + both[2 * span :]) * inside
        for part in range(2):
            for s in range(2):
                start = part * width + s * tile_cols
                value = both[:, start : start + tile_cols]
                value = value * mask if s else value
                for p in range(2):
                    back[2 * p + s, pl.ds(part * NF + f, span, stride=waves), :] = value[p * span : (p + 1) * span]

    ext = tile_rows + 2 * BACK

    def source_row(r):
        spot = pl.ds(pl.multiple_of(r * waves, 8), waves)
        stores = []
        for p in range(2):
            high, low = split(jnp.concatenate([back[2 * p, spot, :], back[2 * p + 1, spot, :]], axis=1))
            both = dot(weights[...], jnp.concatenate([high, low, high], axis=0))
            for n in range(ITERS):
                for s in range(2):
                    value = both[n * depth : (n + 1) * depth, s * tile_cols : (s + 1) * tile_cols]
                    stores.append((source, (n, p, r, s), value))
        return stores

    sweep(0, ext, source_row)
    for copy in started[second:]:
        copy.wait()
    inner = pl.ds(PAD, depth)

    def masked(r):
        scale = 0.5 * row_mask(r, BACK, tile_rows, i, count_rows)
        return (scale, scale * mask)

    def take(n, r, value, own):
        stores = []
        total = accum[r - BACK] if own and n < ITERS - 1 else None
        for part in range(3):
            for s in range(2):
                now = value[part][s]
                if part < 2:
                    extra = source[n, part, r, s]
                    now = extra if now is None else now + extra
                elif now is None:
                    now = jnp.zeros((depth, tile_cols), F32)
                if n > 0:
                    stores.append((electric, (part, r, s), now))
                    stores.append((scaled, (part, r, s, inner), inverse[r + GHOST - BACK, s] * now))
                if own and s == 0:
                    term = now * kept[n, part, r - BACK]
                    total = term if total is None else total + term
        if own:
            stores.append((accum, r - BACK, total))
        return stores

    def first_row(own):
        return lambda r: take(ITERS - 1, r, [[None, None]] * 3, own)

    sweep(0, BACK, first_row(False))
    sweep(BACK, BACK + tile_rows, first_row(True))
    sweep(BACK + tile_rows, ext, first_row(False))
    for n in range(ITERS - 1, 0, -1):

        def magnetic_row(r):
            curl = curl_ahead(scaled, r)
            scale = masked(r)
            stores = []
            for part in range(3):
                for s in range(2):
                    spot = (part, r, s, inner)
                    value = scale[s] * curl[part][s]
                    stores.append((magnetic, spot, value if n == ITERS - 1 else value + magnetic[spot]))
            return stores

        def electric_row(own):
            def step(r):
                curl = curl_behind(magnetic, r)
                value = [[electric[part, r, s] - curl[part][s] for s in range(2)] for part in range(3)]
                return take(n - 1, r, value, own)

            return step

        low, high = BACK - n, BACK + tile_rows + n - 1
        sweep(low, high, magnetic_row)
        sweep(low + 1, BACK, electric_row(False))
        sweep(BACK, BACK + tile_rows, electric_row(True))
        sweep(BACK + tile_rows, high, electric_row(False))

    total = jnp.zeros((depth, tile_cols), F32)
    for x in range(tile_rows):
        value = inverse[GHOST + x, 0]
        value = -2.0 * (value * value) * accum[x]
        gradient[x] = value
        total = total + value * value
    squares[...] = jnp.broadcast_to(jnp.sum(total, keepdims=True), squares.shape)


def scale_kernel(cells, squares, gradient, result):
    total = jnp.sum(squares[...], keepdims=True) / squares.shape[1]
    scale = 1.0 / jnp.sqrt(total / cells + 1e-06)
    for x in range(gradient.shape[0]):
        result[x] = gradient[x] * scale


SMEM = pl.BlockSpec(memory_space=pltpu.SMEM)
VMEM = pl.BlockSpec(memory_space=pltpu.VMEM)
HBM = pl.BlockSpec(memory_space=pltpu.HBM)
DMA = pltpu.SemaphoreType.DMA


def call(kernel, name, specs, outs, scratch=(), out_specs=VMEM):
    return pl.pallas_call(
        kernel,
        name=name,
        in_specs=specs,
        out_specs=out_specs,
        out_shape=outs,
        scratch_shapes=scratch,
        compiler_params=pltpu.CompilerParams(vmem_limit_bytes=VMEM_BYTES),
    )


def array(*shape):
    return jax.ShapeDtypeStruct(shape, F32)


def buffer(*shape):
    return pltpu.VMEM(shape, F32)


def even_swaps(count):
    return [(k, k ^ 1) for k in range(count)]


def odd_swaps(count):
    return [(k, k + 1 if k % 2 else k - 1) for k in range(1, count - 1)]


def body(count_rows, count_cols, e_init, h_init, material, eps_table, target):
    tile_rows, depth, tile_cols = material.shape
    counts = (count_rows, count_cols)
    edge = array(7, GHOST, depth, tile_cols)
    side = array(4, depth, tile_cols)
    row_a, row_b = call(
        pack_rows_kernel,
        "pack_rows",
        [HBM] * 3,
        (edge, edge),
        [
            buffer(6, tile_rows, depth, tile_cols),
            pltpu.VMEM((tile_rows, depth, tile_cols), jnp.int32),
            buffer(2, GHOST, depth, tile_cols),
            DMA((4,)),
        ],
        (HBM, HBM),
    )(e_init, h_init, material)
    rows_a, rows_b = even_swaps(count_rows), odd_swaps(count_rows)
    cols_a, cols_b = even_swaps(count_cols), odd_swaps(count_cols)
    row_b = lax.ppermute(row_b, "gx", rows_b)
    row_a = lax.ppermute(row_a, "gx", rows_a)
    col_a, col_b = call(pack_columns_kernel, "pack_columns", [VMEM] * 3, (side, side), (), (VMEM, VMEM))(
        e_init, h_init, material
    )
    col_b = lax.ppermute(col_b, "gy", cols_b)
    col_a = lax.ppermute(col_a, "gy", cols_a)
    corner = jnp.stack([col_a, col_b])
    corner_b = lax.ppermute(corner, "gx", rows_b)
    corner_a = lax.ppermute(corner, "gx", rows_a)

    table = jnp.asarray(column_table(tile_cols, 2 * tile_cols))
    twist = jnp.asarray(column_twist(count_cols))
    ext = tile_rows + 2 * GHOST
    waves = 2 * NF
    kept = (ITERS, 3, tile_rows, depth, tile_cols)
    inverse = (ext, 2, depth, tile_cols)
    kept_out, inverse_out, mid = call(
        functools.partial(forward_kernel, counts),
        "forward",
        [SMEM, VMEM, VMEM] + [HBM] * 10,
        (array(*kept), array(*inverse), array(NF, 2 * tile_rows, 2 * FAR)),
        [
            buffer(3, ext, 2, depth + 2 * PAD, tile_cols),
            buffer(3, ext, 2, depth + 2 * PAD, tile_cols),
            buffer(*inverse),
            buffer(*kept),
            pltpu.VMEM((tile_rows, depth, tile_cols), jnp.int32),
            buffer(3, 2, 4, depth, tile_cols),
            pltpu.VMEM((NF, 4 * FAR, 2 * tile_cols), BF16),
            pltpu.VMEM((2, tile_rows // 2, 2 * ITERS * depth, 2 * tile_cols), BF16),
            buffer(2 * tile_rows * waves, tile_cols),
            DMA((21,)),
        ],
        (HBM, HBM, VMEM),
    )(
        eps_table, jnp.asarray(lens_table(depth)), twist, e_init, h_init, material, row_a, row_b, col_a, col_b,
        corner_a, corner_b, table,
    )

    whole = mid
    for k in range(1, count_cols):
        whole = whole + lax.ppermute(mid, "gy", [(n, n ^ k) for n in range(count_cols)])
    own = jnp.stack(
        [whole]
        + [lax.ppermute(whole, "gx", [(n, n ^ k) for n in range(count_rows)]) for k in range(2, count_rows, 2)]
    )
    sibling = lax.ppermute(own, "gx", rows_a)

    rows = count_rows * tile_rows
    ext = tile_rows + 2 * BACK
    span = tile_rows + 16
    devices = count_rows * count_cols
    grid = (3, ext, 2, depth + 2 * PAD, tile_cols)
    back_rows = row_back_table(rows)
    gradient, squares = call(
        functools.partial(backward_kernel, counts),
        "backward",
        [HBM] * 2 + [VMEM] * 3 + [HBM] * 2 + [VMEM] + [HBM] * 2,
        (array(tile_rows, depth, tile_cols), array(devices, 128)),
        [
            buffer(NF, rows, 4 * FAR),
            buffer(NF, FAR, 4 * FAR),
            buffer(NF, FAR, 2 * FAR),
            buffer(4, span * waves, tile_cols),
            buffer(ITERS, 2, ext, 2, depth, tile_cols),
            buffer(3, ext, 2, depth, tile_cols),
            buffer(*grid),
            buffer(*grid),
            buffer(tile_rows, depth, tile_cols),
            buffer(*kept),
            buffer(*inverse),
            buffer(*back_rows.shape),
            pltpu.VMEM((NF, 4 * FAR, 4 * tile_cols), BF16),
            DMA((2 * count_rows + 11,)),
        ],
        (VMEM, VMEM),
    )(
        own, sibling, target, twist, jnp.asarray(source_table(depth)),
        kept_out, inverse_out, jnp.asarray(row_table(rows)), jnp.asarray(back_rows), table,
    )
    squares = lax.all_to_all(squares, ("gx", "gy"), 0, 0, tiled=True)
    cells = rows * depth * tile_cols * count_cols
    return call(
        functools.partial(scale_kernel, cells), "scale", [VMEM, VMEM], array(tile_rows, depth, tile_cols)
    )(squares, gradient)


def solution(mesh):
    in_specs = (P(None, "gx", None, "gy"), P(None, "gx", None, "gy"), P("gx", None, "gy"), P(), P())
    out_specs = P("gx", None, "gy")
    part = functools.partial(body, mesh.shape["gx"], mesh.shape["gy"])
    return jax.shard_map(part, mesh=mesh, in_specs=in_specs, out_specs=out_specs, check_vma=False)
```

time: 103 us -> 79.3 us (0.77)
  Pallas kernels: 47.3 us -> 28.4 us
  other arithmetic: 2.45 us -> 0.89 us
  starting transfers between devices: 24.3 us -> 23 us
    pallas_call x3 -> x4, Pallas kernels: 45.5 us -> 26.7 us  [the longest x1 11.8 us: body(): call(functools.partial(backward_kernel, counts), 'backward', [HBM] * 2 +...]
    ppermute x3, starting transfers between devices: 11.1 us -> 4.8 us  [body(): lax.ppermute(whole, 'gx', [(n, n ^ k) for n in range(count_rows)])]
    ppermute x3, starting transfers between devices: 3.49 us -> 8.26 us  [body(): lax.ppermute(mid, 'gy', [(n, n ^ k) for n in range(count_cols)])]
    unnamed x18 -> x8, local copies, waits for them, and re-layouts: 2.49 us -> 2.05 us
  transfers between devices with their start and end apart: 13 -> 13, of which waited for: 9 -> 7; matrix products, arithmetic and copies ran while one was open for 1% -> 0% of each run, Pallas kernels for 0% -> 3%
where the time goes in v1:
time: 79.3 us; the launch traced here: 78.9 us
  Pallas kernels  28.4 us (36%)
  starting transfers between devices  23 us (29%)
  waiting for transfers between devices  13.5 us (17%)
  blocking collectives  11 us (14%)
  local copies, waits for them, and re-layouts  2.05 us (3%)
  other arithmetic  0.89 us (1%)
    pallas_call x1, Pallas kernels, body(): call(functools.partial(backward_kernel, counts), 'backward', [HBM] * 2 +...  11.8 us
    all_to_all x1, blocking collectives, body(): squares = lax.all_to_all(squares, ('gx', 'gy'), 0, 0, tiled=True)  11 us
    pallas_call x1, Pallas kernels, body(): call(functools.partial(forward_kernel, counts), 'forward', [SMEM, VMEM, V...  10.3 us
    ppermute x3, starting transfers between devices, body(): lax.ppermute(mid, 'gy', [(n, n ^ k) for n in range(count_cols)])  8.26 us
    ppermute x3, waiting for transfers between devices, body(): lax.ppermute(whole, 'gx', [(n, n ^ k) for n in range(count_rows)])  5.03 us
    ppermute x3, starting transfers between devices, body(): lax.ppermute(whole, 'gx', [(n, n ^ k) for n in range(count_rows)])  4.8 us
    ppermute x3, waiting for transfers between devices, body(): lax.ppermute(mid, 'gy', [(n, n ^ k) for n in range(count_cols)])  4.01 us
    ppermute x1, starting transfers between devices, body(): corner_a = lax.ppermute(corner, 'gx', rows_a)  3.44 us
  transfers between devices with their start and end apart: 13, of which 7 were waited for; matrix products, arithmetic and copies ran while one was open for 0% of the time, Pallas kernels for 3%

profile of v1, /device:TPU:0, one launch (start us, length us, event | category | flops | bytes accessed | tf_op | source)
XLA Modules:
  0.0 78.9 jit_solution(5790526032486356207)
XLA Ops:
  0.0 2.3 %pack_rows.1 = (f32[7,6,32,128]{3,2,1,0:T(8,128)}, f32[7,6,32,128]{3,2,1,0:T(8,128)}) custom-call(f32[3,8,32,128]{3,2,1,0:T(8,128)} %e.5, f32[3,8,32,128]{3,2,1,0:T(8,128)} %h.5, s32[8,32,128]{2,1,0:T(8,128)} %material.5), custom_call_target="tpu_custom_call" | custom-call | tf_op jit(solution)/shard_map/pack_rows/pallas_call | solution.py:634
  2.3 0.5 collective-permute-start
  2.8 1.5 %collective-permute-start.1 = (f32[7,6,32,128]{3,2,1,0:T(8,128)}, f32[7,6,32,128]{3,2,1,0:T(8,128)}, u32[]{:S(2)}, u32[]{:S(2)}) collective-permute-start(f32[7,6,32,128]{3,2,1,0:T(8,128)} %get-tuple-element.15), channel_id=1, source_target_pairs={{4,8},{8,4},{12,16},{16,12},{20,24},{24,20},{5,9},{9,5},{13,17},{1... | collective-permute-start | bytes 2064392 | tf_op jit(solution)/shard_map/ppermute | solution.py:649
  4.3 2.3 %pack_columns.1 = (f32[4,32,128]{2,1,0:T(8,128)}, f32[4,32,128]{2,1,0:T(8,128)}) custom-call(f32[3,8,32,128]{3,2,1,0:T(8,128)} %e.5, f32[3,8,32,128]{3,2,1,0:T(8,128)} %h.5, s32[8,32,128]{2,1,0:T(8,128)} %material.5), custom_call_target="tpu_custom_call" | custom-call | tf_op jit(solution)/shard_map/pack_columns/pallas_call | solution.py:651
  6.6 2.5 %collective-permute-start.2 = (f32[4,32,128]{2,1,0:T(8,128)}, f32[4,32,128]{2,1,0:T(8,128)S(1)}, u32[]{:S(2)}, u32[]{:S(2)}) collective-permute-start(f32[4,32,128]{2,1,0:T(8,128)} %get-tuple-element.16), channel_id=1, source_target_pairs={{0,1},{1,0},{2,3},{3,2},{4,5},{5,4},{6,7},{7,6},{8,9},{9,8},{10,11... | collective-permute-start | bytes 196616 | tf_op jit(solution)/shard_map/ppermute | solution.py:655
  9.1 0.7 collective-permute-start.3
  9.8 1.8 %collective-permute-done.2.own_a = f32[4,32,128]{2,1,0:T(8,128)S(1)} collective-permute-done((f32[4,32,128]{2,1,0:T(8,128)}, f32[4,32,128]{2,1,0:T(8,128)S(1)}, u32[]{:S(2)}, u32[]{:S(2)}) %collective-permute-start.2) | collective-permute-done | bytes 65568 | tf_op jit(solution)/shard_map/ppermute | solution.py:655
  11.6 0.0 copy-start.1
  11.6 0.0 collective-permute-done.3.own_b
  11.6 0.0 copy-start.2
  11.6 0.6 copy-done.1
  12.2 0.0 copy-done.2
  12.2 1.3 %collective-permute-start.5 = (f32[2,4,32,128]{3,2,1,0:T(8,128)S(1)}, f32[2,4,32,128]{3,2,1,0:T(8,128)}, u32[]{:S(2)}, u32[]{:S(2)}) collective-permute-start(f32[2,4,32,128]{3,2,1,0:T(8,128)S(1)} %pad_maximum_fusion.1), channel_id=1, source_target_pairs={{4,8},{8,4},{12,16},{16,12},{20,24},{24,20},{5,9},{9,5},{13,17},{1... | collective-permute-start | bytes 393224 | tf_op jit(solution)/shard_map/ppermute | solution.py:657
  13.6 3.4 %collective-permute-start.4 = (f32[2,4,32,128]{3,2,1,0:T(8,128)S(1)}, f32[2,4,32,128]{3,2,1,0:T(8,128)}, u32[]{:S(2)}, u32[]{:S(2)}) collective-permute-start(f32[2,4,32,128]{3,2,1,0:T(8,128)S(1)} %pad_maximum_fusion.1), channel_id=1, source_target_pairs={{0,4},{4,0},{8,12},{12,8},{16,20},{20,16},{24,28},{28,24},{1,5},{5... | collective-permute-start | bytes 393224 | tf_op jit(solution)/shard_map/ppermute | solution.py:658
  17.0 0.0 collective-permute-done.5.corner_b
  17.0 1.1 %collective-permute-done.4.corner_a = f32[2,4,32,128]{3,2,1,0:T(8,128)} collective-permute-done((f32[2,4,32,128]{3,2,1,0:T(8,128)S(1)}, f32[2,4,32,128]{3,2,1,0:T(8,128)}, u32[]{:S(2)}, u32[]{:S(2)}) %collective-permute-start.4) | collective-permute-done | bytes 131104 | tf_op jit(solution)/shard_map/ppermute | solution.py:658
  18.1 0.0 collective-permute-done.row_a
  18.1 0.0 collective-permute-done.1.row_b
  18.1 10.3 %forward.1 = (f32[6,3,8,32,128]{4,3,2,1,0:T(8,128)}, f32[20,2,32,128]{3,2,1,0:T(8,128)}, f32[8,16,128]{2,1,0:T(8,128)}) custom-call(f32[8]{0:T(128)} %eps.1, bf16[32,384]{1,0:T(8,128)(2,1)} %constant.14.clone.weights, f32[2,4,8,128]{3,2,1,0:T(8,128)} %constant.13.clone.twist, f32[3,8,32,128]{3,2,1,0:T(8,128)} %e.5, f32[3,8,32,128]{3,2,1,0:T(8,128)} %h.5, ...), custom_call_target="tpu_custom_call" | custom-call | tf_op jit(solution)/shard_map/forward/pallas_call | solution.py:666
  28.5 3.4 %collective-permute-start.8 = (f32[8,16,128]{2,1,0:T(8,128)}, f32[8,16,128]{2,1,0:T(8,128)S(1)}, u32[]{:S(2)}, u32[]{:S(2)}) collective-permute-start(f32[8,16,128]{2,1,0:T(8,128)} %get-tuple-element.18), channel_id=1, source_target_pairs={{0,3},{1,2},{2,1},{3,0},{4,7},{5,6},{6,5},{7,4},{8,11},{9,10},{10,... | collective-permute-start | bytes 196616 | tf_op jit(solution)/shard_map/ppermute | solution.py:691
  31.9 3.5 %collective-permute-start.7 = (f32[8,16,128]{2,1,0:T(8,128)}, f32[8,16,128]{2,1,0:T(8,128)S(1)}, u32[]{:S(2)}, u32[]{:S(2)}) collective-permute-start(f32[8,16,128]{2,1,0:T(8,128)} %get-tuple-element.18), channel_id=1, source_target_pairs={{0,2},{1,3},{2,0},{3,1},{4,6},{5,7},{6,4},{7,5},{8,10},{9,11},{10,... | collective-permute-start | bytes 196616 | tf_op jit(solution)/shard_map/ppermute | solution.py:691
  35.4 1.4 %collective-permute-start.6 = (f32[8,16,128]{2,1,0:T(8,128)}, f32[8,16,128]{2,1,0:T(8,128)S(1)}, u32[]{:S(2)}, u32[]{:S(2)}) collective-permute-start(f32[8,16,128]{2,1,0:T(8,128)} %get-tuple-element.18), channel_id=1, source_target_pairs={{0,1},{1,0},{2,3},{3,2},{4,5},{5,4},{6,7},{7,6},{8,9},{9,8},{10,11... | collective-permute-start | bytes 196616 | tf_op jit(solution)/shard_map/ppermute | solution.py:691
  36.7 0.0 collective-permute-done.8
  36.7 1.1 %collective-permute-done.7 = f32[8,16,128]{2,1,0:T(8,128)S(1)} collective-permute-done((f32[8,16,128]{2,1,0:T(8,128)}, f32[8,16,128]{2,1,0:T(8,128)S(1)}, u32[]{:S(2)}, u32[]{:S(2)}) %collective-permute-start.7) | collective-permute-done | bytes 65568 | tf_op jit(solution)/shard_map/ppermute | solution.py:691
  37.8 2.9 %collective-permute-done.6 = f32[8,16,128]{2,1,0:T(8,128)S(1)} collective-permute-done((f32[8,16,128]{2,1,0:T(8,128)}, f32[8,16,128]{2,1,0:T(8,128)S(1)}, u32[]{:S(2)}, u32[]{:S(2)}) %collective-permute-start.6) | collective-permute-done | bytes 65568 | tf_op jit(solution)/shard_map/ppermute | solution.py:691
  40.8 0.9 %add_add_fusion = f32[8,16,128]{2,1,0:T(8,128)S(1)} fusion(f32[8,16,128]{2,1,0:T(8,128)S(1)} %collective-permute-done.8, f32[8,16,128]{2,1,0:T(8,128)S(1)} %collective-permute-done.7, f32[8,16,128]{2,1,0:T(8,128)} %get-tuple-element.18, f32[8,16,128]{2,1,0:T(8,128)S(1)} %collective-permute-done.6), kind=kLoop, calls=%fused_computation.2 | loop fusion | flops 49152 | bytes 327680 | tf_op jit(solution)/shard_map/add | solution.py:691
  41.6 4.2 %collective-permute-start.11 = (f32[8,16,128]{2,1,0:T(8,128)S(1)}, f32[8,16,128]{2,1,0:T(8,128)S(1)}, u32[]{:S(2)}, u32[]{:S(2)}) collective-permute-start(f32[8,16,128]{2,1,0:T(8,128)S(1)} %add_add_fusion), channel_id=1, source_target_pairs={{0,24},{4,28},{8,16},{12,20},{16,8},{20,12},{24,0},{28,4},{1,25},{... | collective-permute-start | bytes 196616 | tf_op jit(solution)/shard_map/ppermute | solution.py:694
  45.8 0.3 collective-permute-start.10
  46.0 0.4 collective-permute-start.9
  46.4 1.9 %collective-permute-done.11 = f32[8,16,128]{2,1,0:T(8,128)S(1)} collective-permute-done((f32[8,16,128]{2,1,0:T(8,128)S(1)}, f32[8,16,128]{2,1,0:T(8,128)S(1)}, u32[]{:S(2)}, u32[]{:S(2)}) %collective-permute-start.11) | collective-permute-done | bytes 65568 | tf_op jit(solution)/shard_map/ppermute | solution.py:694
  48.3 3.1 %collective-permute-done.10 = f32[8,16,128]{2,1,0:T(8,128)S(1)} collective-permute-done((f32[8,16,128]{2,1,0:T(8,128)S(1)}, f32[8,16,128]{2,1,0:T(8,128)S(1)}, u32[]{:S(2)}, u32[]{:S(2)}) %collective-permute-start.10) | collective-permute-done | bytes 65568 | tf_op jit(solution)/shard_map/ppermute | solution.py:694
  51.4 0.0 collective-permute-done.9
  51.5 0.0 copy-start
  51.5 0.7 copy-done
  52.2 0.0 collective-permute-start.12
  52.2 1.5 %collective-permute-done.12.sibling = f32[4,8,16,128]{3,2,1,0:T(8,128)S(1)} collective-permute-done((f32[4,8,16,128]{3,2,1,0:T(8,128)S(1)}, f32[4,8,16,128]{3,2,1,0:T(8,128)S(1)}, u32[]{:S(2)}, u32[]{:S(2)}) %collective-permute-start.12) | collective-permute-done | bytes 262176 | tf_op jit(solution)/shard_map/ppermute | solution.py:696
  53.7 0.0 copy-start.3
  53.7 0.7 copy-done.3
  54.4 11.8 %backward.1 = (f32[8,32,128]{2,1,0:T(8,128)}, f32[32,128]{1,0:T(8,128)}) custom-call(f32[4,8,16,128]{3,2,1,0:T(8,128)} %copy-done, f32[4,8,16,128]{3,2,1,0:T(8,128)} %copy-done.3, f32[8,64,64]{2,1,0:T(8,128)} %target.1, f32[2,4,8,128]{3,2,1,0:T(8,128)} %constant.13.clone.twist, bf16[192,48]{1,0:T(8,128)(2,1)} %constant.15.clone.weights, ...), custom_call_target="tpu_custom_call" | custom-call | tf_op jit(solution)/shard_map/backward/pallas_call | solution.py:704
  66.2 11.0 %all_to_all.11 = f32[32,1,128]{2,1,0:T(1,128)} all-to-all(f32[32,1,128]{2,1,0:T(1,128)} %bitcast.17), channel_id=1, replica_groups=mesh['gx'=8,'gy'=4] {'gx','gy'}, dimensions={0} | all-to-all | bytes 32768 | tf_op jit(solution)/shard_map/all_to_all | solution.py:730
  77.2 1.7 %scale.1 = f32[8,32,128]{2,1,0:T(8,128)} custom-call(f32[32,128]{1,0:T(8,128)} %bitcast.13, f32[8,32,128]{2,1,0:T(8,128)} %get-tuple-element.22.gradient), custom_call_target="tpu_custom_call" | custom-call | tf_op jit(solution)/shard_map/scale/pallas_call | solution.py:732
  (2 shorter events, 0.0 us)
Async XLA Ops:
  2.3 15.9 %collective-permute-start = (f32[7,6,32,128]{3,2,1,0:T(8,128)}, f32[7,6,32,128]{3,2,1,0:T(8,128)}, u32[]{:S(2)}, u32[]{:S(2)}) collective-permute-start(f32[7,6,32,128]{3,2,1,0:T(8,128)} %get-tuple-element.14), channel_id=1, source_target_pairs={{0,4},{4,0},{8,12},{12,8},{16,20},{20,16},{24,28},{28,24},{1,5},{5... | collective-permute-start | bytes 2064392 | tf_op jit(solution)/shard_map/ppermute | solution.py:650
  2.8 15.3 %collective-permute-start.1 = (f32[7,6,32,128]{3,2,1,0:T(8,128)}, f32[7,6,32,128]{3,2,1,0:T(8,128)}, u32[]{:S(2)}, u32[]{:S(2)}) collective-permute-start(f32[7,6,32,128]{3,2,1,0:T(8,128)} %get-tuple-element.15), channel_id=1, source_target_pairs={{4,8},{8,4},{12,16},{16,12},{20,24},{24,20},{5,9},{9,5},{13,17},{1... | collective-permute-start | bytes 2064392 | tf_op jit(solution)/shard_map/ppermute | solution.py:649
  6.6 5.0 %collective-permute-start.2 = (f32[4,32,128]{2,1,0:T(8,128)}, f32[4,32,128]{2,1,0:T(8,128)S(1)}, u32[]{:S(2)}, u32[]{:S(2)}) collective-permute-start(f32[4,32,128]{2,1,0:T(8,128)} %get-tuple-element.16), channel_id=1, source_target_pairs={{0,1},{1,0},{2,3},{3,2},{4,5},{5,4},{6,7},{7,6},{8,9},{9,8},{10,11... | collective-permute-start | bytes 196616 | tf_op jit(solution)/shard_map/ppermute | solution.py:655
  9.1 2.5 %collective-permute-start.3 = (f32[4,32,128]{2,1,0:T(8,128)}, f32[4,32,128]{2,1,0:T(8,128)S(1)}, u32[]{:S(2)}, u32[]{:S(2)}) collective-permute-start(f32[4,32,128]{2,1,0:T(8,128)} %get-tuple-element.17), channel_id=1, source_target_pairs={{1,2},{2,1},{5,6},{6,5},{9,10},{10,9},{13,14},{14,13},{17,18},{18,... | collective-permute-start | bytes 196616 | tf_op jit(solution)/shard_map/ppermute | solution.py:654
  11.6 0.6 copy-start.1
  11.6 0.6 copy-start.2
  12.2 4.8 %collective-permute-start.5 = (f32[2,4,32,128]{3,2,1,0:T(8,128)S(1)}, f32[2,4,32,128]{3,2,1,0:T(8,128)}, u32[]{:S(2)}, u32[]{:S(2)}) collective-permute-start(f32[2,4,32,128]{3,2,1,0:T(8,128)S(1)} %pad_maximum_fusion.1), channel_id=1, source_target_pairs={{4,8},{8,4},{12,16},{16,12},{20,24},{24,20},{5,9},{9,5},{13,17},{1... | collective-permute-start | bytes 393224 | tf_op jit(solution)/shard_map/ppermute | solution.py:657
  13.6 4.6 %collective-permute-start.4 = (f32[2,4,32,128]{3,2,1,0:T(8,128)S(1)}, f32[2,4,32,128]{3,2,1,0:T(8,128)}, u32[]{:S(2)}, u32[]{:S(2)}) collective-permute-start(f32[2,4,32,128]{3,2,1,0:T(8,128)S(1)} %pad_maximum_fusion.1), channel_id=1, source_target_pairs={{0,4},{4,0},{8,12},{12,8},{16,20},{20,16},{24,28},{28,24},{1,5},{5... | collective-permute-start | bytes 393224 | tf_op jit(solution)/shard_map/ppermute | solution.py:658
  28.5 8.3 %collective-permute-start.8 = (f32[8,16,128]{2,1,0:T(8,128)}, f32[8,16,128]{2,1,0:T(8,128)S(1)}, u32[]{:S(2)}, u32[]{:S(2)}) collective-permute-start(f32[8,16,128]{2,1,0:T(8,128)} %get-tuple-element.18), channel_id=1, source_target_pairs={{0,3},{1,2},{2,1},{3,0},{4,7},{5,6},{6,5},{7,4},{8,11},{9,10},{10,... | collective-permute-start | bytes 196616 | tf_op jit(solution)/shard_map/ppermute | solution.py:691
  31.9 5.9 %collective-permute-start.7 = (f32[8,16,128]{2,1,0:T(8,128)}, f32[8,16,128]{2,1,0:T(8,128)S(1)}, u32[]{:S(2)}, u32[]{:S(2)}) collective-permute-start(f32[8,16,128]{2,1,0:T(8,128)} %get-tuple-element.18), channel_id=1, source_target_pairs={{0,2},{1,3},{2,0},{3,1},{4,6},{5,7},{6,4},{7,5},{8,10},{9,11},{10,... | collective-permute-start | bytes 196616 | tf_op jit(solution)/shard_map/ppermute | solution.py:691
  35.4 5.4 %collective-permute-start.6 = (f32[8,16,128]{2,1,0:T(8,128)}, f32[8,16,128]{2,1,0:T(8,128)S(1)}, u32[]{:S(2)}, u32[]{:S(2)}) collective-permute-start(f32[8,16,128]{2,1,0:T(8,128)} %get-tuple-element.18), channel_id=1, source_target_pairs={{0,1},{1,0},{2,3},{3,2},{4,5},{5,4},{6,7},{7,6},{8,9},{9,8},{10,11... | collective-permute-start | bytes 196616 | tf_op jit(solution)/shard_map/ppermute | solution.py:691
  41.6 6.7 %collective-permute-start.11 = (f32[8,16,128]{2,1,0:T(8,128)S(1)}, f32[8,16,128]{2,1,0:T(8,128)S(1)}, u32[]{:S(2)}, u32[]{:S(2)}) collective-permute-start(f32[8,16,128]{2,1,0:T(8,128)S(1)} %add_add_fusion), channel_id=1, source_target_pairs={{0,24},{4,28},{8,16},{12,20},{16,8},{20,12},{24,0},{28,4},{1,25},{... | collective-permute-start | bytes 196616 | tf_op jit(solution)/shard_map/ppermute | solution.py:694
  45.8 5.7 %collective-permute-start.10 = (f32[8,16,128]{2,1,0:T(8,128)S(1)}, f32[8,16,128]{2,1,0:T(8,128)S(1)}, u32[]{:S(2)}, u32[]{:S(2)}) collective-permute-start(f32[8,16,128]{2,1,0:T(8,128)S(1)} %add_add_fusion), channel_id=1, source_target_pairs={{0,16},{4,20},{8,24},{12,28},{16,0},{20,4},{24,8},{28,12},{1,17},{... | collective-permute-start | bytes 196616 | tf_op jit(solution)/shard_map/ppermute | solution.py:694
  46.0 5.4 %collective-permute-start.9 = (f32[8,16,128]{2,1,0:T(8,128)S(1)}, f32[8,16,128]{2,1,0:T(8,128)S(1)}, u32[]{:S(2)}, u32[]{:S(2)}) collective-permute-start(f32[8,16,128]{2,1,0:T(8,128)S(1)} %add_add_fusion), channel_id=1, source_target_pairs={{0,8},{4,12},{8,0},{12,4},{16,24},{20,28},{24,16},{28,20},{1,9},{5... | collective-permute-start | bytes 196616 | tf_op jit(solution)/shard_map/ppermute | solution.py:694
  51.5 0.7 copy-start
  52.2 1.5 %collective-permute-start.12 = (f32[4,8,16,128]{3,2,1,0:T(8,128)S(1)}, f32[4,8,16,128]{3,2,1,0:T(8,128)S(1)}, u32[]{:S(2)}, u32[]{:S(2)}) collective-permute-start(f32[4,8,16,128]{3,2,1,0:T(8,128)S(1)} %pad_maximum_fusion.own), channel_id=1, source_target_pairs={{0,4},{4,0},{8,12},{12,8},{16,20},{20,16},{24,28},{28,24},{1,5},{5... | collective-permute-start | bytes 786440 | tf_op jit(solution)/shard_map/ppermute | solution.py:696
  53.7 0.7 copy-start.3

commit v2 on v1

--- a/solution.py
+++ b/solution.py
@@ -20,7 +20,7 @@
 F32 = jnp.float32
 BF16 = jnp.bfloat16
 PAD = 8
-VMEM_BYTES = 64 * 1024 * 1024 - 65536
+VMEM_BYTES = 40 * 1024 * 1024
 OWN_GROUP = 8
 GROUP = 8
 
@@ -257,8 +257,8 @@
 
 
 def forward_kernel(
-    counts, eps, weights, twist, e, h, material, row_a, row_b, own_a, own_b, corner_a, corner_b, table,
-    kept_out, inverse_out, mid, electric, magnetic, inverse, kept, index, cols, phases, stash, lens, semaphores,
+    counts, eps_in, weights_in, twist_in, e, h, material, row_a, row_b, own_a, own_b, corner_a, corner_b, table,
+    kept_out, inverse_out, mid, electric, magnetic, inverse, kept, index, cols, phases, stash, lens, eps, weights, twist, semaphores,
 ):
     tile_rows, depth, tile_cols = material.shape
     count_rows, count_cols = counts
@@ -281,8 +281,9 @@
         pairs.append((part.at[3:6], magnetic.at[:, spot, 0, inner, :]))
     pairs.append((e, electric.at[:, own, 0, inner, :]))
     pairs.append((h, magnetic.at[:, own, 0, inner, :]))
+    pairs.append((eps_in, eps))
     early = len(pairs)
-    pairs += column_blocks(table, phases, tile_cols)
+    pairs += [(weights_in, weights), (twist_in, twist)] + column_blocks(table, phases, tile_cols)
     started = copies(pairs, semaphores)
     clear_pads(electric)
     clear_pads(magnetic)
@@ -380,6 +381,8 @@
         sweep(far_edge, ext - 1 - n, electric_row)
         sends += copies([(kept.at[n], kept_out.at[n])], semaphores.at[n + 1 : n + 2])
 
+    for copy in started[early:]:
+        copy.wait()
     waves = 2 * NF
     for p in range(2):
         for q in range(tile_rows // 2):
@@ -388,8 +391,6 @@
             for s in range(2):
                 base = (p * tile_rows + 2 * q + s) * waves
                 lens[base : base + waves, :] = value[:, s * tile_cols : (s + 1) * tile_cols]
-    for copy in started[early:]:
-        copy.wait()
     planes = 2 * tile_rows
     for f in range(NF):
         real = lens[pl.ds(f, planes, stride=waves), :]
@@ -592,9 +593,9 @@
         result[x] = gradient[x] * scale
 
 
-SMEM = pl.BlockSpec(memory_space=pltpu.SMEM)
 VMEM = pl.BlockSpec(memory_space=pltpu.VMEM)
 HBM = pl.BlockSpec(memory_space=pltpu.HBM)
+ANY = pl.BlockSpec(memory_space=pl.ANY)
 DMA = pltpu.SemaphoreType.DMA
 
 
@@ -659,6 +660,7 @@
 
     table = jnp.asarray(column_table(tile_cols, 2 * tile_cols))
     twist = jnp.asarray(column_twist(count_cols))
+    weights = jnp.asarray(lens_table(depth))
     ext = tile_rows + 2 * GHOST
     waves = 2 * NF
     kept = (ITERS, 3, tile_rows, depth, tile_cols)
@@ -666,7 +668,7 @@
     kept_out, inverse_out, mid = call(
         functools.partial(forward_kernel, counts),
         "forward",
-        [SMEM, VMEM, VMEM] + [HBM] * 10,
+        [HBM] * 8 + [ANY] * 4 + [HBM],
         (array(*kept), array(*inverse), array(NF, 2 * tile_rows, 2 * FAR)),
         [
             buffer(3, ext, 2, depth + 2 * PAD, tile_cols),
@@ -678,11 +680,14 @@
             pltpu.VMEM((NF, 4 * FAR, 2 * tile_cols), BF16),
             pltpu.VMEM((2, tile_rows // 2, 2 * ITERS * depth, 2 * tile_cols), BF16),
             buffer(2 * tile_rows * waves, tile_cols),
-            DMA((21,)),
+            pltpu.SMEM(eps_table.shape, F32),
+            pltpu.VMEM(weights.shape, BF16),
+            buffer(*twist.shape),
+            DMA((24,)),
         ],
         (HBM, HBM, VMEM),
     )(
-        eps_table, jnp.asarray(lens_table(depth)), twist, e_init, h_init, material, row_a, row_b, col_a, col_b,
+        eps_table, weights, twist, e_init, h_init, material, row_a, row_b, col_a, col_b,
         corner_a, corner_b, table,
     )
 
@@ -704,7 +709,7 @@
     gradient, squares = call(
         functools.partial(backward_kernel, counts),
         "backward",
-        [HBM] * 2 + [VMEM] * 3 + [HBM] * 2 + [VMEM] + [HBM] * 2,
+        [ANY] * 2 + [VMEM] * 3 + [HBM] * 2 + [VMEM] + [HBM] * 2,
         (array(tile_rows, depth, tile_cols), array(devices, 128)),
         [
             buffer(NF, rows, 4 * FAR),

time: 79.3 us -> 74.8 us (0.943)
  Pallas kernels: 28.4 us -> 22 us
  local copies, waits for them, and re-layouts: 2.05 us -> 5.19 us
  other arithmetic: 0.89 us -> 0.04 us
    unnamed x8 -> x24, local copies, waits for them, and re-layouts: 2.05 us -> 5.19 us
    pallas_call x2, Pallas kernels: 22.1 us -> 19.8 us  [the longest x1 9.91 us: body(): call(functools.partial(backward_kernel, counts), 'backward', [ANY] * 2 +...]
    pallas_call x1, Pallas kernels: 2.31 us -> 0.52 us  [body(): call(pack_columns_kernel, 'pack_columns', [VMEM] * 3, (side, side), (), (...]
    ppermute x1, starting transfers between devices: 3.44 us -> 4.79 us  [body(): corner_a = lax.ppermute(corner, 'gx', rows_a)]
    pallas_call x1, Pallas kernels: 2.27 us -> 0.93 us  [body(): call(pack_rows_kernel, 'pack_rows', [HBM] * 3, (edge, edge), [buffer(6, t...]
    pallas_call x1, Pallas kernels: 1.72 us -> 0.8 us  [body(): call(functools.partial(scale_kernel, cells), 'scale', [VMEM, VMEM], array...]
    add x1, other arithmetic: 0.86 us -> 0.02 us  [body(): whole + lax.ppermute(mid, 'gy', [(n, n ^ k) for n in range(count_cols)])]
    ppermute x1, starting transfers between devices: 1.52 us -> 0.69 us  [body(): row_b = lax.ppermute(row_b, 'gx', rows_b)]
  transfers between devices with their start and end apart: 13 -> 13, of which waited for: 7 -> 7; matrix products, arithmetic and copies ran while one was open for 0% -> 0% of each run, Pallas kernels for 3% -> 1%
where the time goes in v2:
time: 74.8 us; the launch traced here: 74.4 us
  starting transfers between devices  23.3 us (31%)
  Pallas kernels  22 us (29%)
  waiting for transfers between devices  12.9 us (17%)
  blocking collectives  10.7 us (14%)
  local copies, waits for them, and re-layouts  5.19 us (7%)
    all_to_all x1, blocking collectives, body(): squares = lax.all_to_all(squares, ('gx', 'gy'), 0, 0, tiled=True)  10.7 us
    pallas_call x1, Pallas kernels, body(): call(functools.partial(backward_kernel, counts), 'backward', [ANY] * 2 +...  9.91 us
    pallas_call x1, Pallas kernels, body(): call(functools.partial(forward_kernel, counts), 'forward', [HBM] * 8 + [A...  9.86 us
    ppermute x3, starting transfers between devices, body(): lax.ppermute(mid, 'gy', [(n, n ^ k) for n in range(count_cols)])  8.4 us
    unnamed x24, local copies, waits for them, and re-layouts  5.19 us
    ppermute x3, waiting for transfers between devices, body(): lax.ppermute(whole, 'gx', [(n, n ^ k) for n in range(count_rows)])  5.03 us
    ppermute x3, starting transfers between devices, body(): lax.ppermute(whole, 'gx', [(n, n ^ k) for n in range(count_rows)])  4.85 us
    ppermute x1, starting transfers between devices, body(): corner_a = lax.ppermute(corner, 'gx', rows_a)  4.79 us
  transfers between devices with their start and end apart: 13, of which 7 were waited for; matrix products, arithmetic and copies ran while one was open for 0% of the time, Pallas kernels for 1%

profile of v2, /device:TPU:0, one launch (start us, length us, event | category | flops | bytes accessed | tf_op | source)
XLA Modules:
  0.0 74.4 jit_solution(11586889160950432940)
XLA Ops:
  0.0 0.0 copy-start
  0.0 0.0 copy-start.1
  0.0 1.1 %copy-done.1 = f32[3,8,32,128]{3,2,1,0:T(8,128)S(1)} copy-done((f32[3,8,32,128]{3,2,1,0:T(8,128)S(1)}, f32[3,8,32,128]{3,2,1,0:T(8,128)}, u32[]{:S(2)}) %copy-start.1) | copy-done | bytes 393240
  1.1 0.0 copy-start.2
  1.1 1.0 %copy-done.2 = f32[3,8,32,128]{3,2,1,0:T(8,128)S(1)} copy-done((f32[3,8,32,128]{3,2,1,0:T(8,128)S(1)}, f32[3,8,32,128]{3,2,1,0:T(8,128)}, u32[]{:S(2)}) %copy-start.2) | copy-done | bytes 393240
  2.1 0.0 copy-start.3
  2.1 0.9 %copy-done.3 = s32[8,32,128]{2,1,0:T(8,128)S(1)} copy-done((s32[8,32,128]{2,1,0:T(8,128)S(1)}, s32[8,32,128]{2,1,0:T(8,128)}, u32[]{:S(2)}) %copy-start.3) | copy-done | bytes 131096
  3.0 0.9 %pack_rows.1 = (f32[7,6,32,128]{3,2,1,0:T(8,128)S(1)}, f32[7,6,32,128]{3,2,1,0:T(8,128)S(1)}) custom-call(f32[3,8,32,128]{3,2,1,0:T(8,128)S(1)} %copy-done.1, f32[3,8,32,128]{3,2,1,0:T(8,128)S(1)} %copy-done.2, s32[8,32,128]{2,1,0:T(8,128)S(1)} %copy-done.3), custom_call_target="tpu_custom_call" | custom-call | tf_op jit(solution)/shard_map/pack_rows/pallas_call | solution.py:635
  4.0 0.5 collective-permute-start
  4.5 0.7 collective-permute-start.1
  5.2 0.5 pack_columns.1
  5.7 2.6 %collective-permute-start.2 = (f32[4,32,128]{2,1,0:T(8,128)S(1)}, f32[4,32,128]{2,1,0:T(8,128)S(1)}, u32[]{:S(2)}, u32[]{:S(2)}) collective-permute-start(f32[4,32,128]{2,1,0:T(8,128)S(1)} %get-tuple-element.16), channel_id=1, source_target_pairs={{0,1},{1,0},{2,3},{3,2},{4,5},{5,4},{6,7},{7,6},{8,9},{9,8},{10,11... | collective-permute-start | bytes 196616 | tf_op jit(solution)/shard_map/ppermute | solution.py:656
  8.3 0.7 collective-permute-start.3
  8.9 1.6 %collective-permute-done.2.own_a = f32[4,32,128]{2,1,0:T(8,128)S(1)} collective-permute-done((f32[4,32,128]{2,1,0:T(8,128)S(1)}, f32[4,32,128]{2,1,0:T(8,128)S(1)}, u32[]{:S(2)}, u32[]{:S(2)}) %collective-permute-start.2) | collective-permute-done | bytes 65568 | tf_op jit(solution)/shard_map/ppermute | solution.py:656
  10.5 0.0 collective-permute-done.3.own_b
  10.5 0.0 copy-start.8
  10.5 0.0 copy-start.9
  10.5 0.0 copy-start.4
  10.6 0.0 copy-start.5
  10.6 0.0 copy-start.6
  10.6 0.8 %collective-permute-start.5 = (f32[2,4,32,128]{3,2,1,0:T(8,128)S(1)}, f32[2,4,32,128]{3,2,1,0:T(8,128)S(1)}, u32[]{:S(2)}, u32[]{:S(2)}) collective-permute-start(f32[2,4,32,128]{3,2,1,0:T(8,128)S(1)} %pad_maximum_fusion.1), channel_id=1, source_target_pairs={{4,8},{8,4},{12,16},{16,12},{20,24},{24,20},{5,9},{9,5},{13,17},{1... | collective-permute-start | bytes 393224 | tf_op jit(solution)/shard_map/ppermute | solution.py:658
  11.4 4.8 %collective-permute-start.4 = (f32[2,4,32,128]{3,2,1,0:T(8,128)S(1)}, f32[2,4,32,128]{3,2,1,0:T(8,128)S(1)}, u32[]{:S(2)}, u32[]{:S(2)}) collective-permute-start(f32[2,4,32,128]{3,2,1,0:T(8,128)S(1)} %pad_maximum_fusion.1), channel_id=1, source_target_pairs={{0,4},{4,0},{8,12},{12,8},{16,20},{20,16},{24,28},{28,24},{1,5},{5... | collective-permute-start | bytes 393224 | tf_op jit(solution)/shard_map/ppermute | solution.py:659
  16.2 0.0 collective-permute-done.5.corner_b
  16.2 1.0 %collective-permute-done.4.corner_a = f32[2,4,32,128]{3,2,1,0:T(8,128)S(1)} collective-permute-done((f32[2,4,32,128]{3,2,1,0:T(8,128)S(1)}, f32[2,4,32,128]{3,2,1,0:T(8,128)S(1)}, u32[]{:S(2)}, u32[]{:S(2)}) %collective-permute-start.4) | collective-permute-done | bytes 131104 | tf_op jit(solution)/shard_map/ppermute | solution.py:659
  17.2 0.0 collective-permute-done.row_a
  17.2 0.0 collective-permute-done.1.row_b
  17.2 0.0 copy-done
  17.2 0.0 copy-start.7
  17.2 0.7 %copy-done.7 = f32[2,4,8,128]{3,2,1,0:T(8,128)S(1)} copy-done((f32[2,4,8,128]{3,2,1,0:T(8,128)S(1)}, f32[2,4,8,128]{3,2,1,0:T(8,128)}, u32[]{:S(2)}) %copy-start.7) | copy-done | bytes 32792
  17.9 0.0 copy-start.10
  17.9 0.7 copy-done.10
  18.7 0.0 copy-start.11
  18.7 0.7 copy-done.11
  19.3 9.9 %forward.1 = (f32[6,3,8,32,128]{4,3,2,1,0:T(8,128)S(1)}, f32[20,2,32,128]{3,2,1,0:T(8,128)S(1)}, f32[8,16,128]{2,1,0:T(8,128)S(1)}) custom-call(f32[8]{0:T(128)S(1)} %copy-done.11, bf16[32,384]{1,0:T(8,128)(2,1)S(1)} %copy-done.10, f32[2,4,8,128]{3,2,1,0:T(8,128)S(1)} %copy-done.7, f32[3,8,32,128]{3,2,1,0:T(8,128)S(1)} %copy-done.1, ...), custom_call_target="tpu_custom_call" | custom-call | tf_op jit(solution)/shard_map/forward/pallas_call | solution.py:668
  29.2 3.5 %collective-permute-start.8 = (f32[8,16,128]{2,1,0:T(8,128)S(1)}, f32[8,16,128]{2,1,0:T(8,128)S(1)}, u32[]{:S(2)}, u32[]{:S(2)}) collective-permute-start(f32[8,16,128]{2,1,0:T(8,128)S(1)} %get-tuple-element.18), channel_id=1, source_target_pairs={{0,3},{1,2},{2,1},{3,0},{4,7},{5,6},{6,5},{7,4},{8,11},{9,10},{10,... | collective-permute-start | bytes 196616 | tf_op jit(solution)/shard_map/ppermute | solution.py:696
  32.7 3.5 %collective-permute-start.7 = (f32[8,16,128]{2,1,0:T(8,128)S(1)}, f32[8,16,128]{2,1,0:T(8,128)S(1)}, u32[]{:S(2)}, u32[]{:S(2)}) collective-permute-start(f32[8,16,128]{2,1,0:T(8,128)S(1)} %get-tuple-element.18), channel_id=1, source_target_pairs={{0,2},{1,3},{2,0},{3,1},{4,6},{5,7},{6,4},{7,5},{8,10},{9,11},{10,... | collective-permute-start | bytes 196616 | tf_op jit(solution)/shard_map/ppermute | solution.py:696
  36.2 1.4 %collective-permute-start.6 = (f32[8,16,128]{2,1,0:T(8,128)S(1)}, f32[8,16,128]{2,1,0:T(8,128)S(1)}, u32[]{:S(2)}, u32[]{:S(2)}) collective-permute-start(f32[8,16,128]{2,1,0:T(8,128)S(1)} %get-tuple-element.18), channel_id=1, source_target_pairs={{0,1},{1,0},{2,3},{3,2},{4,5},{5,4},{6,7},{7,6},{8,9},{9,8},{10,11... | collective-permute-start | bytes 196616 | tf_op jit(solution)/shard_map/ppermute | solution.py:696
  37.6 0.0 collective-permute-done.8
  37.6 0.9 %collective-permute-done.7 = f32[8,16,128]{2,1,0:T(8,128)S(1)} collective-permute-done((f32[8,16,128]{2,1,0:T(8,128)S(1)}, f32[8,16,128]{2,1,0:T(8,128)S(1)}, u32[]{:S(2)}, u32[]{:S(2)}) %collective-permute-start.7) | collective-permute-done | bytes 65568 | tf_op jit(solution)/shard_map/ppermute | solution.py:696
  38.5 2.9 %collective-permute-done.6 = f32[8,16,128]{2,1,0:T(8,128)S(1)} collective-permute-done((f32[8,16,128]{2,1,0:T(8,128)S(1)}, f32[8,16,128]{2,1,0:T(8,128)S(1)}, u32[]{:S(2)}, u32[]{:S(2)}) %collective-permute-start.6) | collective-permute-done | bytes 65568 | tf_op jit(solution)/shard_map/ppermute | solution.py:696
  41.4 4.2 %collective-permute-start.11 = (f32[8,16,128]{2,1,0:T(8,128)S(1)}, f32[8,16,128]{2,1,0:T(8,128)S(1)}, u32[]{:S(2)}, u32[]{:S(2)}) collective-permute-start(f32[8,16,128]{2,1,0:T(8,128)S(1)} %add_add_fusion), channel_id=1, source_target_pairs={{0,24},{4,28},{8,16},{12,20},{16,8},{20,12},{24,0},{28,4},{1,25},{... | collective-permute-start | bytes 196616 | tf_op jit(solution)/shard_map/ppermute | solution.py:699
  45.6 0.3 collective-permute-start.10
  45.9 0.4 collective-permute-start.9
  46.2 1.9 %collective-permute-done.11 = f32[8,16,128]{2,1,0:T(8,128)S(1)} collective-permute-done((f32[8,16,128]{2,1,0:T(8,128)S(1)}, f32[8,16,128]{2,1,0:T(8,128)S(1)}, u32[]{:S(2)}, u32[]{:S(2)}) %collective-permute-start.11) | collective-permute-done | bytes 65568 | tf_op jit(solution)/shard_map/ppermute | solution.py:699
  48.2 3.1 %collective-permute-done.10 = f32[8,16,128]{2,1,0:T(8,128)S(1)} collective-permute-done((f32[8,16,128]{2,1,0:T(8,128)S(1)}, f32[8,16,128]{2,1,0:T(8,128)S(1)}, u32[]{:S(2)}, u32[]{:S(2)}) %collective-permute-start.10) | collective-permute-done | bytes 65568 | tf_op jit(solution)/shard_map/ppermute | solution.py:699
  51.3 0.0 collective-permute-done.9
  51.3 0.1 collective-permute-start.12
  51.4 1.5 %collective-permute-done.12.sibling = f32[4,8,16,128]{3,2,1,0:T(8,128)S(1)} collective-permute-done((f32[4,8,16,128]{3,2,1,0:T(8,128)S(1)}, f32[4,8,16,128]{3,2,1,0:T(8,128)S(1)}, u32[]{:S(2)}, u32[]{:S(2)}) %collective-permute-start.12) | collective-permute-done | bytes 262176 | tf_op jit(solution)/shard_map/ppermute | solution.py:701
  52.9 0.0 copy-done.8
  52.9 0.0 copy-done.9
  52.9 0.0 copy-done.4
  52.9 0.0 copy-done.5
  52.9 0.0 copy-done.6
  52.9 9.9 %backward.1 = (f32[8,32,128]{2,1,0:T(8,128)S(1)}, f32[32,128]{1,0:T(8,128)S(1)}) custom-call(f32[4,8,16,128]{3,2,1,0:T(8,128)S(1)} %pad_maximum_fusion.own, f32[4,8,16,128]{3,2,1,0:T(8,128)S(1)} %collective-permute-done.12.sibling, f32[8,64,64]{2,1,0:T(8,128)S(1)} %copy-done.6, f32[2,4,8,128]{3,2,1,0:T(8,128)S(1)} %copy-done.8, ...), custom_call_target="tpu_custom_call" | custom-call | tf_op jit(solution)/shard_map/backward/pallas_call | solution.py:709
  62.8 10.7 %all_to_all.11 = f32[32,1,128]{2,1,0:T(1,128)S(1)} all-to-all(f32[32,1,128]{2,1,0:T(1,128)S(1)} %bitcast.13), channel_id=1, replica_groups=mesh['gx'=8,'gy'=4] {'gx','gy'}, dimensions={0} | all-to-all | bytes 32768 | tf_op jit(solution)/shard_map/all_to_all | solution.py:735
  73.6 0.8 %scale.1 = f32[8,32,128]{2,1,0:T(8,128)} custom-call(f32[32,128]{1,0:T(8,128)S(1)} %bitcast.12, f32[8,32,128]{2,1,0:T(8,128)S(1)} %get-tuple-element.22.gradient), custom_call_target="tpu_custom_call" | custom-call | tf_op jit(solution)/shard_map/scale/pallas_call | solution.py:737
  (3 shorter events, 0.0 us)
Async XLA Ops:
  0.0 17.2 %copy-start = (bf16[3,8,128,256]{3,2,1,0:T(8,128)(2,1)S(1)}, bf16[3,8,128,256]{3,2,1,0:T(8,128)(2,1)}, u32[]{:S(2)}) copy-start(bf16[3,8,128,256]{3,2,1,0:T(8,128)(2,1)} %constant.12.clone.table.table_in) | copy-start | bytes 4718596
  0.0 1.1 %copy-start.1 = (f32[3,8,32,128]{3,2,1,0:T(8,128)S(1)}, f32[3,8,32,128]{3,2,1,0:T(8,128)}, u32[]{:S(2)}) copy-start(f32[3,8,32,128]{3,2,1,0:T(8,128)} %e.5) | copy-start | bytes 1179652
  1.1 1.0 %copy-start.2 = (f32[3,8,32,128]{3,2,1,0:T(8,128)S(1)}, f32[3,8,32,128]{3,2,1,0:T(8,128)}, u32[]{:S(2)}) copy-start(f32[3,8,32,128]{3,2,1,0:T(8,128)} %h.5) | copy-start | bytes 1179652
  2.1 0.9 %copy-start.3 = (s32[8,32,128]{2,1,0:T(8,128)S(1)}, s32[8,32,128]{2,1,0:T(8,128)}, u32[]{:S(2)}) copy-start(s32[8,32,128]{2,1,0:T(8,128)} %material.5) | copy-start | bytes 393220
  4.0 13.2 %collective-permute-start = (f32[7,6,32,128]{3,2,1,0:T(8,128)S(1)}, f32[7,6,32,128]{3,2,1,0:T(8,128)S(1)}, u32[]{:S(2)}, u32[]{:S(2)}) collective-permute-start(f32[7,6,32,128]{3,2,1,0:T(8,128)S(1)} %get-tuple-element.14), channel_id=1, source_target_pairs={{0,4},{4,0},{8,12},{12,8},{16,20},{20,16},{24,28},{28,24},{1,5},{5... | collective-permute-start | bytes 2064392 | tf_op jit(solution)/shard_map/ppermute | solution.py:651
  4.5 12.7 %collective-permute-start.1 = (f32[7,6,32,128]{3,2,1,0:T(8,128)S(1)}, f32[7,6,32,128]{3,2,1,0:T(8,128)S(1)}, u32[]{:S(2)}, u32[]{:S(2)}) collective-permute-start(f32[7,6,32,128]{3,2,1,0:T(8,128)S(1)} %get-tuple-element.15), channel_id=1, source_target_pairs={{4,8},{8,4},{12,16},{16,12},{20,24},{24,20},{5,9},{9,5},{13,17},{1... | collective-permute-start | bytes 2064392 | tf_op jit(solution)/shard_map/ppermute | solution.py:650
  5.7 4.8 %collective-permute-start.2 = (f32[4,32,128]{2,1,0:T(8,128)S(1)}, f32[4,32,128]{2,1,0:T(8,128)S(1)}, u32[]{:S(2)}, u32[]{:S(2)}) collective-permute-start(f32[4,32,128]{2,1,0:T(8,128)S(1)} %get-tuple-element.16), channel_id=1, source_target_pairs={{0,1},{1,0},{2,3},{3,2},{4,5},{5,4},{6,7},{7,6},{8,9},{9,8},{10,11... | collective-permute-start | bytes 196616 | tf_op jit(solution)/shard_map/ppermute | solution.py:656
  8.3 2.2 %collective-permute-start.3 = (f32[4,32,128]{2,1,0:T(8,128)S(1)}, f32[4,32,128]{2,1,0:T(8,128)S(1)}, u32[]{:S(2)}, u32[]{:S(2)}) collective-permute-start(f32[4,32,128]{2,1,0:T(8,128)S(1)} %get-tuple-element.17), channel_id=1, source_target_pairs={{1,2},{2,1},{5,6},{6,5},{9,10},{10,9},{13,14},{14,13},{17,18},{18,... | collective-permute-start | bytes 196616 | tf_op jit(solution)/shard_map/ppermute | solution.py:655
  10.5 42.4 %copy-start.8 = (f32[2,4,8,128]{3,2,1,0:T(8,128)S(1)}, f32[2,4,8,128]{3,2,1,0:T(8,128)}, u32[]{:S(2)}) copy-start(f32[2,4,8,128]{3,2,1,0:T(8,128)} %constant.13.clone.twist_in.twist) | copy-start | bytes 98308
  10.5 42.4 %copy-start.9 = (bf16[192,48]{1,0:T(8,128)(2,1)S(1)}, bf16[192,48]{1,0:T(8,128)(2,1)}, u32[]{:S(2)}) copy-start(bf16[192,48]{1,0:T(8,128)(2,1)} %constant.15.clone.weights) | copy-start | bytes 55300
  10.5 42.4 %copy-start.4 = (f32[8,2,80,64]{3,2,1,0:T(8,128)S(1)}, f32[8,2,80,64]{3,2,1,0:T(8,128)}, u32[]{:S(2)}) copy-start(f32[8,2,80,64]{3,2,1,0:T(8,128)} %constant.17.clone.rows_back_in) | copy-start | bytes 983044
  10.6 42.4 %copy-start.5 = (bf16[8,128,192]{2,1,0:T(8,128)(2,1)S(1)}, bf16[8,128,192]{2,1,0:T(8,128)(2,1)}, u32[]{:S(2)}) copy-start(bf16[8,128,192]{2,1,0:T(8,128)(2,1)} %constant.16.clone.rows_far) | copy-start | bytes 1179652
  10.6 42.4 %copy-start.6 = (f32[8,64,64]{2,1,0:T(8,128)S(1)}, f32[8,64,64]{2,1,0:T(8,128)}, u32[]{:S(2)}) copy-start(f32[8,64,64]{2,1,0:T(8,128)} %target.1) | copy-start | bytes 393220
  10.6 5.6 %collective-permute-start.5 = (f32[2,4,32,128]{3,2,1,0:T(8,128)S(1)}, f32[2,4,32,128]{3,2,1,0:T(8,128)S(1)}, u32[]{:S(2)}, u32[]{:S(2)}) collective-permute-start(f32[2,4,32,128]{3,2,1,0:T(8,128)S(1)} %pad_maximum_fusion.1), channel_id=1, source_target_pairs={{4,8},{8,4},{12,16},{16,12},{20,24},{24,20},{5,9},{9,5},{13,17},{1... | collective-permute-start | bytes 393224 | tf_op jit(solution)/shard_map/ppermute | solution.py:658
  11.4 5.8 %collective-permute-start.4 = (f32[2,4,32,128]{3,2,1,0:T(8,128)S(1)}, f32[2,4,32,128]{3,2,1,0:T(8,128)S(1)}, u32[]{:S(2)}, u32[]{:S(2)}) collective-permute-start(f32[2,4,32,128]{3,2,1,0:T(8,128)S(1)} %pad_maximum_fusion.1), channel_id=1, source_target_pairs={{0,4},{4,0},{8,12},{12,8},{16,20},{20,16},{24,28},{28,24},{1,5},{5... | collective-permute-start | bytes 393224 | tf_op jit(solution)/shard_map/ppermute | solution.py:659
  17.2 0.8 %copy-start.7 = (f32[2,4,8,128]{3,2,1,0:T(8,128)S(1)}, f32[2,4,8,128]{3,2,1,0:T(8,128)}, u32[]{:S(2)}) copy-start(f32[2,4,8,128]{3,2,1,0:T(8,128)} %constant.13.clone.twist_in.twist) | copy-start | bytes 98308
  17.9 0.7 copy-start.10
  18.7 0.7 copy-start.11
  29.2 8.4 %collective-permute-start.8 = (f32[8,16,128]{2,1,0:T(8,128)S(1)}, f32[8,16,128]{2,1,0:T(8,128)S(1)}, u32[]{:S(2)}, u32[]{:S(2)}) collective-permute-start(f32[8,16,128]{2,1,0:T(8,128)S(1)} %get-tuple-element.18), channel_id=1, source_target_pairs={{0,3},{1,2},{2,1},{3,0},{4,7},{5,6},{6,5},{7,4},{8,11},{9,10},{10,... | collective-permute-start | bytes 196616 | tf_op jit(solution)/shard_map/ppermute | solution.py:696
  32.7 5.8 %collective-permute-start.7 = (f32[8,16,128]{2,1,0:T(8,128)S(1)}, f32[8,16,128]{2,1,0:T(8,128)S(1)}, u32[]{:S(2)}, u32[]{:S(2)}) collective-permute-start(f32[8,16,128]{2,1,0:T(8,128)S(1)} %get-tuple-element.18), channel_id=1, source_target_pairs={{0,2},{1,3},{2,0},{3,1},{4,6},{5,7},{6,4},{7,5},{8,10},{9,11},{10,... | collective-permute-start | bytes 196616 | tf_op jit(solution)/shard_map/ppermute | solution.py:696
  36.2 5.2 %collective-permute-start.6 = (f32[8,16,128]{2,1,0:T(8,128)S(1)}, f32[8,16,128]{2,1,0:T(8,128)S(1)}, u32[]{:S(2)}, u32[]{:S(2)}) collective-permute-start(f32[8,16,128]{2,1,0:T(8,128)S(1)} %get-tuple-element.18), channel_id=1, source_target_pairs={{0,1},{1,0},{2,3},{3,2},{4,5},{5,4},{6,7},{7,6},{8,9},{9,8},{10,11... | collective-permute-start | bytes 196616 | tf_op jit(solution)/shard_map/ppermute | solution.py:696
  41.4 6.8 %collective-permute-start.11 = (f32[8,16,128]{2,1,0:T(8,128)S(1)}, f32[8,16,128]{2,1,0:T(8,128)S(1)}, u32[]{:S(2)}, u32[]{:S(2)}) collective-permute-start(f32[8,16,128]{2,1,0:T(8,128)S(1)} %add_add_fusion), channel_id=1, source_target_pairs={{0,24},{4,28},{8,16},{12,20},{16,8},{20,12},{24,0},{28,4},{1,25},{... | collective-permute-start | bytes 196616 | tf_op jit(solution)/shard_map/ppermute | solution.py:699
  45.6 5.7 %collective-permute-start.10 = (f32[8,16,128]{2,1,0:T(8,128)S(1)}, f32[8,16,128]{2,1,0:T(8,128)S(1)}, u32[]{:S(2)}, u32[]{:S(2)}) collective-permute-start(f32[8,16,128]{2,1,0:T(8,128)S(1)} %add_add_fusion), channel_id=1, source_target_pairs={{0,16},{4,20},{8,24},{12,28},{16,0},{20,4},{24,8},{28,12},{1,17},{... | collective-permute-start | bytes 196616 | tf_op jit(solution)/shard_map/ppermute | solution.py:699
  45.9 5.4 %collective-permute-start.9 = (f32[8,16,128]{2,1,0:T(8,128)S(1)}, f32[8,16,128]{2,1,0:T(8,128)S(1)}, u32[]{:S(2)}, u32[]{:S(2)}) collective-permute-start(f32[8,16,128]{2,1,0:T(8,128)S(1)} %add_add_fusion), channel_id=1, source_target_pairs={{0,8},{4,12},{8,0},{12,4},{16,24},{20,28},{24,16},{28,20},{1,9},{5... | collective-permute-start | bytes 196616 | tf_op jit(solution)/shard_map/ppermute | solution.py:699
  51.3 1.6 %collective-permute-start.12 = (f32[4,8,16,128]{3,2,1,0:T(8,128)S(1)}, f32[4,8,16,128]{3,2,1,0:T(8,128)S(1)}, u32[]{:S(2)}, u32[]{:S(2)}) collective-permute-start(f32[4,8,16,128]{3,2,1,0:T(8,128)S(1)} %pad_maximum_fusion.own), channel_id=1, source_target_pairs={{0,4},{4,0},{8,12},{12,8},{16,20},{20,16},{24,28},{28,24},{1,5},{5... | collective-permute-start | bytes 786440 | tf_op jit(solution)/shard_map/ppermute | solution.py:701

commit v3 on v2

--- a/solution.py
+++ b/solution.py
@@ -39,13 +39,6 @@
     return np.concatenate([np.cos(angle), -np.sin(angle)], axis=1)
 
 
-def lens_table(depth):
-    weights = time_table(depth)
-    wide = np.stack([weights, weights], axis=2)
-    wide = wide.transpose(1, 0, 2, 3).reshape(2 * NF, -1)
-    return np.concatenate(split_table(wide), axis=0)
-
-
 def source_table(depth):
     flat = time_table(depth).transpose(0, 2, 1).reshape(ITERS * depth, 2 * NF)
     high, low = split_table(flat)
@@ -113,6 +106,25 @@
 
 def dot(left, right):
     return jnp.dot(left, right, preferred_element_type=F32)
+
+
+def lens_weights(depth):
+    shape = (2 * NF, 2 * ITERS * depth)
+    row = lax.broadcasted_iota(jnp.int32, shape, 0)
+    lane = lax.broadcasted_iota(jnp.int32, shape, 1)
+    moment = lane // (2 * depth) + 1
+    turns = (2 * (row % NF) + 1) * (7 * moment + lane % depth)
+    turns = (turns + jnp.where(row < NF, 0, 16)) % 64
+    return jnp.concatenate(split(jnp.cos(turns.astype(F32) * (TWO_PI / 64))), axis=0)
+
+
+def tile_twist(j):
+    shape = (NF, 2 * FAR)
+    freq = lax.broadcasted_iota(jnp.int32, shape, 0)
+    lane = lax.broadcasted_iota(jnp.int32, shape, 1)
+    turns = ((lane % FAR + FAR // 2) * (NF + freq) * j) % 16
+    angle = turns.astype(F32) * (TWO_PI / 16)
+    return jnp.cos(angle), jnp.where(lane < FAR, 1.0, -1.0) * jnp.sin(angle)
 
 
 def half_turn(value):
@@ -257,8 +269,8 @@
 
 
 def forward_kernel(
-    counts, eps_in, weights_in, twist_in, e, h, material, row_a, row_b, own_a, own_b, corner_a, corner_b, table,
-    kept_out, inverse_out, mid, electric, magnetic, inverse, kept, index, cols, phases, stash, lens, eps, weights, twist, semaphores,
+    counts, eps_in, e, h, material, row_a, row_b, own_a, own_b, corner_a, corner_b, table,
+    kept_out, inverse_out, mid, electric, magnetic, inverse, kept, index, cols, phases, stash, lens, eps, semaphores,
 ):
     tile_rows, depth, tile_cols = material.shape
     count_rows, count_cols = counts
@@ -283,10 +295,12 @@
     pairs.append((h, magnetic.at[:, own, 0, inner, :]))
     pairs.append((eps_in, eps))
     early = len(pairs)
-    pairs += [(weights_in, weights), (twist_in, twist)] + column_blocks(table, phases, tile_cols)
+    pairs += column_blocks(table, phases, tile_cols)
     started = copies(pairs, semaphores)
     clear_pads(electric)
     clear_pads(magnetic)
+    weights = lens_weights(depth)
+    twist = tile_twist(j)
     for copy in started[:early]:
         copy.wait()
 
@@ -386,7 +400,7 @@
     waves = 2 * NF
     for p in range(2):
         for q in range(tile_rows // 2):
-            value = dot(weights[...], stash[p, q])
+            value = dot(weights, stash[p, q])
             value = value[:waves] + value[waves:]
             for s in range(2):
                 base = (p * tile_rows + 2 * q + s) * waves
@@ -401,7 +415,7 @@
         )
         value = value[:planes] + value[planes:]
         value = value[:, : 2 * FAR] + value[:, 2 * FAR :]
-        mid[f] = value * twist[0, j, f : f + 1, :] + half_turn(value) * twist[1, j, f : f + 1, :]
+        mid[f] = value * twist[0][f : f + 1] + half_turn(value) * twist[1][f : f + 1]
     for copy in sends:
         copy.wait()
 
@@ -660,7 +674,6 @@
 
     table = jnp.asarray(column_table(tile_cols, 2 * tile_cols))
     twist = jnp.asarray(column_twist(count_cols))
-    weights = jnp.asarray(lens_table(depth))
     ext = tile_rows + 2 * GHOST
     waves = 2 * NF
     kept = (ITERS, 3, tile_rows, depth, tile_cols)
@@ -668,7 +681,7 @@
     kept_out, inverse_out, mid = call(
         functools.partial(forward_kernel, counts),
         "forward",
-        [HBM] * 8 + [ANY] * 4 + [HBM],
+        [HBM] * 6 + [ANY] * 4 + [HBM],
         (array(*kept), array(*inverse), array(NF, 2 * tile_rows, 2 * FAR)),
         [
             buffer(3, ext, 2, depth + 2 * PAD, tile_cols),
@@ -681,13 +694,11 @@
             pltpu.VMEM((2, tile_rows // 2, 2 * ITERS * depth, 2 * tile_cols), BF16),
             buffer(2 * tile_rows * waves, tile_cols),
             pltpu.SMEM(eps_table.shape, F32),
-            pltpu.VMEM(weights.shape, BF16),
-            buffer(*twist.shape),
-            DMA((24,)),
+            DMA((22,)),
         ],
         (HBM, HBM, VMEM),
     )(
-        eps_table, weights, twist, e_init, h_init, material, row_a, row_b, col_a, col_b,
+        eps_table, e_init, h_init, material, row_a, row_b, col_a, col_b,
         corner_a, corner_b, table,
     )
 

time: 74.8 us -> 73.1 us (0.977)
  local copies, waits for them, and re-layouts: 5.19 us -> 3.7 us
    unnamed x24 -> x20, local copies, waits for them, and re-layouts: 5.19 us -> 3.7 us
where the time goes in v3:
time: 73.1 us; the launch traced here: 72.9 us
  starting transfers between devices  23.4 us (32%)
  Pallas kernels  22 us (30%)
  waiting for transfers between devices  12.9 us (18%)
  blocking collectives  10.7 us (15%)
  local copies, waits for them, and re-layouts  3.7 us (5%)
    all_to_all x1, blocking collectives, body(): squares = lax.all_to_all(squares, ('gx', 'gy'), 0, 0, tiled=True)  10.7 us
    pallas_call x1, Pallas kernels, body(): call(functools.partial(backward_kernel, counts), 'backward', [ANY] * 2 +...  9.91 us
    pallas_call x1, Pallas kernels, body(): call(functools.partial(forward_kernel, counts), 'forward', [HBM] * 6 + [A...  9.84 us
    ppermute x3, starting transfers between devices, body(): lax.ppermute(mid, 'gy', [(n, n ^ k) for n in range(count_cols)])  8.4 us
    ppermute x3, waiting for transfers between devices, body(): lax.ppermute(whole, 'gx', [(n, n ^ k) for n in range(count_rows)])  5.03 us
    ppermute x3, starting transfers between devices, body(): lax.ppermute(whole, 'gx', [(n, n ^ k) for n in range(count_rows)])  4.85 us
    ppermute x1, starting transfers between devices, body(): corner_a = lax.ppermute(corner, 'gx', rows_a)  4.79 us
    ppermute x3, waiting for transfers between devices, body(): lax.ppermute(mid, 'gy', [(n, n ^ k) for n in range(count_cols)])  3.77 us
  transfers between devices with their start and end apart: 13, of which 7 were waited for; matrix products, arithmetic and copies ran while one was open for 0% of the time, Pallas kernels for 1%

profile of v3, /device:TPU:0, one launch (start us, length us, event | category | flops | bytes accessed | tf_op | source)
XLA Modules:
  0.0 72.9 jit_solution(14916635598056382325)
XLA Ops:
  0.0 0.0 copy-start
  0.0 0.0 copy-start.1
  0.0 1.1 %copy-done.1 = f32[3,8,32,128]{3,2,1,0:T(8,128)S(1)} copy-done((f32[3,8,32,128]{3,2,1,0:T(8,128)S(1)}, f32[3,8,32,128]{3,2,1,0:T(8,128)}, u32[]{:S(2)}) %copy-start.1) | copy-done | bytes 393240
  1.1 0.0 copy-start.2
  1.1 1.0 %copy-done.2 = f32[3,8,32,128]{3,2,1,0:T(8,128)S(1)} copy-done((f32[3,8,32,128]{3,2,1,0:T(8,128)S(1)}, f32[3,8,32,128]{3,2,1,0:T(8,128)}, u32[]{:S(2)}) %copy-start.2) | copy-done | bytes 393240
  2.1 0.0 copy-start.3
  2.1 0.9 %copy-done.3 = s32[8,32,128]{2,1,0:T(8,128)S(1)} copy-done((s32[8,32,128]{2,1,0:T(8,128)S(1)}, s32[8,32,128]{2,1,0:T(8,128)}, u32[]{:S(2)}) %copy-start.3) | copy-done | bytes 131096
  3.0 0.9 %pack_rows.1 = (f32[7,6,32,128]{3,2,1,0:T(8,128)S(1)}, f32[7,6,32,128]{3,2,1,0:T(8,128)S(1)}) custom-call(f32[3,8,32,128]{3,2,1,0:T(8,128)S(1)} %copy-done.1, f32[3,8,32,128]{3,2,1,0:T(8,128)S(1)} %copy-done.2, s32[8,32,128]{2,1,0:T(8,128)S(1)} %copy-done.3), custom_call_target="tpu_custom_call" | custom-call | tf_op jit(solution)/shard_map/pack_rows/pallas_call | solution.py:649
  4.0 0.5 collective-permute-start
  4.5 0.7 collective-permute-start.1
  5.2 0.5 pack_columns.1
  5.7 2.6 %collective-permute-start.2 = (f32[4,32,128]{2,1,0:T(8,128)S(1)}, f32[4,32,128]{2,1,0:T(8,128)S(1)}, u32[]{:S(2)}, u32[]{:S(2)}) collective-permute-start(f32[4,32,128]{2,1,0:T(8,128)S(1)} %get-tuple-element.16), channel_id=1, source_target_pairs={{0,1},{1,0},{2,3},{3,2},{4,5},{5,4},{6,7},{7,6},{8,9},{9,8},{10,11... | collective-permute-start | bytes 196616 | tf_op jit(solution)/shard_map/ppermute | solution.py:670
  8.3 0.7 collective-permute-start.3
  8.9 1.6 %collective-permute-done.2.own_a = f32[4,32,128]{2,1,0:T(8,128)S(1)} collective-permute-done((f32[4,32,128]{2,1,0:T(8,128)S(1)}, f32[4,32,128]{2,1,0:T(8,128)S(1)}, u32[]{:S(2)}, u32[]{:S(2)}) %collective-permute-start.2) | collective-permute-done | bytes 65568 | tf_op jit(solution)/shard_map/ppermute | solution.py:670
  10.5 0.0 collective-permute-done.3.own_b
  10.5 0.0 copy-start.4
  10.6 0.0 copy-start.5
  10.6 0.0 copy-start.6
  10.6 0.0 copy-start.7
  10.6 0.0 copy-start.8
  10.6 0.8 %collective-permute-start.5 = (f32[2,4,32,128]{3,2,1,0:T(8,128)S(1)}, f32[2,4,32,128]{3,2,1,0:T(8,128)S(1)}, u32[]{:S(2)}, u32[]{:S(2)}) collective-permute-start(f32[2,4,32,128]{3,2,1,0:T(8,128)S(1)} %pad_maximum_fusion.1), channel_id=1, source_target_pairs={{4,8},{8,4},{12,16},{16,12},{20,24},{24,20},{5,9},{9,5},{13,17},{1... | collective-permute-start | bytes 393224 | tf_op jit(solution)/shard_map/ppermute | solution.py:672
  11.4 4.8 %collective-permute-start.4 = (f32[2,4,32,128]{3,2,1,0:T(8,128)S(1)}, f32[2,4,32,128]{3,2,1,0:T(8,128)S(1)}, u32[]{:S(2)}, u32[]{:S(2)}) collective-permute-start(f32[2,4,32,128]{3,2,1,0:T(8,128)S(1)} %pad_maximum_fusion.1), channel_id=1, source_target_pairs={{0,4},{4,0},{8,12},{12,8},{16,20},{20,16},{24,28},{28,24},{1,5},{5... | collective-permute-start | bytes 393224 | tf_op jit(solution)/shard_map/ppermute | solution.py:673
  16.2 0.0 collective-permute-done.5.corner_b
  16.2 1.0 %collective-permute-done.4.corner_a = f32[2,4,32,128]{3,2,1,0:T(8,128)S(1)} collective-permute-done((f32[2,4,32,128]{3,2,1,0:T(8,128)S(1)}, f32[2,4,32,128]{3,2,1,0:T(8,128)S(1)}, u32[]{:S(2)}, u32[]{:S(2)}) %collective-permute-start.4) | collective-permute-done | bytes 131104 | tf_op jit(solution)/shard_map/ppermute | solution.py:673
  17.2 0.0 collective-permute-done.row_a
  17.2 0.0 collective-permute-done.1.row_b
  17.2 0.0 copy-done
  17.2 0.0 copy-start.9
  17.2 0.6 copy-done.9
  17.9 9.8 %forward.1 = (f32[6,3,8,32,128]{4,3,2,1,0:T(8,128)S(1)}, f32[20,2,32,128]{3,2,1,0:T(8,128)S(1)}, f32[8,16,128]{2,1,0:T(8,128)S(1)}) custom-call(f32[8]{0:T(128)S(1)} %copy-done.9, f32[3,8,32,128]{3,2,1,0:T(8,128)S(1)} %copy-done.1, f32[3,8,32,128]{3,2,1,0:T(8,128)S(1)} %copy-done.2, s32[8,32,128]{2,1,0:T(8,128)S(1)} %copy-done.3, ...), custom_call_target="tpu_custom_call" | custom-call | tf_op jit(solution)/shard_map/forward/pallas_call | solution.py:681
  27.7 3.5 %collective-permute-start.8 = (f32[8,16,128]{2,1,0:T(8,128)S(1)}, f32[8,16,128]{2,1,0:T(8,128)S(1)}, u32[]{:S(2)}, u32[]{:S(2)}) collective-permute-start(f32[8,16,128]{2,1,0:T(8,128)S(1)} %get-tuple-element.18), channel_id=1, source_target_pairs={{0,3},{1,2},{2,1},{3,0},{4,7},{5,6},{6,5},{7,4},{8,11},{9,10},{10,... | collective-permute-start | bytes 196616 | tf_op jit(solution)/shard_map/ppermute | solution.py:707
  31.2 3.5 %collective-permute-start.7 = (f32[8,16,128]{2,1,0:T(8,128)S(1)}, f32[8,16,128]{2,1,0:T(8,128)S(1)}, u32[]{:S(2)}, u32[]{:S(2)}) collective-permute-start(f32[8,16,128]{2,1,0:T(8,128)S(1)} %get-tuple-element.18), channel_id=1, source_target_pairs={{0,2},{1,3},{2,0},{3,1},{4,6},{5,7},{6,4},{7,5},{8,10},{9,11},{10,... | collective-permute-start | bytes 196616 | tf_op jit(solution)/shard_map/ppermute | solution.py:707
  34.7 1.4 %collective-permute-start.6 = (f32[8,16,128]{2,1,0:T(8,128)S(1)}, f32[8,16,128]{2,1,0:T(8,128)S(1)}, u32[]{:S(2)}, u32[]{:S(2)}) collective-permute-start(f32[8,16,128]{2,1,0:T(8,128)S(1)} %get-tuple-element.18), channel_id=1, source_target_pairs={{0,1},{1,0},{2,3},{3,2},{4,5},{5,4},{6,7},{7,6},{8,9},{9,8},{10,11... | collective-permute-start | bytes 196616 | tf_op jit(solution)/shard_map/ppermute | solution.py:707
  36.1 0.0 collective-permute-done.8
  36.1 0.9 %collective-permute-done.7 = f32[8,16,128]{2,1,0:T(8,128)S(1)} collective-permute-done((f32[8,16,128]{2,1,0:T(8,128)S(1)}, f32[8,16,128]{2,1,0:T(8,128)S(1)}, u32[]{:S(2)}, u32[]{:S(2)}) %collective-permute-start.7) | collective-permute-done | bytes 65568 | tf_op jit(solution)/shard_map/ppermute | solution.py:707
  37.0 2.9 %collective-permute-done.6 = f32[8,16,128]{2,1,0:T(8,128)S(1)} collective-permute-done((f32[8,16,128]{2,1,0:T(8,128)S(1)}, f32[8,16,128]{2,1,0:T(8,128)S(1)}, u32[]{:S(2)}, u32[]{:S(2)}) %collective-permute-start.6) | collective-permute-done | bytes 65568 | tf_op jit(solution)/shard_map/ppermute | solution.py:707
  39.9 4.2 %collective-permute-start.11 = (f32[8,16,128]{2,1,0:T(8,128)S(1)}, f32[8,16,128]{2,1,0:T(8,128)S(1)}, u32[]{:S(2)}, u32[]{:S(2)}) collective-permute-start(f32[8,16,128]{2,1,0:T(8,128)S(1)} %add_add_fusion), channel_id=1, source_target_pairs={{0,24},{4,28},{8,16},{12,20},{16,8},{20,12},{24,0},{28,4},{1,25},{... | collective-permute-start | bytes 196616 | tf_op jit(solution)/shard_map/ppermute | solution.py:710
  44.1 0.3 collective-permute-start.10
  44.4 0.4 collective-permute-start.9
  44.8 1.9 %collective-permute-done.11 = f32[8,16,128]{2,1,0:T(8,128)S(1)} collective-permute-done((f32[8,16,128]{2,1,0:T(8,128)S(1)}, f32[8,16,128]{2,1,0:T(8,128)S(1)}, u32[]{:S(2)}, u32[]{:S(2)}) %collective-permute-start.11) | collective-permute-done | bytes 65568 | tf_op jit(solution)/shard_map/ppermute | solution.py:710
  46.7 3.1 %collective-permute-done.10 = f32[8,16,128]{2,1,0:T(8,128)S(1)} collective-permute-done((f32[8,16,128]{2,1,0:T(8,128)S(1)}, f32[8,16,128]{2,1,0:T(8,128)S(1)}, u32[]{:S(2)}, u32[]{:S(2)}) %collective-permute-start.10) | collective-permute-done | bytes 65568 | tf_op jit(solution)/shard_map/ppermute | solution.py:710
  49.8 0.0 collective-permute-done.9
  49.8 0.1 collective-permute-start.12
  49.9 1.5 %collective-permute-done.12.sibling = f32[4,8,16,128]{3,2,1,0:T(8,128)S(1)} collective-permute-done((f32[4,8,16,128]{3,2,1,0:T(8,128)S(1)}, f32[4,8,16,128]{3,2,1,0:T(8,128)S(1)}, u32[]{:S(2)}, u32[]{:S(2)}) %collective-permute-start.12) | collective-permute-done | bytes 262176 | tf_op jit(solution)/shard_map/ppermute | solution.py:712
  51.4 0.0 copy-done.4
  51.4 0.0 copy-done.5
  51.4 0.0 copy-done.6
  51.4 0.0 copy-done.7
  51.4 0.0 copy-done.8
  51.4 9.9 %backward.1 = (f32[8,32,128]{2,1,0:T(8,128)S(1)}, f32[32,128]{1,0:T(8,128)S(1)}) custom-call(f32[4,8,16,128]{3,2,1,0:T(8,128)S(1)} %pad_maximum_fusion.own, f32[4,8,16,128]{3,2,1,0:T(8,128)S(1)} %collective-permute-done.12.sibling, f32[8,64,64]{2,1,0:T(8,128)S(1)} %copy-done.6, f32[2,4,8,128]{3,2,1,0:T(8,128)S(1)} %copy-done.8, ...), custom_call_target="tpu_custom_call" | custom-call | tf_op jit(solution)/shard_map/backward/pallas_call | solution.py:720
  61.4 10.7 %all_to_all.11 = f32[32,1,128]{2,1,0:T(1,128)S(1)} all-to-all(f32[32,1,128]{2,1,0:T(1,128)S(1)} %bitcast.13), channel_id=1, replica_groups=mesh['gx'=8,'gy'=4] {'gx','gy'}, dimensions={0} | all-to-all | bytes 32768 | tf_op jit(solution)/shard_map/all_to_all | solution.py:746
  72.1 0.8 %scale.1 = f32[8,32,128]{2,1,0:T(8,128)} custom-call(f32[32,128]{1,0:T(8,128)S(1)} %bitcast.12, f32[8,32,128]{2,1,0:T(8,128)S(1)} %get-tuple-element.22.gradient), custom_call_target="tpu_custom_call" | custom-call | tf_op jit(solution)/shard_map/scale/pallas_call | solution.py:748
  (3 shorter events, 0.0 us)
Async XLA Ops:
  0.0 17.2 %copy-start = (bf16[3,8,128,256]{3,2,1,0:T(8,128)(2,1)S(1)}, bf16[3,8,128,256]{3,2,1,0:T(8,128)(2,1)}, u32[]{:S(2)}) copy-start(bf16[3,8,128,256]{3,2,1,0:T(8,128)(2,1)} %constant.10.clone.table.table_in) | copy-start | bytes 4718596
  0.0 1.1 %copy-start.1 = (f32[3,8,32,128]{3,2,1,0:T(8,128)S(1)}, f32[3,8,32,128]{3,2,1,0:T(8,128)}, u32[]{:S(2)}) copy-start(f32[3,8,32,128]{3,2,1,0:T(8,128)} %e.5) | copy-start | bytes 1179652
  1.1 1.0 %copy-start.2 = (f32[3,8,32,128]{3,2,1,0:T(8,128)S(1)}, f32[3,8,32,128]{3,2,1,0:T(8,128)}, u32[]{:S(2)}) copy-start(f32[3,8,32,128]{3,2,1,0:T(8,128)} %h.5) | copy-start | bytes 1179652
  2.1 0.9 %copy-start.3 = (s32[8,32,128]{2,1,0:T(8,128)S(1)}, s32[8,32,128]{2,1,0:T(8,128)}, u32[]{:S(2)}) copy-start(s32[8,32,128]{2,1,0:T(8,128)} %material.5) | copy-start | bytes 393220
  4.0 13.2 %collective-permute-start = (f32[7,6,32,128]{3,2,1,0:T(8,128)S(1)}, f32[7,6,32,128]{3,2,1,0:T(8,128)S(1)}, u32[]{:S(2)}, u32[]{:S(2)}) collective-permute-start(f32[7,6,32,128]{3,2,1,0:T(8,128)S(1)} %get-tuple-element.14), channel_id=1, source_target_pairs={{0,4},{4,0},{8,12},{12,8},{16,20},{20,16},{24,28},{28,24},{1,5},{5... | collective-permute-start | bytes 2064392 | tf_op jit(solution)/shard_map/ppermute | solution.py:665
  4.5 12.7 %collective-permute-start.1 = (f32[7,6,32,128]{3,2,1,0:T(8,128)S(1)}, f32[7,6,32,128]{3,2,1,0:T(8,128)S(1)}, u32[]{:S(2)}, u32[]{:S(2)}) collective-permute-start(f32[7,6,32,128]{3,2,1,0:T(8,128)S(1)} %get-tuple-element.15), channel_id=1, source_target_pairs={{4,8},{8,4},{12,16},{16,12},{20,24},{24,20},{5,9},{9,5},{13,17},{1... | collective-permute-start | bytes 2064392 | tf_op jit(solution)/shard_map/ppermute | solution.py:664
  5.7 4.8 %collective-permute-start.2 = (f32[4,32,128]{2,1,0:T(8,128)S(1)}, f32[4,32,128]{2,1,0:T(8,128)S(1)}, u32[]{:S(2)}, u32[]{:S(2)}) collective-permute-start(f32[4,32,128]{2,1,0:T(8,128)S(1)} %get-tuple-element.16), channel_id=1, source_target_pairs={{0,1},{1,0},{2,3},{3,2},{4,5},{5,4},{6,7},{7,6},{8,9},{9,8},{10,11... | collective-permute-start | bytes 196616 | tf_op jit(solution)/shard_map/ppermute | solution.py:670
  8.3 2.2 %collective-permute-start.3 = (f32[4,32,128]{2,1,0:T(8,128)S(1)}, f32[4,32,128]{2,1,0:T(8,128)S(1)}, u32[]{:S(2)}, u32[]{:S(2)}) collective-permute-start(f32[4,32,128]{2,1,0:T(8,128)S(1)} %get-tuple-element.17), channel_id=1, source_target_pairs={{1,2},{2,1},{5,6},{6,5},{9,10},{10,9},{13,14},{14,13},{17,18},{18,... | collective-permute-start | bytes 196616 | tf_op jit(solution)/shard_map/ppermute | solution.py:669
  10.5 40.9 %copy-start.4 = (f32[8,2,80,64]{3,2,1,0:T(8,128)S(1)}, f32[8,2,80,64]{3,2,1,0:T(8,128)}, u32[]{:S(2)}) copy-start(f32[8,2,80,64]{3,2,1,0:T(8,128)} %constant.14.clone.rows_back_in) | copy-start | bytes 983044
  10.6 40.9 %copy-start.5 = (bf16[8,128,192]{2,1,0:T(8,128)(2,1)S(1)}, bf16[8,128,192]{2,1,0:T(8,128)(2,1)}, u32[]{:S(2)}) copy-start(bf16[8,128,192]{2,1,0:T(8,128)(2,1)} %constant.13.clone.rows_far) | copy-start | bytes 1179652
  10.6 40.9 %copy-start.6 = (f32[8,64,64]{2,1,0:T(8,128)S(1)}, f32[8,64,64]{2,1,0:T(8,128)}, u32[]{:S(2)}) copy-start(f32[8,64,64]{2,1,0:T(8,128)} %target.1) | copy-start | bytes 393220
  10.6 40.8 %copy-start.7 = (bf16[192,48]{1,0:T(8,128)(2,1)S(1)}, bf16[192,48]{1,0:T(8,128)(2,1)}, u32[]{:S(2)}) copy-start(bf16[192,48]{1,0:T(8,128)(2,1)} %constant.12.clone.weights) | copy-start | bytes 55300
  10.6 40.8 %copy-start.8 = (f32[2,4,8,128]{3,2,1,0:T(8,128)S(1)}, f32[2,4,8,128]{3,2,1,0:T(8,128)}, u32[]{:S(2)}) copy-start(f32[2,4,8,128]{3,2,1,0:T(8,128)} %constant.11.clone.twist) | copy-start | bytes 98308
  10.6 5.6 %collective-permute-start.5 = (f32[2,4,32,128]{3,2,1,0:T(8,128)S(1)}, f32[2,4,32,128]{3,2,1,0:T(8,128)S(1)}, u32[]{:S(2)}, u32[]{:S(2)}) collective-permute-start(f32[2,4,32,128]{3,2,1,0:T(8,128)S(1)} %pad_maximum_fusion.1), channel_id=1, source_target_pairs={{4,8},{8,4},{12,16},{16,12},{20,24},{24,20},{5,9},{9,5},{13,17},{1... | collective-permute-start | bytes 393224 | tf_op jit(solution)/shard_map/ppermute | solution.py:672
  11.4 5.8 %collective-permute-start.4 = (f32[2,4,32,128]{3,2,1,0:T(8,128)S(1)}, f32[2,4,32,128]{3,2,1,0:T(8,128)S(1)}, u32[]{:S(2)}, u32[]{:S(2)}) collective-permute-start(f32[2,4,32,128]{3,2,1,0:T(8,128)S(1)} %pad_maximum_fusion.1), channel_id=1, source_target_pairs={{0,4},{4,0},{8,12},{12,8},{16,20},{20,16},{24,28},{28,24},{1,5},{5... | collective-permute-start | bytes 393224 | tf_op jit(solution)/shard_map/ppermute | solution.py:673
  17.2 0.7 copy-start.9
  27.7 8.4 %collective-permute-start.8 = (f32[8,16,128]{2,1,0:T(8,128)S(1)}, f32[8,16,128]{2,1,0:T(8,128)S(1)}, u32[]{:S(2)}, u32[]{:S(2)}) collective-permute-start(f32[8,16,128]{2,1,0:T(8,128)S(1)} %get-tuple-element.18), channel_id=1, source_target_pairs={{0,3},{1,2},{2,1},{3,0},{4,7},{5,6},{6,5},{7,4},{8,11},{9,10},{10,... | collective-permute-start | bytes 196616 | tf_op jit(solution)/shard_map/ppermute | solution.py:707
  31.2 5.8 %collective-permute-start.7 = (f32[8,16,128]{2,1,0:T(8,128)S(1)}, f32[8,16,128]{2,1,0:T(8,128)S(1)}, u32[]{:S(2)}, u32[]{:S(2)}) collective-permute-start(f32[8,16,128]{2,1,0:T(8,128)S(1)} %get-tuple-element.18), channel_id=1, source_target_pairs={{0,2},{1,3},{2,0},{3,1},{4,6},{5,7},{6,4},{7,5},{8,10},{9,11},{10,... | collective-permute-start | bytes 196616 | tf_op jit(solution)/shard_map/ppermute | solution.py:707
  34.7 5.2 %collective-permute-start.6 = (f32[8,16,128]{2,1,0:T(8,128)S(1)}, f32[8,16,128]{2,1,0:T(8,128)S(1)}, u32[]{:S(2)}, u32[]{:S(2)}) collective-permute-start(f32[8,16,128]{2,1,0:T(8,128)S(1)} %get-tuple-element.18), channel_id=1, source_target_pairs={{0,1},{1,0},{2,3},{3,2},{4,5},{5,4},{6,7},{7,6},{8,9},{9,8},{10,11... | collective-permute-start | bytes 196616 | tf_op jit(solution)/shard_map/ppermute | solution.py:707
  39.9 6.8 %collective-permute-start.11 = (f32[8,16,128]{2,1,0:T(8,128)S(1)}, f32[8,16,128]{2,1,0:T(8,128)S(1)}, u32[]{:S(2)}, u32[]{:S(2)}) collective-permute-start(f32[8,16,128]{2,1,0:T(8,128)S(1)} %add_add_fusion), channel_id=1, source_target_pairs={{0,24},{4,28},{8,16},{12,20},{16,8},{20,12},{24,0},{28,4},{1,25},{... | collective-permute-start | bytes 196616 | tf_op jit(solution)/shard_map/ppermute | solution.py:710
  44.1 5.7 %collective-permute-start.10 = (f32[8,16,128]{2,1,0:T(8,128)S(1)}, f32[8,16,128]{2,1,0:T(8,128)S(1)}, u32[]{:S(2)}, u32[]{:S(2)}) collective-permute-start(f32[8,16,128]{2,1,0:T(8,128)S(1)} %add_add_fusion), channel_id=1, source_target_pairs={{0,16},{4,20},{8,24},{12,28},{16,0},{20,4},{24,8},{28,12},{1,17},{... | collective-permute-start | bytes 196616 | tf_op jit(solution)/shard_map/ppermute | solution.py:710
  44.4 5.4 %collective-permute-start.9 = (f32[8,16,128]{2,1,0:T(8,128)S(1)}, f32[8,16,128]{2,1,0:T(8,128)S(1)}, u32[]{:S(2)}, u32[]{:S(2)}) collective-permute-start(f32[8,16,128]{2,1,0:T(8,128)S(1)} %add_add_fusion), channel_id=1, source_target_pairs={{0,8},{4,12},{8,0},{12,4},{16,24},{20,28},{24,16},{28,20},{1,9},{5... | collective-permute-start | bytes 196616 | tf_op jit(solution)/shard_map/ppermute | solution.py:710
  49.8 1.6 %collective-permute-start.12 = (f32[4,8,16,128]{3,2,1,0:T(8,128)S(1)}, f32[4,8,16,128]{3,2,1,0:T(8,128)S(1)}, u32[]{:S(2)}, u32[]{:S(2)}) collective-permute-start(f32[4,8,16,128]{3,2,1,0:T(8,128)S(1)} %pad_maximum_fusion.own), channel_id=1, source_target_pairs={{0,4},{4,0},{8,12},{12,8},{16,20},{20,16},{24,28},{28,24},{1,5},{5... | collective-permute-start | bytes 786440 | tf_op jit(solution)/shard_map/ppermute | solution.py:712

commit v4 on v3

--- a/solution.py
+++ b/solution.py
@@ -301,7 +301,7 @@
     clear_pads(magnetic)
     weights = lens_weights(depth)
     twist = tile_twist(j)
-    for copy in started[:early]:
+    for copy in started[1:5]:
         copy.wait()
 
     lane = lax.broadcasted_iota(jnp.int32, (depth, tile_cols), 1)
@@ -313,7 +313,6 @@
         shift = shift % tile_cols
         return pltpu.roll(value, shift, 1) if shift else value
 
-    inverse[GHOST:far_edge, 0] = index[...].astype(F32)
     for part in range(7):
         for base, block, skip, rows in (
             (GHOST, 0, 0, tile_rows),
@@ -331,6 +330,9 @@
                 else:
                     inverse[base + x, 1] = value
 
+    for copy in started[:1] + started[5:early]:
+        copy.wait()
+    inverse[GHOST:far_edge, 0] = index[...].astype(F32)
     mask = ghost_mask(tile_cols, j, count_cols)
 
     def masked(row):
@@ -468,10 +470,11 @@
         return jnp.concatenate([target[f], target[f]], axis=1)
 
     power = jnp.sum(total, keepdims=True) / (2.0 * samples)
+    over = 1.0 / power
     total = jnp.zeros((FAR, wide), F32)
     for f in range(NF):
         level = intensity[f]
-        total = total + (level / power - wanted(f)) * level
+        total = total + (level * over - wanted(f)) * level
     spread = jnp.sum(total, keepdims=True) / (2.0 * samples * power)
 
     for copy in started[first:second]:
@@ -484,32 +487,40 @@
     highest = jnp.where(i < count_rows - 1, span, BACK + tile_rows)
     inside = jnp.where((row >= lowest) & (row < highest), 1.0, 0.0)
     waves = 2 * NF
+    gradients = []
     for f in range(NF):
-        slope = 2.0 / power * (intensity[f] / power - wanted(f) - spread)
-        slope = 2.0 * slope
-        high, low = split(far[f] * jnp.concatenate([slope, slope], axis=1))
-        start = pl.multiple_of(i * tile_rows, 8)
+        slope = 2.0 * ((2.0 * over) * (intensity[f] * over - wanted(f) - spread))
+        gradients.append(split(far[f] * jnp.concatenate([slope, slope], axis=1)))
+    start = pl.multiple_of(i * tile_rows, 8)
+    crossed = []
+    for f in range(NF):
+        high, low = gradients[f]
         phases = jnp.concatenate(
             [rows_back[f, 0, pl.ds(start, span), :], rows_back[f, 1, pl.ds(start, span), :]], axis=0
         )
         phase_high, phase_low = split(phases)
-        both = dot(phase_high, high) + dot(phase_high, low) + dot(phase_low, high)
+        crossed.append(dot(phase_high, high) + dot(phase_high, low) + dot(phase_low, high))
+    lefts = []
+    for f in range(NF):
         turned = []
         for p in range(2):
-            cos = both[:span, p * wide : (p + 1) * wide]
-            sin = both[span:, p * wide : (p + 1) * wide]
+            cos = crossed[f][:span, p * wide : (p + 1) * wide]
+            sin = crossed[f][span:, p * wide : (p + 1) * wide]
             value = cos - sign * half_turn(sin)
             turned.append(value * twist[0, j, f : f + 1, :] - half_turn(value) * twist[1, j, f : f + 1, :])
-        high, low = split(jnp.concatenate(turned, axis=0))
-        left = jnp.concatenate(
-            [jnp.concatenate([high, high], axis=1), jnp.concatenate([low, low], axis=1)], axis=0
+        high, low = split(jnp.concatenate(turned, axis=0) * inside)
+        lefts.append(
+            jnp.concatenate(
+                [jnp.concatenate([high, high], axis=1), jnp.concatenate([low, low], axis=1)], axis=0
+            )
         )
-        both = dot(left, table[f])
-        both = (both[: 2 * span] + both[2 * span :]) * inside
+    for f in range(NF):
+        both = dot(lefts[f], table[f])
+        both = both[: 2 * span] + both[2 * span :]
         for part in range(2):
             for s in range(2):
-                start = part * width + s * tile_cols
-                value = both[:, start : start + tile_cols]
+                begin = part * width + s * tile_cols
+                value = both[:, begin : begin + tile_cols]
                 value = value * mask if s else value
                 for p in range(2):
                     back[2 * p + s, pl.ds(part * NF + f, span, stride=waves), :] = value[p * span : (p + 1) * span]

time: 73.1 us -> 71.4 us (0.977)
  Pallas kernels: 22 us -> 20.3 us
    pallas_call x1, Pallas kernels: 9.91 us -> 8.35 us  [body(): call(functools.partial(backward_kernel, counts), 'backward', [ANY] * 2 +...]
where the time goes in v4:
time: 71.4 us; the launch traced here: 71.2 us
  starting transfers between devices  23.4 us (33%)
  Pallas kernels  20.3 us (28%)
  waiting for transfers between devices  12.9 us (18%)
  blocking collectives  10.8 us (15%)
  local copies, waits for them, and re-layouts  3.7 us (5%)
    all_to_all x1, blocking collectives, body(): squares = lax.all_to_all(squares, ('gx', 'gy'), 0, 0, tiled=True)  10.8 us
    pallas_call x1, Pallas kernels, body(): call(functools.partial(forward_kernel, counts), 'forward', [HBM] * 6 + [A...  9.67 us
    ppermute x3, starting transfers between devices, body(): lax.ppermute(mid, 'gy', [(n, n ^ k) for n in range(count_cols)])  8.4 us
    pallas_call x1, Pallas kernels, body(): call(functools.partial(backward_kernel, counts), 'backward', [ANY] * 2 +...  8.35 us
    ppermute x3, waiting for transfers between devices, body(): lax.ppermute(whole, 'gx', [(n, n ^ k) for n in range(count_rows)])  5.03 us
    ppermute x3, starting transfers between devices, body(): lax.ppermute(whole, 'gx', [(n, n ^ k) for n in range(count_rows)])  4.85 us
    ppermute x1, starting transfers between devices, body(): corner_a = lax.ppermute(corner, 'gx', rows_a)  4.79 us
    ppermute x3, waiting for transfers between devices, body(): lax.ppermute(mid, 'gy', [(n, n ^ k) for n in range(count_cols)])  3.77 us
  transfers between devices with their start and end apart: 13, of which 7 were waited for; matrix products, arithmetic and copies ran while one was open for 0% of the time, Pallas kernels for 1%

profile of v4, /device:TPU:0, one launch (start us, length us, event | category | flops | bytes accessed | tf_op | source)
XLA Modules:
  0.0 71.2 jit_solution(8865240167802687332)
XLA Ops:
  0.0 0.0 copy-start
  0.0 0.0 copy-start.1
  0.0 1.1 %copy-done.1 = f32[3,8,32,128]{3,2,1,0:T(8,128)S(1)} copy-done((f32[3,8,32,128]{3,2,1,0:T(8,128)S(1)}, f32[3,8,32,128]{3,2,1,0:T(8,128)}, u32[]{:S(2)}) %copy-start.1) | copy-done | bytes 393240
  1.1 0.0 copy-start.2
  1.1 1.0 %copy-done.2 = f32[3,8,32,128]{3,2,1,0:T(8,128)S(1)} copy-done((f32[3,8,32,128]{3,2,1,0:T(8,128)S(1)}, f32[3,8,32,128]{3,2,1,0:T(8,128)}, u32[]{:S(2)}) %copy-start.2) | copy-done | bytes 393240
  2.1 0.0 copy-start.3
  2.1 0.9 %copy-done.3 = s32[8,32,128]{2,1,0:T(8,128)S(1)} copy-done((s32[8,32,128]{2,1,0:T(8,128)S(1)}, s32[8,32,128]{2,1,0:T(8,128)}, u32[]{:S(2)}) %copy-start.3) | copy-done | bytes 131096
  3.0 0.9 %pack_rows.1 = (f32[7,6,32,128]{3,2,1,0:T(8,128)S(1)}, f32[7,6,32,128]{3,2,1,0:T(8,128)S(1)}) custom-call(f32[3,8,32,128]{3,2,1,0:T(8,128)S(1)} %copy-done.1, f32[3,8,32,128]{3,2,1,0:T(8,128)S(1)} %copy-done.2, s32[8,32,128]{2,1,0:T(8,128)S(1)} %copy-done.3), custom_call_target="tpu_custom_call" | custom-call | tf_op jit(solution)/shard_map/pack_rows/pallas_call | solution.py:660
  4.0 0.5 collective-permute-start
  4.5 0.7 collective-permute-start.1
  5.2 0.5 pack_columns.1
  5.7 2.6 %collective-permute-start.2 = (f32[4,32,128]{2,1,0:T(8,128)S(1)}, f32[4,32,128]{2,1,0:T(8,128)S(1)}, u32[]{:S(2)}, u32[]{:S(2)}) collective-permute-start(f32[4,32,128]{2,1,0:T(8,128)S(1)} %get-tuple-element.16), channel_id=1, source_target_pairs={{0,1},{1,0},{2,3},{3,2},{4,5},{5,4},{6,7},{7,6},{8,9},{9,8},{10,11... | collective-permute-start | bytes 196616 | tf_op jit(solution)/shard_map/ppermute | solution.py:681
  8.3 0.7 collective-permute-start.3
  8.9 1.6 %collective-permute-done.2.own_a = f32[4,32,128]{2,1,0:T(8,128)S(1)} collective-permute-done((f32[4,32,128]{2,1,0:T(8,128)S(1)}, f32[4,32,128]{2,1,0:T(8,128)S(1)}, u32[]{:S(2)}, u32[]{:S(2)}) %collective-permute-start.2) | collective-permute-done | bytes 65568 | tf_op jit(solution)/shard_map/ppermute | solution.py:681
  10.5 0.0 collective-permute-done.3.own_b
  10.5 0.0 copy-start.4
  10.6 0.0 copy-start.5
  10.6 0.0 copy-start.6
  10.6 0.0 copy-start.7
  10.6 0.0 copy-start.8
  10.6 0.8 %collective-permute-start.5 = (f32[2,4,32,128]{3,2,1,0:T(8,128)S(1)}, f32[2,4,32,128]{3,2,1,0:T(8,128)S(1)}, u32[]{:S(2)}, u32[]{:S(2)}) collective-permute-start(f32[2,4,32,128]{3,2,1,0:T(8,128)S(1)} %pad_maximum_fusion.1), channel_id=1, source_target_pairs={{4,8},{8,4},{12,16},{16,12},{20,24},{24,20},{5,9},{9,5},{13,17},{1... | collective-permute-start | bytes 393224 | tf_op jit(solution)/shard_map/ppermute | solution.py:683
  11.4 4.8 %collective-permute-start.4 = (f32[2,4,32,128]{3,2,1,0:T(8,128)S(1)}, f32[2,4,32,128]{3,2,1,0:T(8,128)S(1)}, u32[]{:S(2)}, u32[]{:S(2)}) collective-permute-start(f32[2,4,32,128]{3,2,1,0:T(8,128)S(1)} %pad_maximum_fusion.1), channel_id=1, source_target_pairs={{0,4},{4,0},{8,12},{12,8},{16,20},{20,16},{24,28},{28,24},{1,5},{5... | collective-permute-start | bytes 393224 | tf_op jit(solution)/shard_map/ppermute | solution.py:684
  16.2 0.0 collective-permute-done.5.corner_b
  16.2 1.0 %collective-permute-done.4.corner_a = f32[2,4,32,128]{3,2,1,0:T(8,128)S(1)} collective-permute-done((f32[2,4,32,128]{3,2,1,0:T(8,128)S(1)}, f32[2,4,32,128]{3,2,1,0:T(8,128)S(1)}, u32[]{:S(2)}, u32[]{:S(2)}) %collective-permute-start.4) | collective-permute-done | bytes 131104 | tf_op jit(solution)/shard_map/ppermute | solution.py:684
  17.2 0.0 collective-permute-done.row_a
  17.2 0.0 collective-permute-done.1.row_b
  17.2 0.0 copy-done
  17.2 0.0 copy-start.9
  17.2 0.6 copy-done.9
  17.9 9.7 %forward.1 = (f32[6,3,8,32,128]{4,3,2,1,0:T(8,128)S(1)}, f32[20,2,32,128]{3,2,1,0:T(8,128)S(1)}, f32[8,16,128]{2,1,0:T(8,128)S(1)}) custom-call(f32[8]{0:T(128)S(1)} %copy-done.9, f32[3,8,32,128]{3,2,1,0:T(8,128)S(1)} %copy-done.1, f32[3,8,32,128]{3,2,1,0:T(8,128)S(1)} %copy-done.2, s32[8,32,128]{2,1,0:T(8,128)S(1)} %copy-done.3, ...), custom_call_target="tpu_custom_call" | custom-call | tf_op jit(solution)/shard_map/forward/pallas_call | solution.py:692
  27.5 3.5 %collective-permute-start.8 = (f32[8,16,128]{2,1,0:T(8,128)S(1)}, f32[8,16,128]{2,1,0:T(8,128)S(1)}, u32[]{:S(2)}, u32[]{:S(2)}) collective-permute-start(f32[8,16,128]{2,1,0:T(8,128)S(1)} %get-tuple-element.18), channel_id=1, source_target_pairs={{0,3},{1,2},{2,1},{3,0},{4,7},{5,6},{6,5},{7,4},{8,11},{9,10},{10,... | collective-permute-start | bytes 196616 | tf_op jit(solution)/shard_map/ppermute | solution.py:718
  31.0 3.5 %collective-permute-start.7 = (f32[8,16,128]{2,1,0:T(8,128)S(1)}, f32[8,16,128]{2,1,0:T(8,128)S(1)}, u32[]{:S(2)}, u32[]{:S(2)}) collective-permute-start(f32[8,16,128]{2,1,0:T(8,128)S(1)} %get-tuple-element.18), channel_id=1, source_target_pairs={{0,2},{1,3},{2,0},{3,1},{4,6},{5,7},{6,4},{7,5},{8,10},{9,11},{10,... | collective-permute-start | bytes 196616 | tf_op jit(solution)/shard_map/ppermute | solution.py:718
  34.6 1.4 %collective-permute-start.6 = (f32[8,16,128]{2,1,0:T(8,128)S(1)}, f32[8,16,128]{2,1,0:T(8,128)S(1)}, u32[]{:S(2)}, u32[]{:S(2)}) collective-permute-start(f32[8,16,128]{2,1,0:T(8,128)S(1)} %get-tuple-element.18), channel_id=1, source_target_pairs={{0,1},{1,0},{2,3},{3,2},{4,5},{5,4},{6,7},{7,6},{8,9},{9,8},{10,11... | collective-permute-start | bytes 196616 | tf_op jit(solution)/shard_map/ppermute | solution.py:718
  35.9 0.0 collective-permute-done.8
  35.9 0.9 %collective-permute-done.7 = f32[8,16,128]{2,1,0:T(8,128)S(1)} collective-permute-done((f32[8,16,128]{2,1,0:T(8,128)S(1)}, f32[8,16,128]{2,1,0:T(8,128)S(1)}, u32[]{:S(2)}, u32[]{:S(2)}) %collective-permute-start.7) | collective-permute-done | bytes 65568 | tf_op jit(solution)/shard_map/ppermute | solution.py:718
  36.8 2.9 %collective-permute-done.6 = f32[8,16,128]{2,1,0:T(8,128)S(1)} collective-permute-done((f32[8,16,128]{2,1,0:T(8,128)S(1)}, f32[8,16,128]{2,1,0:T(8,128)S(1)}, u32[]{:S(2)}, u32[]{:S(2)}) %collective-permute-start.6) | collective-permute-done | bytes 65568 | tf_op jit(solution)/shard_map/ppermute | solution.py:718
  39.7 4.2 %collective-permute-start.11 = (f32[8,16,128]{2,1,0:T(8,128)S(1)}, f32[8,16,128]{2,1,0:T(8,128)S(1)}, u32[]{:S(2)}, u32[]{:S(2)}) collective-permute-start(f32[8,16,128]{2,1,0:T(8,128)S(1)} %add_add_fusion), channel_id=1, source_target_pairs={{0,24},{4,28},{8,16},{12,20},{16,8},{20,12},{24,0},{28,4},{1,25},{... | collective-permute-start | bytes 196616 | tf_op jit(solution)/shard_map/ppermute | solution.py:721
  43.9 0.3 collective-permute-start.10
  44.2 0.4 collective-permute-start.9
  44.6 1.9 %collective-permute-done.11 = f32[8,16,128]{2,1,0:T(8,128)S(1)} collective-permute-done((f32[8,16,128]{2,1,0:T(8,128)S(1)}, f32[8,16,128]{2,1,0:T(8,128)S(1)}, u32[]{:S(2)}, u32[]{:S(2)}) %collective-permute-start.11) | collective-permute-done | bytes 65568 | tf_op jit(solution)/shard_map/ppermute | solution.py:721
  46.5 3.1 %collective-permute-done.10 = f32[8,16,128]{2,1,0:T(8,128)S(1)} collective-permute-done((f32[8,16,128]{2,1,0:T(8,128)S(1)}, f32[8,16,128]{2,1,0:T(8,128)S(1)}, u32[]{:S(2)}, u32[]{:S(2)}) %collective-permute-start.10) | collective-permute-done | bytes 65568 | tf_op jit(solution)/shard_map/ppermute | solution.py:721
  49.6 0.0 collective-permute-done.9
  49.6 0.1 collective-permute-start.12
  49.7 1.5 %collective-permute-done.12.sibling = f32[4,8,16,128]{3,2,1,0:T(8,128)S(1)} collective-permute-done((f32[4,8,16,128]{3,2,1,0:T(8,128)S(1)}, f32[4,8,16,128]{3,2,1,0:T(8,128)S(1)}, u32[]{:S(2)}, u32[]{:S(2)}) %collective-permute-start.12) | collective-permute-done | bytes 262176 | tf_op jit(solution)/shard_map/ppermute | solution.py:723
  51.2 0.0 copy-done.4
  51.2 0.0 copy-done.5
  51.2 0.0 copy-done.6
  51.2 0.0 copy-done.7
  51.3 0.0 copy-done.8
  51.3 8.3 %backward.1 = (f32[8,32,128]{2,1,0:T(8,128)S(1)}, f32[32,128]{1,0:T(8,128)S(1)}) custom-call(f32[4,8,16,128]{3,2,1,0:T(8,128)S(1)} %pad_maximum_fusion.own, f32[4,8,16,128]{3,2,1,0:T(8,128)S(1)} %collective-permute-done.12.sibling, f32[8,64,64]{2,1,0:T(8,128)S(1)} %copy-done.6, f32[2,4,8,128]{3,2,1,0:T(8,128)S(1)} %copy-done.8, ...), custom_call_target="tpu_custom_call" | custom-call | tf_op jit(solution)/shard_map/backward/pallas_call | solution.py:731
  59.6 10.8 %all_to_all.11 = f32[32,1,128]{2,1,0:T(1,128)S(1)} all-to-all(f32[32,1,128]{2,1,0:T(1,128)S(1)} %bitcast.13), channel_id=1, replica_groups=mesh['gx'=8,'gy'=4] {'gx','gy'}, dimensions={0} | all-to-all | bytes 32768 | tf_op jit(solution)/shard_map/all_to_all | solution.py:757
  70.4 0.8 %scale.1 = f32[8,32,128]{2,1,0:T(8,128)} custom-call(f32[32,128]{1,0:T(8,128)S(1)} %bitcast.12, f32[8,32,128]{2,1,0:T(8,128)S(1)} %get-tuple-element.22.gradient), custom_call_target="tpu_custom_call" | custom-call | tf_op jit(solution)/shard_map/scale/pallas_call | solution.py:759
  (3 shorter events, 0.0 us)
Async XLA Ops:
  0.0 17.2 %copy-start = (bf16[3,8,128,256]{3,2,1,0:T(8,128)(2,1)S(1)}, bf16[3,8,128,256]{3,2,1,0:T(8,128)(2,1)}, u32[]{:S(2)}) copy-start(bf16[3,8,128,256]{3,2,1,0:T(8,128)(2,1)} %constant.10.clone.table.table_in) | copy-start | bytes 4718596
  0.0 1.1 %copy-start.1 = (f32[3,8,32,128]{3,2,1,0:T(8,128)S(1)}, f32[3,8,32,128]{3,2,1,0:T(8,128)}, u32[]{:S(2)}) copy-start(f32[3,8,32,128]{3,2,1,0:T(8,128)} %e.5) | copy-start | bytes 1179652
  1.1 1.0 %copy-start.2 = (f32[3,8,32,128]{3,2,1,0:T(8,128)S(1)}, f32[3,8,32,128]{3,2,1,0:T(8,128)}, u32[]{:S(2)}) copy-start(f32[3,8,32,128]{3,2,1,0:T(8,128)} %h.5) | copy-start | bytes 1179652
  2.1 0.9 %copy-start.3 = (s32[8,32,128]{2,1,0:T(8,128)S(1)}, s32[8,32,128]{2,1,0:T(8,128)}, u32[]{:S(2)}) copy-start(s32[8,32,128]{2,1,0:T(8,128)} %material.5) | copy-start | bytes 393220
  4.0 13.2 %collective-permute-start = (f32[7,6,32,128]{3,2,1,0:T(8,128)S(1)}, f32[7,6,32,128]{3,2,1,0:T(8,128)S(1)}, u32[]{:S(2)}, u32[]{:S(2)}) collective-permute-start(f32[7,6,32,128]{3,2,1,0:T(8,128)S(1)} %get-tuple-element.14), channel_id=1, source_target_pairs={{0,4},{4,0},{8,12},{12,8},{16,20},{20,16},{24,28},{28,24},{1,5},{5... | collective-permute-start | bytes 2064392 | tf_op jit(solution)/shard_map/ppermute | solution.py:676
  4.5 12.7 %collective-permute-start.1 = (f32[7,6,32,128]{3,2,1,0:T(8,128)S(1)}, f32[7,6,32,128]{3,2,1,0:T(8,128)S(1)}, u32[]{:S(2)}, u32[]{:S(2)}) collective-permute-start(f32[7,6,32,128]{3,2,1,0:T(8,128)S(1)} %get-tuple-element.15), channel_id=1, source_target_pairs={{4,8},{8,4},{12,16},{16,12},{20,24},{24,20},{5,9},{9,5},{13,17},{1... | collective-permute-start | bytes 2064392 | tf_op jit(solution)/shard_map/ppermute | solution.py:675
  5.7 4.8 %collective-permute-start.2 = (f32[4,32,128]{2,1,0:T(8,128)S(1)}, f32[4,32,128]{2,1,0:T(8,128)S(1)}, u32[]{:S(2)}, u32[]{:S(2)}) collective-permute-start(f32[4,32,128]{2,1,0:T(8,128)S(1)} %get-tuple-element.16), channel_id=1, source_target_pairs={{0,1},{1,0},{2,3},{3,2},{4,5},{5,4},{6,7},{7,6},{8,9},{9,8},{10,11... | collective-permute-start | bytes 196616 | tf_op jit(solution)/shard_map/ppermute | solution.py:681
  8.3 2.2 %collective-permute-start.3 = (f32[4,32,128]{2,1,0:T(8,128)S(1)}, f32[4,32,128]{2,1,0:T(8,128)S(1)}, u32[]{:S(2)}, u32[]{:S(2)}) collective-permute-start(f32[4,32,128]{2,1,0:T(8,128)S(1)} %get-tuple-element.17), channel_id=1, source_target_pairs={{1,2},{2,1},{5,6},{6,5},{9,10},{10,9},{13,14},{14,13},{17,18},{18,... | collective-permute-start | bytes 196616 | tf_op jit(solution)/shard_map/ppermute | solution.py:680
  10.5 40.7 %copy-start.4 = (f32[8,2,80,64]{3,2,1,0:T(8,128)S(1)}, f32[8,2,80,64]{3,2,1,0:T(8,128)}, u32[]{:S(2)}) copy-start(f32[8,2,80,64]{3,2,1,0:T(8,128)} %constant.14.clone.rows_back_in) | copy-start | bytes 983044
  10.6 40.7 %copy-start.5 = (bf16[8,128,192]{2,1,0:T(8,128)(2,1)S(1)}, bf16[8,128,192]{2,1,0:T(8,128)(2,1)}, u32[]{:S(2)}) copy-start(bf16[8,128,192]{2,1,0:T(8,128)(2,1)} %constant.13.clone.rows_far) | copy-start | bytes 1179652
  10.6 40.7 %copy-start.6 = (f32[8,64,64]{2,1,0:T(8,128)S(1)}, f32[8,64,64]{2,1,0:T(8,128)}, u32[]{:S(2)}) copy-start(f32[8,64,64]{2,1,0:T(8,128)} %target.1) | copy-start | bytes 393220
  10.6 40.7 %copy-start.7 = (bf16[192,48]{1,0:T(8,128)(2,1)S(1)}, bf16[192,48]{1,0:T(8,128)(2,1)}, u32[]{:S(2)}) copy-start(bf16[192,48]{1,0:T(8,128)(2,1)} %constant.12.clone.weights) | copy-start | bytes 55300
  10.6 40.7 %copy-start.8 = (f32[2,4,8,128]{3,2,1,0:T(8,128)S(1)}, f32[2,4,8,128]{3,2,1,0:T(8,128)}, u32[]{:S(2)}) copy-start(f32[2,4,8,128]{3,2,1,0:T(8,128)} %constant.11.clone.twist) | copy-start | bytes 98308
  10.6 5.6 %collective-permute-start.5 = (f32[2,4,32,128]{3,2,1,0:T(8,128)S(1)}, f32[2,4,32,128]{3,2,1,0:T(8,128)S(1)}, u32[]{:S(2)}, u32[]{:S(2)}) collective-permute-start(f32[2,4,32,128]{3,2,1,0:T(8,128)S(1)} %pad_maximum_fusion.1), channel_id=1, source_target_pairs={{4,8},{8,4},{12,16},{16,12},{20,24},{24,20},{5,9},{9,5},{13,17},{1... | collective-permute-start | bytes 393224 | tf_op jit(solution)/shard_map/ppermute | solution.py:683
  11.4 5.8 %collective-permute-start.4 = (f32[2,4,32,128]{3,2,1,0:T(8,128)S(1)}, f32[2,4,32,128]{3,2,1,0:T(8,128)S(1)}, u32[]{:S(2)}, u32[]{:S(2)}) collective-permute-start(f32[2,4,32,128]{3,2,1,0:T(8,128)S(1)} %pad_maximum_fusion.1), channel_id=1, source_target_pairs={{0,4},{4,0},{8,12},{12,8},{16,20},{20,16},{24,28},{28,24},{1,5},{5... | collective-permute-start | bytes 393224 | tf_op jit(solution)/shard_map/ppermute | solution.py:684
  17.2 0.7 copy-start.9
  27.5 8.4 %collective-permute-start.8 = (f32[8,16,128]{2,1,0:T(8,128)S(1)}, f32[8,16,128]{2,1,0:T(8,128)S(1)}, u32[]{:S(2)}, u32[]{:S(2)}) collective-permute-start(f32[8,16,128]{2,1,0:T(8,128)S(1)} %get-tuple-element.18), channel_id=1, source_target_pairs={{0,3},{1,2},{2,1},{3,0},{4,7},{5,6},{6,5},{7,4},{8,11},{9,10},{10,... | collective-permute-start | bytes 196616 | tf_op jit(solution)/shard_map/ppermute | solution.py:718
  31.0 5.8 %collective-permute-start.7 = (f32[8,16,128]{2,1,0:T(8,128)S(1)}, f32[8,16,128]{2,1,0:T(8,128)S(1)}, u32[]{:S(2)}, u32[]{:S(2)}) collective-permute-start(f32[8,16,128]{2,1,0:T(8,128)S(1)} %get-tuple-element.18), channel_id=1, source_target_pairs={{0,2},{1,3},{2,0},{3,1},{4,6},{5,7},{6,4},{7,5},{8,10},{9,11},{10,... | collective-permute-start | bytes 196616 | tf_op jit(solution)/shard_map/ppermute | solution.py:718
  34.6 5.2 %collective-permute-start.6 = (f32[8,16,128]{2,1,0:T(8,128)S(1)}, f32[8,16,128]{2,1,0:T(8,128)S(1)}, u32[]{:S(2)}, u32[]{:S(2)}) collective-permute-start(f32[8,16,128]{2,1,0:T(8,128)S(1)} %get-tuple-element.18), channel_id=1, source_target_pairs={{0,1},{1,0},{2,3},{3,2},{4,5},{5,4},{6,7},{7,6},{8,9},{9,8},{10,11... | collective-permute-start | bytes 196616 | tf_op jit(solution)/shard_map/ppermute | solution.py:718
  39.7 6.8 %collective-permute-start.11 = (f32[8,16,128]{2,1,0:T(8,128)S(1)}, f32[8,16,128]{2,1,0:T(8,128)S(1)}, u32[]{:S(2)}, u32[]{:S(2)}) collective-permute-start(f32[8,16,128]{2,1,0:T(8,128)S(1)} %add_add_fusion), channel_id=1, source_target_pairs={{0,24},{4,28},{8,16},{12,20},{16,8},{20,12},{24,0},{28,4},{1,25},{... | collective-permute-start | bytes 196616 | tf_op jit(solution)/shard_map/ppermute | solution.py:721
  43.9 5.7 %collective-permute-start.10 = (f32[8,16,128]{2,1,0:T(8,128)S(1)}, f32[8,16,128]{2,1,0:T(8,128)S(1)}, u32[]{:S(2)}, u32[]{:S(2)}) collective-permute-start(f32[8,16,128]{2,1,0:T(8,128)S(1)} %add_add_fusion), channel_id=1, source_target_pairs={{0,16},{4,20},{8,24},{12,28},{16,0},{20,4},{24,8},{28,12},{1,17},{... | collective-permute-start | bytes 196616 | tf_op jit(solution)/shard_map/ppermute | solution.py:721
  44.2 5.4 %collective-permute-start.9 = (f32[8,16,128]{2,1,0:T(8,128)S(1)}, f32[8,16,128]{2,1,0:T(8,128)S(1)}, u32[]{:S(2)}, u32[]{:S(2)}) collective-permute-start(f32[8,16,128]{2,1,0:T(8,128)S(1)} %add_add_fusion), channel_id=1, source_target_pairs={{0,8},{4,12},{8,0},{12,4},{16,24},{20,28},{24,16},{28,20},{1,9},{5... | collective-permute-start | bytes 196616 | tf_op jit(solution)/shard_map/ppermute | solution.py:721
  49.6 1.6 %collective-permute-start.12 = (f32[4,8,16,128]{3,2,1,0:T(8,128)S(1)}, f32[4,8,16,128]{3,2,1,0:T(8,128)S(1)}, u32[]{:S(2)}, u32[]{:S(2)}) collective-permute-start(f32[4,8,16,128]{3,2,1,0:T(8,128)S(1)} %pad_maximum_fusion.own), channel_id=1, source_target_pairs={{0,4},{4,0},{8,12},{12,8},{16,20},{20,16},{24,28},{28,24},{1,5},{5... | collective-permute-start | bytes 786440 | tf_op jit(solution)/shard_map/ppermute | solution.py:723

commit v5 on v4

--- a/solution.py
+++ b/solution.py
@@ -22,7 +22,7 @@
 PAD = 8
 VMEM_BYTES = 40 * 1024 * 1024
 OWN_GROUP = 8
-GROUP = 8
+GROUP = 10
 
 
 def split_table(table):
@@ -193,16 +193,21 @@
         for ref, index, value in stores:
             ref[index] = value
 
-    whole = (high - low) // GROUP
-    if whole:
-
-        def body(k, carry):
-            group(low + GROUP * k, GROUP)
-            return carry
-
-        lax.fori_loop(0, whole, body, 0)
-    if (high - low) % GROUP:
-        group(low + GROUP * whole, (high - low) % GROUP)
+    count = high - low
+    groups = -(-count // GROUP)
+    size, longer = divmod(count, max(groups, 1))
+    start = low
+    for number, rows in ((longer, size + 1), (groups - longer, size)):
+        if number == 1:
+            group(start, rows)
+        elif number:
+
+            def body(k, carry, start=start, rows=rows):
+                group(start + rows * k, rows)
+                return carry
+
+            lax.fori_loop(0, number, body, 0)
+        start += number * rows
 
 
 def copies(pairs, semaphores):

time: 71.4 us -> 71 us (level)
  no operation moved by 1% of the time
where the time goes in v5:
time: 71 us; the launch traced here: 70.8 us
  starting transfers between devices  23.4 us (33%)
  Pallas kernels  19.9 us (28%)
  waiting for transfers between devices  12.9 us (18%)
  blocking collectives  10.7 us (15%)
  local copies, waits for them, and re-layouts  3.7 us (5%)
    all_to_all x1, blocking collectives, body(): squares = lax.all_to_all(squares, ('gx', 'gy'), 0, 0, tiled=True)  10.7 us
    pallas_call x1, Pallas kernels, body(): call(functools.partial(forward_kernel, counts), 'forward', [HBM] * 6 + [A...  9.58 us
    ppermute x3, starting transfers between devices, body(): lax.ppermute(mid, 'gy', [(n, n ^ k) for n in range(count_cols)])  8.4 us
    pallas_call x1, Pallas kernels, body(): call(functools.partial(backward_kernel, counts), 'backward', [ANY] * 2 +...  8.02 us
    ppermute x3, waiting for transfers between devices, body(): lax.ppermute(whole, 'gx', [(n, n ^ k) for n in range(count_rows)])  5.03 us
    ppermute x3, starting transfers between devices, body(): lax.ppermute(whole, 'gx', [(n, n ^ k) for n in range(count_rows)])  4.85 us
    ppermute x1, starting transfers between devices, body(): corner_a = lax.ppermute(corner, 'gx', rows_a)  4.79 us
    ppermute x3, waiting for transfers between devices, body(): lax.ppermute(mid, 'gy', [(n, n ^ k) for n in range(count_cols)])  3.77 us
  transfers between devices with their start and end apart: 13, of which 7 were waited for; matrix products, arithmetic and copies ran while one was open for 0% of the time, Pallas kernels for 1%

profile of v5, /device:TPU:0, one launch (start us, length us, event | category | flops | bytes accessed | tf_op | source)
XLA Modules:
  0.0 70.8 jit_solution(13240897885303565487)
XLA Ops:
  0.0 0.0 copy-start
  0.0 0.0 copy-start.1
  0.0 1.1 %copy-done.1 = f32[3,8,32,128]{3,2,1,0:T(8,128)S(1)} copy-done((f32[3,8,32,128]{3,2,1,0:T(8,128)S(1)}, f32[3,8,32,128]{3,2,1,0:T(8,128)}, u32[]{:S(2)}) %copy-start.1) | copy-done | bytes 393240
  1.1 0.0 copy-start.2
  1.1 1.0 %copy-done.2 = f32[3,8,32,128]{3,2,1,0:T(8,128)S(1)} copy-done((f32[3,8,32,128]{3,2,1,0:T(8,128)S(1)}, f32[3,8,32,128]{3,2,1,0:T(8,128)}, u32[]{:S(2)}) %copy-start.2) | copy-done | bytes 393240
  2.1 0.0 copy-start.3
  2.1 0.9 %copy-done.3 = s32[8,32,128]{2,1,0:T(8,128)S(1)} copy-done((s32[8,32,128]{2,1,0:T(8,128)S(1)}, s32[8,32,128]{2,1,0:T(8,128)}, u32[]{:S(2)}) %copy-start.3) | copy-done | bytes 131096
  3.0 0.9 %pack_rows.1 = (f32[7,6,32,128]{3,2,1,0:T(8,128)S(1)}, f32[7,6,32,128]{3,2,1,0:T(8,128)S(1)}) custom-call(f32[3,8,32,128]{3,2,1,0:T(8,128)S(1)} %copy-done.1, f32[3,8,32,128]{3,2,1,0:T(8,128)S(1)} %copy-done.2, s32[8,32,128]{2,1,0:T(8,128)S(1)} %copy-done.3), custom_call_target="tpu_custom_call" | custom-call | tf_op jit(solution)/shard_map/pack_rows/pallas_call | solution.py:665
  4.0 0.5 collective-permute-start
  4.5 0.7 collective-permute-start.1
  5.2 0.5 pack_columns.1
  5.7 2.6 %collective-permute-start.2 = (f32[4,32,128]{2,1,0:T(8,128)S(1)}, f32[4,32,128]{2,1,0:T(8,128)S(1)}, u32[]{:S(2)}, u32[]{:S(2)}) collective-permute-start(f32[4,32,128]{2,1,0:T(8,128)S(1)} %get-tuple-element.16), channel_id=1, source_target_pairs={{0,1},{1,0},{2,3},{3,2},{4,5},{5,4},{6,7},{7,6},{8,9},{9,8},{10,11... | collective-permute-start | bytes 196616 | tf_op jit(solution)/shard_map/ppermute | solution.py:686
  8.3 0.7 collective-permute-start.3
  8.9 1.6 %collective-permute-done.2.own_a = f32[4,32,128]{2,1,0:T(8,128)S(1)} collective-permute-done((f32[4,32,128]{2,1,0:T(8,128)S(1)}, f32[4,32,128]{2,1,0:T(8,128)S(1)}, u32[]{:S(2)}, u32[]{:S(2)}) %collective-permute-start.2) | collective-permute-done | bytes 65568 | tf_op jit(solution)/shard_map/ppermute | solution.py:686
  10.5 0.0 collective-permute-done.3.own_b
  10.5 0.0 copy-start.4
  10.6 0.0 copy-start.5
  10.6 0.0 copy-start.6
  10.6 0.0 copy-start.7
  10.6 0.0 copy-start.8
  10.6 0.8 %collective-permute-start.5 = (f32[2,4,32,128]{3,2,1,0:T(8,128)S(1)}, f32[2,4,32,128]{3,2,1,0:T(8,128)S(1)}, u32[]{:S(2)}, u32[]{:S(2)}) collective-permute-start(f32[2,4,32,128]{3,2,1,0:T(8,128)S(1)} %pad_maximum_fusion.1), channel_id=1, source_target_pairs={{4,8},{8,4},{12,16},{16,12},{20,24},{24,20},{5,9},{9,5},{13,17},{1... | collective-permute-start | bytes 393224 | tf_op jit(solution)/shard_map/ppermute | solution.py:688
  11.4 4.8 %collective-permute-start.4 = (f32[2,4,32,128]{3,2,1,0:T(8,128)S(1)}, f32[2,4,32,128]{3,2,1,0:T(8,128)S(1)}, u32[]{:S(2)}, u32[]{:S(2)}) collective-permute-start(f32[2,4,32,128]{3,2,1,0:T(8,128)S(1)} %pad_maximum_fusion.1), channel_id=1, source_target_pairs={{0,4},{4,0},{8,12},{12,8},{16,20},{20,16},{24,28},{28,24},{1,5},{5... | collective-permute-start | bytes 393224 | tf_op jit(solution)/shard_map/ppermute | solution.py:689
  16.2 0.0 collective-permute-done.5.corner_b
  16.2 1.0 %collective-permute-done.4.corner_a = f32[2,4,32,128]{3,2,1,0:T(8,128)S(1)} collective-permute-done((f32[2,4,32,128]{3,2,1,0:T(8,128)S(1)}, f32[2,4,32,128]{3,2,1,0:T(8,128)S(1)}, u32[]{:S(2)}, u32[]{:S(2)}) %collective-permute-start.4) | collective-permute-done | bytes 131104 | tf_op jit(solution)/shard_map/ppermute | solution.py:689
  17.2 0.0 collective-permute-done.row_a
  17.2 0.0 collective-permute-done.1.row_b
  17.2 0.0 copy-done
  17.2 0.0 copy-start.9
  17.2 0.6 copy-done.9
  17.9 9.6 %forward.1 = (f32[6,3,8,32,128]{4,3,2,1,0:T(8,128)S(1)}, f32[20,2,32,128]{3,2,1,0:T(8,128)S(1)}, f32[8,16,128]{2,1,0:T(8,128)S(1)}) custom-call(f32[8]{0:T(128)S(1)} %copy-done.9, f32[3,8,32,128]{3,2,1,0:T(8,128)S(1)} %copy-done.1, f32[3,8,32,128]{3,2,1,0:T(8,128)S(1)} %copy-done.2, s32[8,32,128]{2,1,0:T(8,128)S(1)} %copy-done.3, ...), custom_call_target="tpu_custom_call" | custom-call | tf_op jit(solution)/shard_map/forward/pallas_call | solution.py:697
  27.5 3.5 %collective-permute-start.8 = (f32[8,16,128]{2,1,0:T(8,128)S(1)}, f32[8,16,128]{2,1,0:T(8,128)S(1)}, u32[]{:S(2)}, u32[]{:S(2)}) collective-permute-start(f32[8,16,128]{2,1,0:T(8,128)S(1)} %get-tuple-element.18), channel_id=1, source_target_pairs={{0,3},{1,2},{2,1},{3,0},{4,7},{5,6},{6,5},{7,4},{8,11},{9,10},{10,... | collective-permute-start | bytes 196616 | tf_op jit(solution)/shard_map/ppermute | solution.py:723
  31.0 3.5 %collective-permute-start.7 = (f32[8,16,128]{2,1,0:T(8,128)S(1)}, f32[8,16,128]{2,1,0:T(8,128)S(1)}, u32[]{:S(2)}, u32[]{:S(2)}) collective-permute-start(f32[8,16,128]{2,1,0:T(8,128)S(1)} %get-tuple-element.18), channel_id=1, source_target_pairs={{0,2},{1,3},{2,0},{3,1},{4,6},{5,7},{6,4},{7,5},{8,10},{9,11},{10,... | collective-permute-start | bytes 196616 | tf_op jit(solution)/shard_map/ppermute | solution.py:723
  34.5 1.4 %collective-permute-start.6 = (f32[8,16,128]{2,1,0:T(8,128)S(1)}, f32[8,16,128]{2,1,0:T(8,128)S(1)}, u32[]{:S(2)}, u32[]{:S(2)}) collective-permute-start(f32[8,16,128]{2,1,0:T(8,128)S(1)} %get-tuple-element.18), channel_id=1, source_target_pairs={{0,1},{1,0},{2,3},{3,2},{4,5},{5,4},{6,7},{7,6},{8,9},{9,8},{10,11... | collective-permute-start | bytes 196616 | tf_op jit(solution)/shard_map/ppermute | solution.py:723
  35.9 0.0 collective-permute-done.8
  35.9 0.9 %collective-permute-done.7 = f32[8,16,128]{2,1,0:T(8,128)S(1)} collective-permute-done((f32[8,16,128]{2,1,0:T(8,128)S(1)}, f32[8,16,128]{2,1,0:T(8,128)S(1)}, u32[]{:S(2)}, u32[]{:S(2)}) %collective-permute-start.7) | collective-permute-done | bytes 65568 | tf_op jit(solution)/shard_map/ppermute | solution.py:723
  36.7 2.9 %collective-permute-done.6 = f32[8,16,128]{2,1,0:T(8,128)S(1)} collective-permute-done((f32[8,16,128]{2,1,0:T(8,128)S(1)}, f32[8,16,128]{2,1,0:T(8,128)S(1)}, u32[]{:S(2)}, u32[]{:S(2)}) %collective-permute-start.6) | collective-permute-done | bytes 65568 | tf_op jit(solution)/shard_map/ppermute | solution.py:723
  39.6 4.2 %collective-permute-start.11 = (f32[8,16,128]{2,1,0:T(8,128)S(1)}, f32[8,16,128]{2,1,0:T(8,128)S(1)}, u32[]{:S(2)}, u32[]{:S(2)}) collective-permute-start(f32[8,16,128]{2,1,0:T(8,128)S(1)} %add_add_fusion), channel_id=1, source_target_pairs={{0,24},{4,28},{8,16},{12,20},{16,8},{20,12},{24,0},{28,4},{1,25},{... | collective-permute-start | bytes 196616 | tf_op jit(solution)/shard_map/ppermute | solution.py:726
  43.9 0.2 collective-permute-start.10
  44.1 0.4 collective-permute-start.9
  44.5 1.9 %collective-permute-done.11 = f32[8,16,128]{2,1,0:T(8,128)S(1)} collective-permute-done((f32[8,16,128]{2,1,0:T(8,128)S(1)}, f32[8,16,128]{2,1,0:T(8,128)S(1)}, u32[]{:S(2)}, u32[]{:S(2)}) %collective-permute-start.11) | collective-permute-done | bytes 65568 | tf_op jit(solution)/shard_map/ppermute | solution.py:726
  46.4 3.1 %collective-permute-done.10 = f32[8,16,128]{2,1,0:T(8,128)S(1)} collective-permute-done((f32[8,16,128]{2,1,0:T(8,128)S(1)}, f32[8,16,128]{2,1,0:T(8,128)S(1)}, u32[]{:S(2)}, u32[]{:S(2)}) %collective-permute-start.10) | collective-permute-done | bytes 65568 | tf_op jit(solution)/shard_map/ppermute | solution.py:726
  49.5 0.0 collective-permute-done.9
  49.5 0.1 collective-permute-start.12
  49.6 1.5 %collective-permute-done.12.sibling = f32[4,8,16,128]{3,2,1,0:T(8,128)S(1)} collective-permute-done((f32[4,8,16,128]{3,2,1,0:T(8,128)S(1)}, f32[4,8,16,128]{3,2,1,0:T(8,128)S(1)}, u32[]{:S(2)}, u32[]{:S(2)}) %collective-permute-start.12) | collective-permute-done | bytes 262176 | tf_op jit(solution)/shard_map/ppermute | solution.py:728
  51.1 0.0 copy-done.4
  51.1 0.0 copy-done.5
  51.1 0.0 copy-done.6
  51.2 0.0 copy-done.7
  51.2 0.0 copy-done.8
  51.2 8.0 %backward.1 = (f32[8,32,128]{2,1,0:T(8,128)S(1)}, f32[32,128]{1,0:T(8,128)S(1)}) custom-call(f32[4,8,16,128]{3,2,1,0:T(8,128)S(1)} %pad_maximum_fusion.own, f32[4,8,16,128]{3,2,1,0:T(8,128)S(1)} %collective-permute-done.12.sibling, f32[8,64,64]{2,1,0:T(8,128)S(1)} %copy-done.6, f32[2,4,8,128]{3,2,1,0:T(8,128)S(1)} %copy-done.8, ...), custom_call_target="tpu_custom_call" | custom-call | tf_op jit(solution)/shard_map/backward/pallas_call | solution.py:736
  59.2 10.7 %all_to_all.11 = f32[32,1,128]{2,1,0:T(1,128)S(1)} all-to-all(f32[32,1,128]{2,1,0:T(1,128)S(1)} %bitcast.13), channel_id=1, replica_groups=mesh['gx'=8,'gy'=4] {'gx','gy'}, dimensions={0} | all-to-all | bytes 32768 | tf_op jit(solution)/shard_map/all_to_all | solution.py:762
  69.9 0.8 %scale.1 = f32[8,32,128]{2,1,0:T(8,128)} custom-call(f32[32,128]{1,0:T(8,128)S(1)} %bitcast.12, f32[8,32,128]{2,1,0:T(8,128)S(1)} %get-tuple-element.22.gradient), custom_call_target="tpu_custom_call" | custom-call | tf_op jit(solution)/shard_map/scale/pallas_call | solution.py:764
  (3 shorter events, 0.0 us)
Async XLA Ops:
  0.0 17.2 %copy-start = (bf16[3,8,128,256]{3,2,1,0:T(8,128)(2,1)S(1)}, bf16[3,8,128,256]{3,2,1,0:T(8,128)(2,1)}, u32[]{:S(2)}) copy-start(bf16[3,8,128,256]{3,2,1,0:T(8,128)(2,1)} %constant.10.clone.table.table_in) | copy-start | bytes 4718596
  0.0 1.1 %copy-start.1 = (f32[3,8,32,128]{3,2,1,0:T(8,128)S(1)}, f32[3,8,32,128]{3,2,1,0:T(8,128)}, u32[]{:S(2)}) copy-start(f32[3,8,32,128]{3,2,1,0:T(8,128)} %e.5) | copy-start | bytes 1179652
  1.1 1.0 %copy-start.2 = (f32[3,8,32,128]{3,2,1,0:T(8,128)S(1)}, f32[3,8,32,128]{3,2,1,0:T(8,128)}, u32[]{:S(2)}) copy-start(f32[3,8,32,128]{3,2,1,0:T(8,128)} %h.5) | copy-start | bytes 1179652
  2.1 0.9 %copy-start.3 = (s32[8,32,128]{2,1,0:T(8,128)S(1)}, s32[8,32,128]{2,1,0:T(8,128)}, u32[]{:S(2)}) copy-start(s32[8,32,128]{2,1,0:T(8,128)} %material.5) | copy-start | bytes 393220
  4.0 13.2 %collective-permute-start = (f32[7,6,32,128]{3,2,1,0:T(8,128)S(1)}, f32[7,6,32,128]{3,2,1,0:T(8,128)S(1)}, u32[]{:S(2)}, u32[]{:S(2)}) collective-permute-start(f32[7,6,32,128]{3,2,1,0:T(8,128)S(1)} %get-tuple-element.14), channel_id=1, source_target_pairs={{0,4},{4,0},{8,12},{12,8},{16,20},{20,16},{24,28},{28,24},{1,5},{5... | collective-permute-start | bytes 2064392 | tf_op jit(solution)/shard_map/ppermute | solution.py:681
  4.5 12.7 %collective-permute-start.1 = (f32[7,6,32,128]{3,2,1,0:T(8,128)S(1)}, f32[7,6,32,128]{3,2,1,0:T(8,128)S(1)}, u32[]{:S(2)}, u32[]{:S(2)}) collective-permute-start(f32[7,6,32,128]{3,2,1,0:T(8,128)S(1)} %get-tuple-element.15), channel_id=1, source_target_pairs={{4,8},{8,4},{12,16},{16,12},{20,24},{24,20},{5,9},{9,5},{13,17},{1... | collective-permute-start | bytes 2064392 | tf_op jit(solution)/shard_map/ppermute | solution.py:680
  5.7 4.8 %collective-permute-start.2 = (f32[4,32,128]{2,1,0:T(8,128)S(1)}, f32[4,32,128]{2,1,0:T(8,128)S(1)}, u32[]{:S(2)}, u32[]{:S(2)}) collective-permute-start(f32[4,32,128]{2,1,0:T(8,128)S(1)} %get-tuple-element.16), channel_id=1, source_target_pairs={{0,1},{1,0},{2,3},{3,2},{4,5},{5,4},{6,7},{7,6},{8,9},{9,8},{10,11... | collective-permute-start | bytes 196616 | tf_op jit(solution)/shard_map/ppermute | solution.py:686
  8.3 2.2 %collective-permute-start.3 = (f32[4,32,128]{2,1,0:T(8,128)S(1)}, f32[4,32,128]{2,1,0:T(8,128)S(1)}, u32[]{:S(2)}, u32[]{:S(2)}) collective-permute-start(f32[4,32,128]{2,1,0:T(8,128)S(1)} %get-tuple-element.17), channel_id=1, source_target_pairs={{1,2},{2,1},{5,6},{6,5},{9,10},{10,9},{13,14},{14,13},{17,18},{18,... | collective-permute-start | bytes 196616 | tf_op jit(solution)/shard_map/ppermute | solution.py:685
  10.5 40.6 %copy-start.4 = (f32[8,2,80,64]{3,2,1,0:T(8,128)S(1)}, f32[8,2,80,64]{3,2,1,0:T(8,128)}, u32[]{:S(2)}) copy-start(f32[8,2,80,64]{3,2,1,0:T(8,128)} %constant.14.clone.rows_back_in) | copy-start | bytes 983044
  10.6 40.6 %copy-start.5 = (bf16[8,128,192]{2,1,0:T(8,128)(2,1)S(1)}, bf16[8,128,192]{2,1,0:T(8,128)(2,1)}, u32[]{:S(2)}) copy-start(bf16[8,128,192]{2,1,0:T(8,128)(2,1)} %constant.13.clone.rows_far) | copy-start | bytes 1179652
  10.6 40.6 %copy-start.6 = (f32[8,64,64]{2,1,0:T(8,128)S(1)}, f32[8,64,64]{2,1,0:T(8,128)}, u32[]{:S(2)}) copy-start(f32[8,64,64]{2,1,0:T(8,128)} %target.1) | copy-start | bytes 393220
  10.6 40.6 %copy-start.7 = (bf16[192,48]{1,0:T(8,128)(2,1)S(1)}, bf16[192,48]{1,0:T(8,128)(2,1)}, u32[]{:S(2)}) copy-start(bf16[192,48]{1,0:T(8,128)(2,1)} %constant.12.clone.weights) | copy-start | bytes 55300
  10.6 40.6 %copy-start.8 = (f32[2,4,8,128]{3,2,1,0:T(8,128)S(1)}, f32[2,4,8,128]{3,2,1,0:T(8,128)}, u32[]{:S(2)}) copy-start(f32[2,4,8,128]{3,2,1,0:T(8,128)} %constant.11.clone.twist) | copy-start | bytes 98308
  10.6 5.6 %collective-permute-start.5 = (f32[2,4,32,128]{3,2,1,0:T(8,128)S(1)}, f32[2,4,32,128]{3,2,1,0:T(8,128)S(1)}, u32[]{:S(2)}, u32[]{:S(2)}) collective-permute-start(f32[2,4,32,128]{3,2,1,0:T(8,128)S(1)} %pad_maximum_fusion.1), channel_id=1, source_target_pairs={{4,8},{8,4},{12,16},{16,12},{20,24},{24,20},{5,9},{9,5},{13,17},{1... | collective-permute-start | bytes 393224 | tf_op jit(solution)/shard_map/ppermute | solution.py:688
  11.4 5.8 %collective-permute-start.4 = (f32[2,4,32,128]{3,2,1,0:T(8,128)S(1)}, f32[2,4,32,128]{3,2,1,0:T(8,128)S(1)}, u32[]{:S(2)}, u32[]{:S(2)}) collective-permute-start(f32[2,4,32,128]{3,2,1,0:T(8,128)S(1)} %pad_maximum_fusion.1), channel_id=1, source_target_pairs={{0,4},{4,0},{8,12},{12,8},{16,20},{20,16},{24,28},{28,24},{1,5},{5... | collective-permute-start | bytes 393224 | tf_op jit(solution)/shard_map/ppermute | solution.py:689
  17.2 0.7 copy-start.9
  27.5 8.4 %collective-permute-start.8 = (f32[8,16,128]{2,1,0:T(8,128)S(1)}, f32[8,16,128]{2,1,0:T(8,128)S(1)}, u32[]{:S(2)}, u32[]{:S(2)}) collective-permute-start(f32[8,16,128]{2,1,0:T(8,128)S(1)} %get-tuple-element.18), channel_id=1, source_target_pairs={{0,3},{1,2},{2,1},{3,0},{4,7},{5,6},{6,5},{7,4},{8,11},{9,10},{10,... | collective-permute-start | bytes 196616 | tf_op jit(solution)/shard_map/ppermute | solution.py:723
  31.0 5.8 %collective-permute-start.7 = (f32[8,16,128]{2,1,0:T(8,128)S(1)}, f32[8,16,128]{2,1,0:T(8,128)S(1)}, u32[]{:S(2)}, u32[]{:S(2)}) collective-permute-start(f32[8,16,128]{2,1,0:T(8,128)S(1)} %get-tuple-element.18), channel_id=1, source_target_pairs={{0,2},{1,3},{2,0},{3,1},{4,6},{5,7},{6,4},{7,5},{8,10},{9,11},{10,... | collective-permute-start | bytes 196616 | tf_op jit(solution)/shard_map/ppermute | solution.py:723
  34.5 5.2 %collective-permute-start.6 = (f32[8,16,128]{2,1,0:T(8,128)S(1)}, f32[8,16,128]{2,1,0:T(8,128)S(1)}, u32[]{:S(2)}, u32[]{:S(2)}) collective-permute-start(f32[8,16,128]{2,1,0:T(8,128)S(1)} %get-tuple-element.18), channel_id=1, source_target_pairs={{0,1},{1,0},{2,3},{3,2},{4,5},{5,4},{6,7},{7,6},{8,9},{9,8},{10,11... | collective-permute-start | bytes 196616 | tf_op jit(solution)/shard_map/ppermute | solution.py:723
  39.6 6.8 %collective-permute-start.11 = (f32[8,16,128]{2,1,0:T(8,128)S(1)}, f32[8,16,128]{2,1,0:T(8,128)S(1)}, u32[]{:S(2)}, u32[]{:S(2)}) collective-permute-start(f32[8,16,128]{2,1,0:T(8,128)S(1)} %add_add_fusion), channel_id=1, source_target_pairs={{0,24},{4,28},{8,16},{12,20},{16,8},{20,12},{24,0},{28,4},{1,25},{... | collective-permute-start | bytes 196616 | tf_op jit(solution)/shard_map/ppermute | solution.py:726
  43.9 5.7 %collective-permute-start.10 = (f32[8,16,128]{2,1,0:T(8,128)S(1)}, f32[8,16,128]{2,1,0:T(8,128)S(1)}, u32[]{:S(2)}, u32[]{:S(2)}) collective-permute-start(f32[8,16,128]{2,1,0:T(8,128)S(1)} %add_add_fusion), channel_id=1, source_target_pairs={{0,16},{4,20},{8,24},{12,28},{16,0},{20,4},{24,8},{28,12},{1,17},{... | collective-permute-start | bytes 196616 | tf_op jit(solution)/shard_map/ppermute | solution.py:726
  44.1 5.4 %collective-permute-start.9 = (f32[8,16,128]{2,1,0:T(8,128)S(1)}, f32[8,16,128]{2,1,0:T(8,128)S(1)}, u32[]{:S(2)}, u32[]{:S(2)}) collective-permute-start(f32[8,16,128]{2,1,0:T(8,128)S(1)} %add_add_fusion), channel_id=1, source_target_pairs={{0,8},{4,12},{8,0},{12,4},{16,24},{20,28},{24,16},{28,20},{1,9},{5... | collective-permute-start | bytes 196616 | tf_op jit(solution)/shard_map/ppermute | solution.py:726
  49.5 1.6 %collective-permute-start.12 = (f32[4,8,16,128]{3,2,1,0:T(8,128)S(1)}, f32[4,8,16,128]{3,2,1,0:T(8,128)S(1)}, u32[]{:S(2)}, u32[]{:S(2)}) collective-permute-start(f32[4,8,16,128]{3,2,1,0:T(8,128)S(1)} %pad_maximum_fusion.own), channel_id=1, source_target_pairs={{0,4},{4,0},{8,12},{12,8},{16,20},{20,16},{24,28},{28,24},{1,5},{5... | collective-permute-start | bytes 786440 | tf_op jit(solution)/shard_map/ppermute | solution.py:728

commit v6 on v5

--- a/solution.py
+++ b/solution.py
@@ -376,7 +376,8 @@
                 for s in range(2):
                     spot = (part, r, s, inner)
                     value = electric[spot] + inverse[r, s] * curl[part][s]
-                    stores.append((electric, spot, value))
+                    if n < ITERS - 1:
+                        stores.append((electric, spot, value))
                     if s == 0 and x is not None:
                         stores.append((kept, (n, part, x), curl[part][0]))
                         if part < 2:
@@ -428,7 +429,7 @@
 
 
 def backward_kernel(
-    counts, own, sibling, target, twist, weights, kept_in, inverse_in, rows_far, rows_back_in, table_in,
+    counts, blocks, target, twist, weights, kept_in, inverse_in, rows_far, rows_back_in, table_in,
     gradient, squares, mid, far, intensity, back, source, electric, magnetic, scaled, accum,
     kept, inverse, rows_back, table, semaphores,
 ):
@@ -441,11 +442,11 @@
     pairs = []
     for k in range(count_rows // 2):
         near = i ^ (2 * k)
-        for block, index in ((own, near), (sibling, near ^ 1)):
+        for block, index in ((blocks[2 * k], near), (blocks[2 * k + 1], near ^ 1)):
             spot = pl.ds(pl.multiple_of(index * tile_rows, 8), tile_rows)
             for p in range(2):
                 pairs.append(
-                    (block.at[k, :, p * tile_rows : (p + 1) * tile_rows], mid.at[:, spot, p * wide : (p + 1) * wide])
+                    (block.at[:, p * tile_rows : (p + 1) * tile_rows], mid.at[:, spot, p * wide : (p + 1) * wide])
                 )
     first = len(pairs)
     pairs += [(rows_back_in, rows_back)] + column_blocks(table_in, table, width)
@@ -682,8 +683,8 @@
     col_a, col_b = call(pack_columns_kernel, "pack_columns", [VMEM] * 3, (side, side), (), (VMEM, VMEM))(
         e_init, h_init, material
     )
+    col_a = lax.ppermute(col_a, "gy", cols_a)
     col_b = lax.ppermute(col_b, "gy", cols_b)
-    col_a = lax.ppermute(col_a, "gy", cols_a)
     corner = jnp.stack([col_a, col_b])
     corner_b = lax.ppermute(corner, "gx", rows_b)
     corner_a = lax.ppermute(corner, "gx", rows_a)
@@ -721,11 +722,10 @@
     whole = mid
     for k in range(1, count_cols):
         whole = whole + lax.ppermute(mid, "gy", [(n, n ^ k) for n in range(count_cols)])
-    own = jnp.stack(
-        [whole]
-        + [lax.ppermute(whole, "gx", [(n, n ^ k) for n in range(count_rows)]) for k in range(2, count_rows, 2)]
-    )
-    sibling = lax.ppermute(own, "gx", rows_a)
+    blocks = []
+    for k in range(0, count_rows, 2):
+        part = lax.ppermute(whole, "gx", [(n, n ^ k) for n in range(count_rows)]) if k else whole
+        blocks += [part, lax.ppermute(part, "gx", rows_a)]
 
     rows = count_rows * tile_rows
     ext = tile_rows + 2 * BACK
@@ -734,9 +734,9 @@
     grid = (3, ext, 2, depth + 2 * PAD, tile_cols)
     back_rows = row_back_table(rows)
     gradient, squares = call(
-        functools.partial(backward_kernel, counts),
+        lambda *refs: backward_kernel(counts, refs[:count_rows], *refs[count_rows:]),
         "backward",
-        [ANY] * 2 + [VMEM] * 3 + [HBM] * 2 + [VMEM] + [HBM] * 2,
+        [ANY] * count_rows + [VMEM] * 3 + [HBM] * 2 + [VMEM] + [HBM] * 2,
         (array(tile_rows, depth, tile_cols), array(devices, 128)),
         [
             buffer(NF, rows, 4 * FAR),
@@ -756,7 +756,7 @@
         ],
         (VMEM, VMEM),
     )(
-        own, sibling, target, twist, jnp.asarray(source_table(depth)),
+        *blocks, target, twist, jnp.asarray(source_table(depth)),
         kept_out, inverse_out, jnp.asarray(row_table(rows)), jnp.asarray(back_rows), table,
     )
     squares = lax.all_to_all(squares, ("gx", "gy"), 0, 0, tiled=True)

time: 71 us -> 70.6 us (level)
    ppermute x1 -> x4, waiting for transfers between devices: 1.52 us -> 0.9 us  [body(): blocks += [part, lax.ppermute(part, 'gx', rows_a)]]
  transfers between devices with their start and end apart: 13 -> 16, of which waited for: 7 -> 8; matrix products, arithmetic and copies ran while one was open for 0% -> 0% of each run, Pallas kernels for 1% -> 1%
where the time goes in v6:
time: 70.6 us; the launch traced here: 70.4 us
  starting transfers between devices  23.8 us (34%)
  Pallas kernels  19.8 us (28%)
  waiting for transfers between devices  12.3 us (17%)
  blocking collectives  10.6 us (15%)
  local copies, waits for them, and re-layouts  3.7 us (5%)
    all_to_all x1, blocking collectives, body(): squares = lax.all_to_all(squares, ('gx', 'gy'), 0, 0, tiled=True)  10.6 us
    pallas_call x1, Pallas kernels, body(): call(functools.partial(forward_kernel, counts), 'forward', [HBM] * 6 + [A...  9.55 us
    ppermute x3, starting transfers between devices, body(): lax.ppermute(mid, 'gy', [(n, n ^ k) for n in range(count_cols)])  8.4 us
    pallas_call x1, Pallas kernels, body(): call(lambda *refs: backward_kernel(counts, refs[:count_rows], *refs[count...  8.02 us
    ppermute x3, waiting for transfers between devices, body(): lax.ppermute(whole, 'gx', [(n, n ^ k) for n in range(count_rows)])  5.02 us
    ppermute x3, starting transfers between devices, body(): lax.ppermute(whole, 'gx', [(n, n ^ k) for n in range(count_rows)])  4.85 us
    ppermute x1, starting transfers between devices, body(): corner_a = lax.ppermute(corner, 'gx', rows_a)  4.79 us
    ppermute x3, waiting for transfers between devices, body(): lax.ppermute(mid, 'gy', [(n, n ^ k) for n in range(count_cols)])  3.77 us
  transfers between devices with their start and end apart: 16, of which 8 were waited for; matrix products, arithmetic and copies ran while one was open for 0% of the time, Pallas kernels for 1%

profile of v6, /device:TPU:0, one launch (start us, length us, event | category | flops | bytes accessed | tf_op | source)
XLA Modules:
  0.0 70.4 jit_solution(8062482391516196746)
XLA Ops:
  0.0 0.0 copy-start
  0.0 0.0 copy-start.1
  0.0 1.1 %copy-done.1 = f32[3,8,32,128]{3,2,1,0:T(8,128)S(1)} copy-done((f32[3,8,32,128]{3,2,1,0:T(8,128)S(1)}, f32[3,8,32,128]{3,2,1,0:T(8,128)}, u32[]{:S(2)}) %copy-start.1) | copy-done | bytes 393240
  1.1 0.0 copy-start.2
  1.1 1.0 %copy-done.2 = f32[3,8,32,128]{3,2,1,0:T(8,128)S(1)} copy-done((f32[3,8,32,128]{3,2,1,0:T(8,128)S(1)}, f32[3,8,32,128]{3,2,1,0:T(8,128)}, u32[]{:S(2)}) %copy-start.2) | copy-done | bytes 393240
  2.1 0.0 copy-start.3
  2.1 0.9 %copy-done.3 = s32[8,32,128]{2,1,0:T(8,128)S(1)} copy-done((s32[8,32,128]{2,1,0:T(8,128)S(1)}, s32[8,32,128]{2,1,0:T(8,128)}, u32[]{:S(2)}) %copy-start.3) | copy-done | bytes 131096
  3.0 0.9 %pack_rows.1 = (f32[7,6,32,128]{3,2,1,0:T(8,128)S(1)}, f32[7,6,32,128]{3,2,1,0:T(8,128)S(1)}) custom-call(f32[3,8,32,128]{3,2,1,0:T(8,128)S(1)} %copy-done.1, f32[3,8,32,128]{3,2,1,0:T(8,128)S(1)} %copy-done.2, s32[8,32,128]{2,1,0:T(8,128)S(1)} %copy-done.3), custom_call_target="tpu_custom_call" | custom-call | tf_op jit(solution)/shard_map/pack_rows/pallas_call | solution.py:666
  4.0 0.5 collective-permute-start
  4.5 0.7 collective-permute-start.1
  5.2 0.5 pack_columns.1
  5.7 2.6 %collective-permute-start.2 = (f32[4,32,128]{2,1,0:T(8,128)S(1)}, f32[4,32,128]{2,1,0:T(8,128)S(1)}, u32[]{:S(2)}, u32[]{:S(2)}) collective-permute-start(f32[4,32,128]{2,1,0:T(8,128)S(1)} %get-tuple-element.16), channel_id=1, source_target_pairs={{0,1},{1,0},{2,3},{3,2},{4,5},{5,4},{6,7},{7,6},{8,9},{9,8},{10,11... | collective-permute-start | bytes 196616 | tf_op jit(solution)/shard_map/ppermute | solution.py:686
  8.3 0.7 collective-permute-start.3
  8.9 1.6 %collective-permute-done.2.own_a = f32[4,32,128]{2,1,0:T(8,128)S(1)} collective-permute-done((f32[4,32,128]{2,1,0:T(8,128)S(1)}, f32[4,32,128]{2,1,0:T(8,128)S(1)}, u32[]{:S(2)}, u32[]{:S(2)}) %collective-permute-start.2) | collective-permute-done | bytes 65568 | tf_op jit(solution)/shard_map/ppermute | solution.py:686
  10.5 0.0 collective-permute-done.3.own_b
  10.5 0.0 copy-start.4
  10.6 0.0 copy-start.5
  10.6 0.0 copy-start.6
  10.6 0.0 copy-start.7
  10.6 0.0 copy-start.8
  10.6 0.8 %collective-permute-start.5 = (f32[2,4,32,128]{3,2,1,0:T(8,128)S(1)}, f32[2,4,32,128]{3,2,1,0:T(8,128)S(1)}, u32[]{:S(2)}, u32[]{:S(2)}) collective-permute-start(f32[2,4,32,128]{3,2,1,0:T(8,128)S(1)} %pad_maximum_fusion), channel_id=1, source_target_pairs={{4,8},{8,4},{12,16},{16,12},{20,24},{24,20},{5,9},{9,5},{13,17},{1... | collective-permute-start | bytes 393224 | tf_op jit(solution)/shard_map/ppermute | solution.py:689
  11.4 4.8 %collective-permute-start.4 = (f32[2,4,32,128]{3,2,1,0:T(8,128)S(1)}, f32[2,4,32,128]{3,2,1,0:T(8,128)S(1)}, u32[]{:S(2)}, u32[]{:S(2)}) collective-permute-start(f32[2,4,32,128]{3,2,1,0:T(8,128)S(1)} %pad_maximum_fusion), channel_id=1, source_target_pairs={{0,4},{4,0},{8,12},{12,8},{16,20},{20,16},{24,28},{28,24},{1,5},{5... | collective-permute-start | bytes 393224 | tf_op jit(solution)/shard_map/ppermute | solution.py:690
  16.2 0.0 collective-permute-done.5.corner_b
  16.2 1.0 %collective-permute-done.4.corner_a = f32[2,4,32,128]{3,2,1,0:T(8,128)S(1)} collective-permute-done((f32[2,4,32,128]{3,2,1,0:T(8,128)S(1)}, f32[2,4,32,128]{3,2,1,0:T(8,128)S(1)}, u32[]{:S(2)}, u32[]{:S(2)}) %collective-permute-start.4) | collective-permute-done | bytes 131104 | tf_op jit(solution)/shard_map/ppermute | solution.py:690
  17.2 0.0 collective-permute-done.row_a
  17.2 0.0 collective-permute-done.1.row_b
  17.2 0.0 copy-done
  17.2 0.0 copy-start.9
  17.2 0.6 copy-done.9
  17.9 9.6 %forward.1 = (f32[6,3,8,32,128]{4,3,2,1,0:T(8,128)S(1)}, f32[20,2,32,128]{3,2,1,0:T(8,128)S(1)}, f32[8,16,128]{2,1,0:T(8,128)S(1)}) custom-call(f32[8]{0:T(128)S(1)} %copy-done.9, f32[3,8,32,128]{3,2,1,0:T(8,128)S(1)} %copy-done.1, f32[3,8,32,128]{3,2,1,0:T(8,128)S(1)} %copy-done.2, s32[8,32,128]{2,1,0:T(8,128)S(1)} %copy-done.3, ...), custom_call_target="tpu_custom_call" | custom-call | tf_op jit(solution)/shard_map/forward/pallas_call | solution.py:698
  27.4 3.5 %collective-permute-start.8 = (f32[8,16,128]{2,1,0:T(8,128)S(1)}, f32[8,16,128]{2,1,0:T(8,128)S(1)}, u32[]{:S(2)}, u32[]{:S(2)}) collective-permute-start(f32[8,16,128]{2,1,0:T(8,128)S(1)} %get-tuple-element.18), channel_id=1, source_target_pairs={{0,3},{1,2},{2,1},{3,0},{4,7},{5,6},{6,5},{7,4},{8,11},{9,10},{10,... | collective-permute-start | bytes 196616 | tf_op jit(solution)/shard_map/ppermute | solution.py:724
  30.9 3.5 %collective-permute-start.7 = (f32[8,16,128]{2,1,0:T(8,128)S(1)}, f32[8,16,128]{2,1,0:T(8,128)S(1)}, u32[]{:S(2)}, u32[]{:S(2)}) collective-permute-start(f32[8,16,128]{2,1,0:T(8,128)S(1)} %get-tuple-element.18), channel_id=1, source_target_pairs={{0,2},{1,3},{2,0},{3,1},{4,6},{5,7},{6,4},{7,5},{8,10},{9,11},{10,... | collective-permute-start | bytes 196616 | tf_op jit(solution)/shard_map/ppermute | solution.py:724
  34.4 1.4 %collective-permute-start.6 = (f32[8,16,128]{2,1,0:T(8,128)S(1)}, f32[8,16,128]{2,1,0:T(8,128)S(1)}, u32[]{:S(2)}, u32[]{:S(2)}) collective-permute-start(f32[8,16,128]{2,1,0:T(8,128)S(1)} %get-tuple-element.18), channel_id=1, source_target_pairs={{0,1},{1,0},{2,3},{3,2},{4,5},{5,4},{6,7},{7,6},{8,9},{9,8},{10,11... | collective-permute-start | bytes 196616 | tf_op jit(solution)/shard_map/ppermute | solution.py:724
  35.8 0.0 collective-permute-done.8
  35.8 0.9 %collective-permute-done.7 = f32[8,16,128]{2,1,0:T(8,128)S(1)} collective-permute-done((f32[8,16,128]{2,1,0:T(8,128)S(1)}, f32[8,16,128]{2,1,0:T(8,128)S(1)}, u32[]{:S(2)}, u32[]{:S(2)}) %collective-permute-start.7) | collective-permute-done | bytes 65568 | tf_op jit(solution)/shard_map/ppermute | solution.py:724
  36.7 2.9 %collective-permute-done.6 = f32[8,16,128]{2,1,0:T(8,128)S(1)} collective-permute-done((f32[8,16,128]{2,1,0:T(8,128)S(1)}, f32[8,16,128]{2,1,0:T(8,128)S(1)}, u32[]{:S(2)}, u32[]{:S(2)}) %collective-permute-start.6) | collective-permute-done | bytes 65568 | tf_op jit(solution)/shard_map/ppermute | solution.py:724
  39.6 4.2 %collective-permute-start.14 = (f32[8,16,128]{2,1,0:T(8,128)S(1)}, f32[8,16,128]{2,1,0:T(8,128)S(1)}, u32[]{:S(2)}, u32[]{:S(2)}) collective-permute-start(f32[8,16,128]{2,1,0:T(8,128)S(1)} %add_add_fusion.refs_0_), channel_id=1, source_target_pairs={{0,24},{4,28},{8,16},{12,20},{16,8},{20,12},{24,0},{28,4},{1,25},{... | collective-permute-start | bytes 196616 | tf_op jit(solution)/shard_map/ppermute | solution.py:727
  43.8 0.3 collective-permute-start.12
  44.1 0.4 collective-permute-start.10
  44.5 0.0 collective-permute-start.9
  44.5 1.9 %collective-permute-done.14.refs_6_ = f32[8,16,128]{2,1,0:T(8,128)S(1)} collective-permute-done((f32[8,16,128]{2,1,0:T(8,128)S(1)}, f32[8,16,128]{2,1,0:T(8,128)S(1)}, u32[]{:S(2)}, u32[]{:S(2)}) %collective-permute-start.14) | collective-permute-done | bytes 65568 | tf_op jit(solution)/shard_map/ppermute | solution.py:727
  46.4 0.0 collective-permute-start.15
  46.4 3.1 %collective-permute-done.12.refs_4_ = f32[8,16,128]{2,1,0:T(8,128)S(1)} collective-permute-done((f32[8,16,128]{2,1,0:T(8,128)S(1)}, f32[8,16,128]{2,1,0:T(8,128)S(1)}, u32[]{:S(2)}, u32[]{:S(2)}) %collective-permute-start.12) | collective-permute-done | bytes 65568 | tf_op jit(solution)/shard_map/ppermute | solution.py:727
  49.5 0.0 collective-permute-start.13
  49.5 0.0 collective-permute-done.10.refs_2_
  49.5 0.5 collective-permute-start.11
  50.0 0.0 collective-permute-done.9.refs_1_
  50.0 0.0 collective-permute-done.15.refs_7_
  50.0 0.7 %collective-permute-done.13.refs_5_ = f32[8,16,128]{2,1,0:T(8,128)S(1)} collective-permute-done((f32[8,16,128]{2,1,0:T(8,128)S(1)}, f32[8,16,128]{2,1,0:T(8,128)S(1)}, u32[]{:S(2)}, u32[]{:S(2)}) %collective-permute-start.13) | collective-permute-done | bytes 65568 | tf_op jit(solution)/shard_map/ppermute | solution.py:728
  50.7 0.2 collective-permute-done.11.refs_3_
  50.9 0.0 copy-done.4
  50.9 0.0 copy-done.5
  50.9 0.0 copy-done.6
  50.9 0.0 copy-done.7
  50.9 0.0 copy-done.8
  50.9 8.0 %backward.1 = (f32[8,32,128]{2,1,0:T(8,128)S(1)}, f32[32,128]{1,0:T(8,128)S(1)}) custom-call(f32[8,16,128]{2,1,0:T(8,128)S(1)} %add_add_fusion.refs_0_, f32[8,16,128]{2,1,0:T(8,128)S(1)} %collective-permute-done.9.refs_1_, f32[8,16,128]{2,1,0:T(8,128)S(1)} %collective-permute-done.10.refs_2_, f32[8,16,128]{2,1,0:T(8,128)S(1)} %collective-permute-done.11.refs_3_, ...), custom_call_target="tpu_custom_call" | custom-call | tf_op jit(solution)/shard_map/backward/pallas_call | solution.py:736
  59.0 10.6 %all_to_all.11 = f32[32,1,128]{2,1,0:T(1,128)S(1)} all-to-all(f32[32,1,128]{2,1,0:T(1,128)S(1)} %bitcast.9), channel_id=1, replica_groups=mesh['gx'=8,'gy'=4] {'gx','gy'}, dimensions={0} | all-to-all | bytes 32768 | tf_op jit(solution)/shard_map/all_to_all | solution.py:762
  69.6 0.8 %scale.1 = f32[8,32,128]{2,1,0:T(8,128)} custom-call(f32[32,128]{1,0:T(8,128)S(1)} %bitcast.8, f32[8,32,128]{2,1,0:T(8,128)S(1)} %get-tuple-element.22.gradient), custom_call_target="tpu_custom_call" | custom-call | tf_op jit(solution)/shard_map/scale/pallas_call | solution.py:764
  (2 shorter events, 0.0 us)
Async XLA Ops:
  0.0 17.2 %copy-start = (bf16[3,8,128,256]{3,2,1,0:T(8,128)(2,1)S(1)}, bf16[3,8,128,256]{3,2,1,0:T(8,128)(2,1)}, u32[]{:S(2)}) copy-start(bf16[3,8,128,256]{3,2,1,0:T(8,128)(2,1)} %constant.10.clone.table.refs_15_) | copy-start | bytes 4718596
  0.0 1.1 %copy-start.1 = (f32[3,8,32,128]{3,2,1,0:T(8,128)S(1)}, f32[3,8,32,128]{3,2,1,0:T(8,128)}, u32[]{:S(2)}) copy-start(f32[3,8,32,128]{3,2,1,0:T(8,128)} %e.5) | copy-start | bytes 1179652
  1.1 1.0 %copy-start.2 = (f32[3,8,32,128]{3,2,1,0:T(8,128)S(1)}, f32[3,8,32,128]{3,2,1,0:T(8,128)}, u32[]{:S(2)}) copy-start(f32[3,8,32,128]{3,2,1,0:T(8,128)} %h.5) | copy-start | bytes 1179652
  2.1 0.9 %copy-start.3 = (s32[8,32,128]{2,1,0:T(8,128)S(1)}, s32[8,32,128]{2,1,0:T(8,128)}, u32[]{:S(2)}) copy-start(s32[8,32,128]{2,1,0:T(8,128)} %material.5) | copy-start | bytes 393220
  4.0 13.2 %collective-permute-start = (f32[7,6,32,128]{3,2,1,0:T(8,128)S(1)}, f32[7,6,32,128]{3,2,1,0:T(8,128)S(1)}, u32[]{:S(2)}, u32[]{:S(2)}) collective-permute-start(f32[7,6,32,128]{3,2,1,0:T(8,128)S(1)} %get-tuple-element.14), channel_id=1, source_target_pairs={{0,4},{4,0},{8,12},{12,8},{16,20},{20,16},{24,28},{28,24},{1,5},{5... | collective-permute-start | bytes 2064392 | tf_op jit(solution)/shard_map/ppermute | solution.py:682
  4.5 12.7 %collective-permute-start.1 = (f32[7,6,32,128]{3,2,1,0:T(8,128)S(1)}, f32[7,6,32,128]{3,2,1,0:T(8,128)S(1)}, u32[]{:S(2)}, u32[]{:S(2)}) collective-permute-start(f32[7,6,32,128]{3,2,1,0:T(8,128)S(1)} %get-tuple-element.15), channel_id=1, source_target_pairs={{4,8},{8,4},{12,16},{16,12},{20,24},{24,20},{5,9},{9,5},{13,17},{1... | collective-permute-start | bytes 2064392 | tf_op jit(solution)/shard_map/ppermute | solution.py:681
  5.7 4.8 %collective-permute-start.2 = (f32[4,32,128]{2,1,0:T(8,128)S(1)}, f32[4,32,128]{2,1,0:T(8,128)S(1)}, u32[]{:S(2)}, u32[]{:S(2)}) collective-permute-start(f32[4,32,128]{2,1,0:T(8,128)S(1)} %get-tuple-element.16), channel_id=1, source_target_pairs={{0,1},{1,0},{2,3},{3,2},{4,5},{5,4},{6,7},{7,6},{8,9},{9,8},{10,11... | collective-permute-start | bytes 196616 | tf_op jit(solution)/shard_map/ppermute | solution.py:686
  8.3 2.2 %collective-permute-start.3 = (f32[4,32,128]{2,1,0:T(8,128)S(1)}, f32[4,32,128]{2,1,0:T(8,128)S(1)}, u32[]{:S(2)}, u32[]{:S(2)}) collective-permute-start(f32[4,32,128]{2,1,0:T(8,128)S(1)} %get-tuple-element.17), channel_id=1, source_target_pairs={{1,2},{2,1},{5,6},{6,5},{9,10},{10,9},{13,14},{14,13},{17,18},{18,... | collective-permute-start | bytes 196616 | tf_op jit(solution)/shard_map/ppermute | solution.py:687
  10.5 40.4 %copy-start.4 = (f32[8,2,80,64]{3,2,1,0:T(8,128)S(1)}, f32[8,2,80,64]{3,2,1,0:T(8,128)}, u32[]{:S(2)}) copy-start(f32[8,2,80,64]{3,2,1,0:T(8,128)} %constant.14.clone.refs_14_) | copy-start | bytes 983044
  10.6 40.4 %copy-start.5 = (bf16[8,128,192]{2,1,0:T(8,128)(2,1)S(1)}, bf16[8,128,192]{2,1,0:T(8,128)(2,1)}, u32[]{:S(2)}) copy-start(bf16[8,128,192]{2,1,0:T(8,128)(2,1)} %constant.13.clone.refs_13_) | copy-start | bytes 1179652
  10.6 40.3 %copy-start.6 = (f32[8,64,64]{2,1,0:T(8,128)S(1)}, f32[8,64,64]{2,1,0:T(8,128)}, u32[]{:S(2)}) copy-start(f32[8,64,64]{2,1,0:T(8,128)} %refs_8_.1) | copy-start | bytes 393220
  10.6 40.3 %copy-start.7 = (bf16[192,48]{1,0:T(8,128)(2,1)S(1)}, bf16[192,48]{1,0:T(8,128)(2,1)}, u32[]{:S(2)}) copy-start(bf16[192,48]{1,0:T(8,128)(2,1)} %constant.12.clone.refs_10_) | copy-start | bytes 55300
  10.6 40.3 %copy-start.8 = (f32[2,4,8,128]{3,2,1,0:T(8,128)S(1)}, f32[2,4,8,128]{3,2,1,0:T(8,128)}, u32[]{:S(2)}) copy-start(f32[2,4,8,128]{3,2,1,0:T(8,128)} %constant.11.clone.refs_9_) | copy-start | bytes 98308
  10.6 5.6 %collective-permute-start.5 = (f32[2,4,32,128]{3,2,1,0:T(8,128)S(1)}, f32[2,4,32,128]{3,2,1,0:T(8,128)S(1)}, u32[]{:S(2)}, u32[]{:S(2)}) collective-permute-start(f32[2,4,32,128]{3,2,1,0:T(8,128)S(1)} %pad_maximum_fusion), channel_id=1, source_target_pairs={{4,8},{8,4},{12,16},{16,12},{20,24},{24,20},{5,9},{9,5},{13,17},{1... | collective-permute-start | bytes 393224 | tf_op jit(solution)/shard_map/ppermute | solution.py:689
  11.4 5.8 %collective-permute-start.4 = (f32[2,4,32,128]{3,2,1,0:T(8,128)S(1)}, f32[2,4,32,128]{3,2,1,0:T(8,128)S(1)}, u32[]{:S(2)}, u32[]{:S(2)}) collective-permute-start(f32[2,4,32,128]{3,2,1,0:T(8,128)S(1)} %pad_maximum_fusion), channel_id=1, source_target_pairs={{0,4},{4,0},{8,12},{12,8},{16,20},{20,16},{24,28},{28,24},{1,5},{5... | collective-permute-start | bytes 393224 | tf_op jit(solution)/shard_map/ppermute | solution.py:690
  17.2 0.7 copy-start.9
  27.4 8.4 %collective-permute-start.8 = (f32[8,16,128]{2,1,0:T(8,128)S(1)}, f32[8,16,128]{2,1,0:T(8,128)S(1)}, u32[]{:S(2)}, u32[]{:S(2)}) collective-permute-start(f32[8,16,128]{2,1,0:T(8,128)S(1)} %get-tuple-element.18), channel_id=1, source_target_pairs={{0,3},{1,2},{2,1},{3,0},{4,7},{5,6},{6,5},{7,4},{8,11},{9,10},{10,... | collective-permute-start | bytes 196616 | tf_op jit(solution)/shard_map/ppermute | solution.py:724
  30.9 5.8 %collective-permute-start.7 = (f32[8,16,128]{2,1,0:T(8,128)S(1)}, f32[8,16,128]{2,1,0:T(8,128)S(1)}, u32[]{:S(2)}, u32[]{:S(2)}) collective-permute-start(f32[8,16,128]{2,1,0:T(8,128)S(1)} %get-tuple-element.18), channel_id=1, source_target_pairs={{0,2},{1,3},{2,0},{3,1},{4,6},{5,7},{6,4},{7,5},{8,10},{9,11},{10,... | collective-permute-start | bytes 196616 | tf_op jit(solution)/shard_map/ppermute | solution.py:724
  34.4 5.2 %collective-permute-start.6 = (f32[8,16,128]{2,1,0:T(8,128)S(1)}, f32[8,16,128]{2,1,0:T(8,128)S(1)}, u32[]{:S(2)}, u32[]{:S(2)}) collective-permute-start(f32[8,16,128]{2,1,0:T(8,128)S(1)} %get-tuple-element.18), channel_id=1, source_target_pairs={{0,1},{1,0},{2,3},{3,2},{4,5},{5,4},{6,7},{7,6},{8,9},{9,8},{10,11... | collective-permute-start | bytes 196616 | tf_op jit(solution)/shard_map/ppermute | solution.py:724
  39.6 6.8 %collective-permute-start.14 = (f32[8,16,128]{2,1,0:T(8,128)S(1)}, f32[8,16,128]{2,1,0:T(8,128)S(1)}, u32[]{:S(2)}, u32[]{:S(2)}) collective-permute-start(f32[8,16,128]{2,1,0:T(8,128)S(1)} %add_add_fusion.refs_0_), channel_id=1, source_target_pairs={{0,24},{4,28},{8,16},{12,20},{16,8},{20,12},{24,0},{28,4},{1,25},{... | collective-permute-start | bytes 196616 | tf_op jit(solution)/shard_map/ppermute | solution.py:727
  43.8 5.7 %collective-permute-start.12 = (f32[8,16,128]{2,1,0:T(8,128)S(1)}, f32[8,16,128]{2,1,0:T(8,128)S(1)}, u32[]{:S(2)}, u32[]{:S(2)}) collective-permute-start(f32[8,16,128]{2,1,0:T(8,128)S(1)} %add_add_fusion.refs_0_), channel_id=1, source_target_pairs={{0,16},{4,20},{8,24},{12,28},{16,0},{20,4},{24,8},{28,12},{1,17},{... | collective-permute-start | bytes 196616 | tf_op jit(solution)/shard_map/ppermute | solution.py:727
  44.1 5.4 %collective-permute-start.10 = (f32[8,16,128]{2,1,0:T(8,128)S(1)}, f32[8,16,128]{2,1,0:T(8,128)S(1)}, u32[]{:S(2)}, u32[]{:S(2)}) collective-permute-start(f32[8,16,128]{2,1,0:T(8,128)S(1)} %add_add_fusion.refs_0_), channel_id=1, source_target_pairs={{0,8},{4,12},{8,0},{12,4},{16,24},{20,28},{24,16},{28,20},{1,9},{5... | collective-permute-start | bytes 196616 | tf_op jit(solution)/shard_map/ppermute | solution.py:727
  44.5 5.5 %collective-permute-start.9 = (f32[8,16,128]{2,1,0:T(8,128)S(1)}, f32[8,16,128]{2,1,0:T(8,128)S(1)}, u32[]{:S(2)}, u32[]{:S(2)}) collective-permute-start(f32[8,16,128]{2,1,0:T(8,128)S(1)} %add_add_fusion.refs_0_), channel_id=1, source_target_pairs={{0,4},{4,0},{8,12},{12,8},{16,20},{20,16},{24,28},{28,24},{1,5},{5... | collective-permute-start | bytes 196616 | tf_op jit(solution)/shard_map/ppermute | solution.py:728
  46.4 3.6 %collective-permute-start.15 = (f32[8,16,128]{2,1,0:T(8,128)S(1)}, f32[8,16,128]{2,1,0:T(8,128)S(1)}, u32[]{:S(2)}, u32[]{:S(2)}) collective-permute-start(f32[8,16,128]{2,1,0:T(8,128)S(1)} %collective-permute-done.14.refs_6_), channel_id=1, source_target_pairs={{0,4},{4,0},{8,12},{12,8},{16,20},{20,16},{24,28},{28,24},{1,5},{5... | collective-permute-start | bytes 196616 | tf_op jit(solution)/shard_map/ppermute | solution.py:728
  49.5 1.3 %collective-permute-start.13 = (f32[8,16,128]{2,1,0:T(8,128)S(1)}, f32[8,16,128]{2,1,0:T(8,128)S(1)}, u32[]{:S(2)}, u32[]{:S(2)}) collective-permute-start(f32[8,16,128]{2,1,0:T(8,128)S(1)} %collective-permute-done.12.refs_4_), channel_id=1, source_target_pairs={{0,4},{4,0},{8,12},{12,8},{16,20},{20,16},{24,28},{28,24},{1,5},{5... | collective-permute-start | bytes 196616 | tf_op jit(solution)/shard_map/ppermute | solution.py:728
  49.5 1.4 %collective-permute-start.11 = (f32[8,16,128]{2,1,0:T(8,128)S(1)}, f32[8,16,128]{2,1,0:T(8,128)S(1)}, u32[]{:S(2)}, u32[]{:S(2)}) collective-permute-start(f32[8,16,128]{2,1,0:T(8,128)S(1)} %collective-permute-done.10.refs_2_), channel_id=1, source_target_pairs={{0,4},{4,0},{8,12},{12,8},{16,20},{20,16},{24,28},{28,24},{1,5},{5... | collective-permute-start | bytes 196616 | tf_op jit(solution)/shard_map/ppermute | solution.py:728
